TPU v7x, 512 devices: a whole 4x8x8 slice. The times are simulated.
512 devices in a mesh: dp: 16 (over y, core), context: 32 (over z, x).
Axes of the slice: x: 4, y: 8, z: 8, core: 2. Of those that a mesh axis runs over, the one named last changes fastest.
Arguments:
- queries: bfloat16 [16, 4096, 2048], P('dp', 'context'), may hold values from -6 to 6
- keys: bfloat16 [16, 4096, 2048], P('dp', 'context'), may hold values from -6 to 6
- values: bfloat16 [16, 4096, 2048], P('dp', 'context'), may hold values from -6 to 6
- out_grad: bfloat16 [16, 4096, 2048], P('dp', 'context'), may hold values from -6 to 6
- log_gates: float32 [16, 16, 4096], P('dp', None, 'context'), may hold values from -1 to 0, as said below
- query_map: bfloat16 [16, 128, 128], replicated, may hold values from -0.5 to 0.5
- key_map: bfloat16 [16, 128, 128], replicated, may hold values from -0.5 to 0.5
Outputs:
- query_grad: bfloat16 [16, 4096, 2048], P('dp', 'context')
- key_grad: bfloat16 [16, 4096, 2048], P('dp', 'context')
- value_grad: bfloat16 [16, 4096, 2048], P('dp', 'context')
- map_grads: float32 [4096, 128], P(('dp', 'context'))
Inputs may be any that keep to these rules, and one draw needn't show every extreme that they name: `log_gates`: every entry is negative.
All inputs are finite; a program needn't handle non-finite values.
Results may differ from a plain program's by a relative error of at most 0.019.
Values may be sent and summed in bfloat16 or wider, within the bound.
No kernel may reach another device: no remote copies, remote signals or barrier semaphores. Data moves between devices by JAX's collectives and lax.ppermute only.
A program may use at most 128 MiB of HBM per device.

v0:
```python
import jax
import jax.numpy as jnp
from jax import lax
from jax.sharding import PartitionSpec as P

split_mode = lax.Precision.HIGH


def carried_in(value, axis, combine, identity, reverse):
    devices, mine = (lax.axis_size(axis), lax.axis_index(axis))
    everything = jax.tree.map(lambda part: lax.all_gather(part, axis), value)
    start = jax.tree.map(
        lambda part, zero: jnp.broadcast_to(jnp.asarray(zero, part.dtype), part.shape),
        value,
        identity,
    )

    def hop(k, before):
        at = devices - 1 - k if reverse else k
        reached = at > mine if reverse else at < mine
        new = combine(before, jax.tree.map(lambda part: part[at], everything))
        return jax.tree.map(lambda a, b: jnp.where(reached, a, b), new, before)

    return lax.fori_loop(0, devices, hop, start)


def decay_tables(gates):
    running = jnp.cumsum(gates, axis=2)
    closing = running[:, :, -1]
    length = gates.shape[2]
    causal = jnp.arange(length)[:, None] >= jnp.arange(length)[None, :]
    spread = running[:, :, :, None] - running[:, :, None, :]
    within = jnp.where(causal, jnp.exp(jnp.where(causal, spread, 0.0)), 0.0)
    to_end = jnp.exp(closing[:, :, None] - running)
    from_start = jnp.exp(running)
    return (within, to_end, from_start, closing)


def chain(earlier, later):
    later_log = later[0].astype(jnp.float32)
    factor = jnp.exp(later_log)[:, :, None, None]
    total = factor * earlier[1].astype(jnp.float32) + later[1].astype(jnp.float32)
    joined_log = earlier[0].astype(jnp.float32) + later_log
    return (joined_log.astype(jnp.bfloat16), total.astype(jnp.bfloat16))


def per_device(queries, keys, values, out_grad, log_gates, query_map, key_map):
    heads, width = (query_map.shape[0], query_map.shape[1])
    batch, length = (queries.shape[0], queries.shape[1])
    shape = (batch, length, heads, width)
    key_scale = width ** (-0.5) / 16.0
    query_heads = queries.reshape(shape)
    key_heads = keys.reshape(shape)
    value_heads = values.reshape(shape)
    grad_heads = out_grad.reshape(shape)
    feat_query = jnp.einsum(
        "btha,had->bthd", query_heads, query_map, preferred_element_type=jnp.float32
    ).astype(jnp.bfloat16)
    feat_key = (
        jnp.einsum("btha,had->bthd", key_heads, key_map, preferred_element_type=jnp.float32)
        * key_scale
    ).astype(jnp.bfloat16)
    within, to_end, from_start, closing = decay_tables(log_gates)
    closing_log = closing.astype(jnp.bfloat16)
    scores = (
        jnp.einsum("bthd,bshd->bhts", feat_query, feat_key, preferred_element_type=jnp.float32)
        * within
    ).astype(jnp.bfloat16)
    grad_scores = (
        jnp.einsum("bthd,bshd->bhts", grad_heads, value_heads, preferred_element_type=jnp.float32)
        * within
    ).astype(jnp.bfloat16)
    start_weight = jnp.transpose(from_start, (0, 2, 1))[..., None]
    end_weight = jnp.transpose(to_end, (0, 2, 1))[..., None]
    key_weighted = feat_key * end_weight
    query_weighted = feat_query * start_weight
    states_local = jnp.einsum(
        "bshi,bshj->bhij",
        key_weighted,
        value_heads,
        precision=split_mode,
        preferred_element_type=jnp.float32,
    ).astype(jnp.bfloat16)
    grads_local = jnp.einsum(
        "bthi,bthj->bhij",
        query_weighted,
        grad_heads,
        precision=split_mode,
        preferred_element_type=jnp.float32,
    ).astype(jnp.bfloat16)
    identity = (jnp.zeros_like(closing_log), jnp.zeros_like(states_local))
    state_in = carried_in((closing_log, states_local), "context", chain, identity, False)[1]
    grad_in = carried_in((closing_log, grads_local), "context", chain, identity, True)[1]
    query_total = (
        jnp.einsum("bhts,bshd->bthd", grad_scores, feat_key, preferred_element_type=jnp.float32)
        + jnp.einsum("bthj,bhij->bthi", grad_heads, state_in, preferred_element_type=jnp.float32)
        * start_weight
    )
    key_total = (
        jnp.einsum("bhts,bthd->bshd", grad_scores, feat_query, preferred_element_type=jnp.float32)
        + jnp.einsum("bshj,bhij->bshi", value_heads, grad_in, preferred_element_type=jnp.float32)
        * end_weight
    )
    value_total = (
        jnp.einsum("bhts,bthd->bshd", scores, grad_heads, preferred_element_type=jnp.float32)
        + jnp.einsum("bshi,bhij->bshj", feat_key, grad_in, preferred_element_type=jnp.float32)
        * end_weight
    )
    query_back = query_total.astype(jnp.bfloat16)
    key_back = (key_total * key_scale).astype(jnp.bfloat16)
    query_grad = (
        jnp.einsum("bthd,had->btha", query_back, query_map, preferred_element_type=jnp.float32)
        .astype(jnp.bfloat16)
        .reshape(batch, length, heads * width)
    )
    key_grad = (
        jnp.einsum("bthd,had->btha", key_back, key_map, preferred_element_type=jnp.float32)
        .astype(jnp.bfloat16)
        .reshape(batch, length, heads * width)
    )
    value_grad = value_total.astype(jnp.bfloat16).reshape(batch, length, heads * width)
    total_tokens = batch * lax.axis_size("dp") * length * lax.axis_size("context")
    partial_sums = jnp.stack(
        [
            jnp.einsum(
                "btha,bthd->had", query_heads, query_back, preferred_element_type=jnp.float32
            ),
            jnp.einsum("btha,bthd->had", key_heads, key_back, preferred_element_type=jnp.float32),
        ]
    ).reshape(2 * heads * width, width) * total_tokens ** (-0.5)
    map_grads = lax.psum_scatter(partial_sums, ("dp", "context"), scatter_dimension=0, tiled=True)
    return (query_grad, key_grad, value_grad, map_grads)


def solution(mesh):
    return jax.shard_map(
        per_device,
        mesh=mesh,
        in_specs=(
            P("dp", "context", None),
            P("dp", "context", None),
            P("dp", "context", None),
            P("dp", "context", None),
            P("dp", None, "context"),
            P(),
            P(),
        ),
        out_specs=(
            P("dp", "context", None),
            P("dp", "context", None),
            P("dp", "context", None),
            P(("dp", "context"), None),
        ),
        check_vma=False,
    )
```

profile of v0, /device:TPU:1, one launch (start us, length us, event | category | flops | bytes accessed | tf_op | source)
XLA Modules:
  0.0 647.6 jit_solution(8936444497241248702)
XLA Ops:
  13.3 1.5 copy.137
  15.2 1.6 convolution_convert_fusion.3
  16.9 39.0 %all-gather = bf16[32,16,1]{1,2,0:T(2,128)(2,1)S(1)} all-gather(bf16[1,16,1]{1,2,0:T(2,128)(2,1)S(1)} %convert_element_type.196), channel_id=2, replica_groups=mesh['dp'=16,'context'=32] {'context'}, dimensions={0}, use_global_device_ids=true | all-gather | bytes 1056 | tf_op jit(solution)/shard_map/all_gather | solution.py:11
  56.2 2.4 fusion.15
  58.6 105.2 %all-gather.6.cloned.1.call-done = bf16[512,128,128]{2,1,0:T(8,128)(2,1)} async-done(((bf16[16,128,128]{2,1,0:T(8,128)(2,1)}), bf16[512,128,128]{2,1,0:T(8,128)(2,1)}) %all-gather.6.cloned.1.call-update) | async-done | bytes 16777232 | tf_op jit(solution)/shard_map/all_gather | solution.py:11
  163.8 46.7 %while.30 = (s32[]{:T(128)}, bf16[1,16,128,128]{3,2,1,0:T(8,128)(2,1)S(1)}, s32[]{:T(128)}, bf16[32,1,16]{2,1,0:T(2,128)(2,1)S(1)}, bf16[32,1,16,128,128]{4,3,2,1,0:T(8,128)(2,1)}, /*index=5*/s32[]{:T(128)}, s32[]{:T(128)}) while((s32[]{:T(128)}, bf16[1,16,128,128]{3,2,1,0:T(8,128)(2,1)S(1)}, s32[]{:T(128)}, ...), condition=%wide.region_2.3_spmd.clone, body=%wide.region_1.2_spmd.clone.sunk | while | flops 1835028 | bytes 1573129 | solution.py:24
  163.8 1.4 fusion.67
  165.3 1.4 fusion.67
  166.7 1.4 fusion.67
  168.2 1.4 fusion.67
  169.6 1.4 fusion.67
  171.1 1.4 fusion.67
  172.6 1.4 fusion.67
  174.0 1.4 fusion.67
  176.9 1.4 fusion.67
  178.4 1.4 fusion.67
  179.9 1.4 fusion.67
  181.4 1.4 fusion.67
  182.8 1.4 fusion.67
  184.3 1.4 fusion.67
  194.5 1.4 fusion.67
  200.3 1.4 fusion.67
  201.8 1.4 fusion.67
  203.3 1.4 fusion.67
  204.7 1.4 fusion.67
  212.1 1.5 convolution_bitcast_fusion.2
  213.5 95.9 %all-gather.8.cloned.1.call-done = bf16[512,128,128]{2,1,0:T(8,128)(2,1)} async-done(((bf16[16,128,128]{2,1,0:T(8,128)(2,1)}), bf16[512,128,128]{2,1,0:T(8,128)(2,1)}) %all-gather.8.cloned.1.call-update) | async-done | bytes 16777232 | tf_op jit(solution)/shard_map/all_gather | solution.py:11
  309.5 47.1 %while.31 = (s32[]{:T(128)}, bf16[1,16,128,128]{3,2,1,0:T(8,128)(2,1)S(1)}, s32[]{:T(128)}, bf16[32,1,16]{2,1,0:T(2,128)(2,1)S(1)}, bf16[32,1,16,128,128]{4,3,2,...) while((s32[]{:T(128)}, bf16[1,16,128,128]{3,2,1,0:T(8,128)(2,1)S(1)}, ...), condition=%wide.region_4.5_spmd.clone, body=%wide.region_3.4_spmd.clone.sunk | while | flops 1835032 | bytes 1573191 | solution.py:24
  309.5 1.5 fusion.68
  311.0 1.4 fusion.68
  312.5 1.4 fusion.68
  314.0 1.4 fusion.68
  315.4 1.4 fusion.68
  316.9 1.4 fusion.68
  318.4 1.4 fusion.68
  319.8 1.4 fusion.68
  321.3 1.4 fusion.68
  322.8 1.4 fusion.68
  324.3 1.4 fusion.68
  325.7 1.4 fusion.68
  327.2 1.4 fusion.68
  328.7 1.4 fusion.68
  330.1 1.4 fusion.68
  331.6 1.4 fusion.68
  333.1 1.4 fusion.68
  334.6 1.4 fusion.68
  336.0 1.4 fusion.68
  337.5 1.4 fusion.68
  339.0 1.4 fusion.68
  340.4 1.4 fusion.68
  341.9 1.4 fusion.68
  343.4 1.4 fusion.68
  344.9 1.4 fusion.68
  346.3 1.4 fusion.68
  347.8 1.4 fusion.68
  349.3 1.4 fusion.68
  350.7 1.4 fusion.68
  352.2 1.4 fusion.68
  353.7 1.4 fusion.68
  355.2 1.4 fusion.68
  358.9 1.5 maximum_multiply_fusion
  360.4 2.7 convolution_bitcast_fusion
  363.1 1.6 fusion.11
  368.4 271.4 %all-reduce.3.cloned.1.call-done = f32[4096,128]{1,0:T(8,128)} async-done(((f32[4096,128]{1,0:T(8,128)}), f32[4096,128]{1,0:T(8,128)}) %all-reduce.3.cloned.1.call-update) | async-done | bytes 2097168
  (138 shorter events, 34.3 us)
Async XLA Ops:
  7.2 7.6 %copy-start = (bf16[16,128,128]{2,1,0:T(8,128)(2,1)S(1)}, bf16[16,128,128]{2,1,0:T(8,128)(2,1)}, u32[]{:S(2)}) copy-start(bf16[16,128,128]{2,1,0:T(8,128)(2,1)} %param.16) | copy-start | bytes 1572868
  7.2 4.1 copy-start.9
  7.2 156.6 %all-gather.6.cloned.1.call-start = ((), (), s32[]{:S(2)}) async-start(), calls=%async_computation | async-start | bytes 17301504 | tf_op jit(solution)/shard_map/all_gather | solution.py:11
  9.9 3.0 copy-start.1
  11.2 2.0 copy-start.4
  11.2 1.7 copy-start.13
  12.9 296.5 %all-gather.8.cloned.1.call-start = ((), (), s32[]{:S(2)}) async-start(), calls=%async_computation.1 | async-start | bytes 17301504 | tf_op jit(solution)/shard_map/all_gather | solution.py:11
  13.3 197.3 %copy-start.3 = (bf16[1,128,2048]{1,2,0:T(8,128)(2,1)}, bf16[1,128,2048]{1,2,0:T(8,128)(2,1)S(1)}, u32[]{:S(2)}) copy-start(bf16[1,128,2048]{1,2,0:T(8,128)(2,1)S(1)} %copy.136) | copy-start | bytes 1572868
  14.8 2.1 copy-start.6
  16.8 622.9 %all-reduce.3.cloned.1.call-start = ((), (), s32[]{:S(2)}) async-start(), calls=%async_computation.2 | async-start | bytes 4194304
  210.5 1.0 copy-start.11
  210.6 1.5 copy-start.7
  309.5 47.1 %copy-start.5 = (bf16[16,8,16,128]{3,2,1,0:T(8,128)(2,1)S(1)}, bf16[16,8,16,128]{3,2,1,0:T(8,128)(2,1)}, u32[]{:S(2)}) copy-start(bf16[16,8,16,128]{3,2,1,0:T(8,128)(2,1)} %copy-done.4) | copy-start | bytes 1572868
  356.6 1.0 copy-start.12
  356.6 1.3 copy-start.2
  357.6 1.3 copy-start.8
  364.7 2.3 copy-start.10
Sparse Core Ops, SparseCore 0:
  13.1 150.7 all-gather.5
  167.0 142.4 all-gather.7
  360.5 279.1 all-reduce.2
where the time goes:
time: 651 us; the launch traced here: 648 us
  waiting for transfers between devices  473 us (73%)
  other arithmetic  94 us (14%)
  blocking collectives  39 us (6%)
  matrix products  14.4 us (2%)
  between operations  14.1 us (2%)
  local copies, waits for them, and re-layouts  10.8 us (2%)
    unnamed x4, waiting for transfers between devices  271 us
    all_gather x2, waiting for transfers between devices, carried_in(): everything = jax.tree.map(lambda part: lax.all_gather(part, axis), value)  201 us
    select_n x64, other arithmetic, hop(): return jax.tree.map(lambda a, b: jnp.where(reached, a, b), new, before)  90.7 us
    all_gather x1, blocking collectives, carried_in(): everything = jax.tree.map(lambda part: lax.all_gather(part, axis), value)  39 us
  transfers between devices with their start and end apart: 3, of which 3 were waited for; matrix products, arithmetic and copies ran while one was open for 10% of the time, Pallas kernels for 0%

commit v1 on v0

v1 whole, which is shorter than its diff:
```python
import functools

import jax
import jax.numpy as jnp
from jax import lax
from jax.experimental import pallas as pl
from jax.experimental.pallas import tpu as pltpu
from jax.sharding import PartitionSpec as P

F32 = jnp.float32
BF16 = jnp.bfloat16
GROUP = 8
PAD = 8


def dot(a, b, contract, precision=None):
    return lax.dot_general(
        a, b, ((contract[:1], contract[1:]), ((), ())), precision=precision, preferred_element_type=F32
    )


def running_tables(gates):
    length = gates.shape[1]
    t = lax.broadcasted_iota(jnp.int32, (length, length), 0)
    s = lax.broadcasted_iota(jnp.int32, (length, length), 1)
    causal = t >= s
    lower = jnp.where(causal, 1.0, 0.0).astype(F32)
    rows = dot(gates, lower, (1, 1), lax.Precision.HIGHEST)
    columns = dot(lower, gates, (1, 1), lax.Precision.HIGHEST)
    return causal, rows, columns


def states_kernel(key_scale, q_ref, k_ref, v_ref, g_ref, gates_ref, mq_ref, mk_ref, fq_ref, fk_ref, out_ref):
    width = mq_ref.shape[1]
    length = q_ref.shape[0]
    half = width // 2
    _, _, columns = running_tables(gates_ref[...])
    for j in range(GROUP):
        lanes = slice(j * width, (j + 1) * width)
        run = columns[:, j : j + 1]
        closing = run[length - 1 : length]
        fq = dot(q_ref[:, lanes], mq_ref[j], (1, 0)).astype(BF16)
        fk = (dot(k_ref[:, lanes], mk_ref[j], (1, 0)) * key_scale).astype(BF16)
        fq_ref[:, lanes] = fq
        fk_ref[:, lanes] = fk
        fk_end = (fk.astype(F32) * jnp.exp(closing - run)).astype(BF16)
        fq_start = (fq.astype(F32) * jnp.exp(run)).astype(BF16)
        state = dot(fk_end, v_ref[:, lanes], (0, 0)).astype(BF16)
        grad = dot(fq_start, g_ref[:, lanes], (0, 0)).astype(BF16)
        log = jnp.broadcast_to(closing, (PAD, width)).astype(BF16)
        for part in range(2):
            rows = slice(part * half, (part + 1) * half)
            out_ref[2 * j + part, 0:half] = state[rows]
            out_ref[2 * j + part, half:width] = grad[rows]
            out_ref[2 * j + part, width : width + PAD] = log


def scan_kernel(in_ref, out_ref):
    blocks, width = in_ref.shape[0], in_ref.shape[2]
    half = width // 2

    def step(carry, at, low):
        out_ref[at, low : low + half] = carry.reshape(half, width).astype(BF16)
        decay = jnp.exp(in_ref[at, width : width + PAD].astype(F32))
        new = in_ref[at, low : low + half].astype(F32).reshape(half // PAD, PAD, width)
        return decay[None] * carry + new

    zero = jnp.zeros((half // PAD, PAD, width), F32)
    ahead, back = zero, zero
    for c in range(blocks):
        ahead = step(ahead, c, 0)
        back = step(back, blocks - 1 - c, half)


def grads_kernel(
    key_scale, map_scale, q_ref, k_ref, v_ref, g_ref, fq_ref, fk_ref, gates_ref, mq_ref, mk_ref, in_ref,
    qg_ref, kg_ref, vg_ref, maps_ref,
):
    width = mq_ref.shape[1]
    length = q_ref.shape[0]
    half = width // 2
    causal, rows, columns = running_tables(gates_ref[...])
    for j in range(GROUP):
        lanes = slice(j * width, (j + 1) * width)
        run = columns[:, j : j + 1]
        closing = run[length - 1 : length]
        start = jnp.exp(run)
        end = jnp.exp(closing - run)
        within = jnp.exp(jnp.where(causal, run - rows[j : j + 1], -1e30))
        q, k, v, g = q_ref[:, lanes], k_ref[:, lanes], v_ref[:, lanes], g_ref[:, lanes]
        fq, fk = fq_ref[:, lanes], fk_ref[:, lanes]
        state_in = jnp.concatenate([in_ref[2 * j, 0:half], in_ref[2 * j + 1, 0:half]], axis=0)
        grad_in = jnp.concatenate([in_ref[2 * j, half:width], in_ref[2 * j + 1, half:width]], axis=0)
        scores = (dot(fq, fk, (1, 1)) * within).astype(BF16)
        grad_scores = (dot(g, v, (1, 1)) * within).astype(BF16)
        query_back = (dot(grad_scores, fk, (1, 0)) + dot(g, state_in, (1, 1)) * start).astype(BF16)
        key_back = (
            (dot(grad_scores, fq, (0, 0)) + dot(v, grad_in, (1, 1)) * end) * key_scale
        ).astype(BF16)
        value_grad = dot(scores, g, (0, 0)) + dot(fk, grad_in, (1, 0)) * end
        vg_ref[:, lanes] = value_grad.astype(BF16)
        qg_ref[:, lanes] = dot(query_back, mq_ref[j], (1, 1)).astype(BF16)
        kg_ref[:, lanes] = dot(key_back, mk_ref[j], (1, 1)).astype(BF16)
        core, where, y = (j // 2) % 2, (j % 2) * (width // 8), j // 4
        for m, (x, back) in enumerate(((q, query_back), (k, key_back))):
            part = (dot(x, back, (0, 0)) * map_scale).astype(BF16)
            maps_ref[core, where : where + width // 8, m, y] = part.reshape(width // 8, 8, width)


def sum_kernel(in_ref, out_ref):
    out_ref[...] = jnp.sum(in_ref[...].astype(F32), axis=0).astype(out_ref.dtype)


def add_up(value, dtype):
    return pl.pallas_call(sum_kernel, out_shape=jax.ShapeDtypeStruct(value.shape[1:], dtype))(value)


def exchange(value, axis, groups=None):
    return lax.all_to_all(value, axis, 0, 0, axis_index_groups=groups, tiled=True)


def per_device(queries, keys, values, out_grad, log_gates, query_map, key_map):
    heads, width = query_map.shape[0], query_map.shape[1]
    length = queries.shape[1]
    dp, context = lax.axis_size("dp"), lax.axis_size("context")
    key_scale = width ** (-0.5) / 16.0
    map_scale = (dp * context * length) ** (-0.5)
    steps = heads // GROUP
    q, k, v, g = (x.reshape(length, heads * width) for x in (queries, keys, values, out_grad))
    gates = log_gates.reshape(heads, length)
    wide = pl.BlockSpec((length, GROUP * width), lambda i: (0, i))
    gate_spec = pl.BlockSpec((GROUP, length), lambda i: (i, 0))
    map_spec = pl.BlockSpec((GROUP, width, width), lambda i: (i, 0, 0))
    wide_shape = jax.ShapeDtypeStruct((length, heads * width), BF16)
    fq, fk, sent = pl.pallas_call(
        functools.partial(states_kernel, key_scale),
        grid=(steps,),
        in_specs=[wide, wide, wide, wide, gate_spec, map_spec, map_spec],
        out_specs=[wide, wide, pl.BlockSpec((2 * GROUP, width + PAD, width), lambda i: (i, 0, 0))],
        out_shape=[wide_shape, wide_shape, jax.ShapeDtypeStruct((2 * heads, width + PAD, width), BF16)],
    )(q, k, v, g, gates, query_map, key_map)
    received = exchange(sent, "context")
    scanned = pl.pallas_call(
        scan_kernel,
        out_shape=jax.ShapeDtypeStruct((context, width, width), BF16),
    )(received)
    carried = exchange(scanned, "context")
    query_grad, key_grad, value_grad, maps = pl.pallas_call(
        functools.partial(grads_kernel, key_scale, map_scale),
        grid=(steps,),
        in_specs=[wide] * 6 + [gate_spec, map_spec, map_spec]
        + [pl.BlockSpec((2 * GROUP, width, width), lambda i: (i, 0, 0))],
        out_specs=[wide, wide, wide, pl.BlockSpec((2, 32, 2, 2, 8, width), lambda i: (0, 0, 0, i, 0, 0))],
        out_shape=[wide_shape] * 3 + [jax.ShapeDtypeStruct((2, 32, 2, heads // 4, 8, width), BF16)],
    )(q, k, v, g, fq, fk, gates, query_map, key_map, carried)
    cores = [[2 * y, 2 * y + 1] for y in range(dp // 2)]
    chips = [[2 * y + c for y in range(dp // 2)] for c in range(2)]
    maps = exchange(maps, "dp", cores)
    maps = exchange(add_up(maps, BF16), "context")
    maps = exchange(add_up(maps, BF16).reshape(dp // 2, 8, width), "dp", chips)
    map_grads = add_up(maps, F32)
    whole = queries.shape
    return query_grad.reshape(whole), key_grad.reshape(whole), value_grad.reshape(whole), map_grads


def solution(mesh):
    split = P("dp", "context", None)
    return jax.shard_map(
        per_device,
        mesh=mesh,
        in_specs=(split, split, split, split, P("dp", None, "context"), P(), P()),
        out_specs=(split, split, split, P(("dp", "context"), None)),
        check_vma=False,
    )
```

time: 651 us -> 145 us (0.22)
  waiting for transfers between devices: 473 us -> 0 us
  other arithmetic: 94 us -> 0 us
  blocking collectives: 39 us -> 119 us
  Pallas kernels: 0 us -> 23.2 us
  matrix products: 14.4 us -> 0 us
  between operations: 14.1 us -> 0.64 us
  local copies, waits for them, and re-layouts: 10.8 us -> 0 us
    unnamed x4 -> x0, waiting for transfers between devices: 271 us -> none
    all_gather x2 -> x0, waiting for transfers between devices: 201 us -> none  [carried_in(): everything = jax.tree.map(lambda part: lax.all_gather(part, axis), value)]
    all_to_all x0 -> x5, blocking collectives: none -> 119 us  [exchange(): lax.all_to_all(value, axis, 0, 0, axis_index_groups=groups, tiled=True)]
    select_n x64 -> x0, other arithmetic: 90.7 us -> none  [hop(): return jax.tree.map(lambda a, b: jnp.where(reached, a, b), new, before)]
    all_gather x1 -> x0, blocking collectives: 39 us -> none  [carried_in(): everything = jax.tree.map(lambda part: lax.all_gather(part, axis), value)]
    pallas_call x0 -> x6, Pallas kernels: none -> 23.2 us  [the longest x1 9.22 us: per_device(): pl.pallas_call(functools.partial(grads_kernel, key_scale, map_scale), gri...]
    dot_general x15 -> x0, matrix products: 14.4 us -> none  [the longest x1 2.74 us: per_device(): jnp.einsum('bhts,bthd->bshd', scores, grad_heads, preferred_element_type=...]
    unnamed x35 -> x0, local copies, waits for them, and re-layouts: 7.59 us -> none
  transfers between devices with their start and end apart: 3 -> 0, of which waited for: 3 -> 0; matrix products, arithmetic and copies ran while one was open for 10% -> 0% of each run, Pallas kernels for 0% -> 0%
where the time goes in v1:
time: 145 us; the launch traced here: 143 us
  blocking collectives  119 us (82%)
  Pallas kernels  23.2 us (16%)
    all_to_all x5, blocking collectives, exchange(): lax.all_to_all(value, axis, 0, 0, axis_index_groups=groups, tiled=True)  119 us
    pallas_call x1, Pallas kernels, per_device(): pl.pallas_call(functools.partial(grads_kernel, key_scale, map_scale), gri...  9.22 us
    pallas_call x1, Pallas kernels, per_device(): pl.pallas_call(functools.partial(states_kernel, key_scale), grid=(steps,)...  6.24 us
    pallas_call x3, Pallas kernels, add_up(): pl.pallas_call(sum_kernel, out_shape=jax.ShapeDtypeStruct(value.shape[1:]...  5.2 us

profile of v1, /device:TPU:1, one launch (start us, length us, event | category | flops | bytes accessed | tf_op | source)
XLA Modules:
  0.0 143.1 jit_solution(9966623437270639978)
XLA Ops:
  0.6 6.2 %shard_map.102 = (bf16[128,2048]{1,0:T(8,128)(2,1)}, bf16[128,2048]{1,0:T(8,128)(2,1)}, bf16[32,136,128]{2,1,0:T(8,128)(2,1)}) custom-call(bf16[128,2048]{1,0:T(8,128)(2,1)} %bitcast.9, bf16[128,2048]{1,0:T(8,128)(2,1)} %bitcast.11, bf16[128,2048]{1,0:T(8,128)(2,1)} %bitcast.13, bf16[128,2048]{1,0:T(8,128)(2,1)} %bitcast.15, f32[16,128]{1,0:T(8,128)} %bitcast.18, ...), custom_call_target="tpu_custom_call" | custom-call | tf_op jit(solution)/shard_map/pallas_call | solution.py:135
  6.9 43.8 %all_to_all.25.in_ref = bf16[32,136,128]{2,1,0:T(8,128)(2,1)} all-to-all(bf16[32,136,128]{2,1,0:T(8,128)(2,1)} %get-tuple-element.13), channel_id=1, replica_groups=mesh['dp'=16,'context'=32] {'context'}, dimensions={0} | all-to-all | bytes 2228224 | tf_op jit(solution)/shard_map/all_to_all | solution.py:119
  50.6 2.5 %shard_map.103 = bf16[32,128,128]{2,1,0:T(8,128)(2,1)} custom-call(bf16[32,136,128]{2,1,0:T(8,128)(2,1)} %all_to_all.25.in_ref), custom_call_target="tpu_custom_call" | custom-call | tf_op jit(solution)/shard_map/pallas_call | solution.py:143
  53.1 29.2 %all_to_all.26.in_ref = bf16[32,128,128]{2,1,0:T(8,128)(2,1)} all-to-all(bf16[32,128,128]{2,1,0:T(8,128)(2,1)} %shard_map.103), channel_id=1, replica_groups=mesh['dp'=16,'context'=32] {'context'}, dimensions={0} | all-to-all | bytes 2097152 | tf_op jit(solution)/shard_map/all_to_all | solution.py:119
  82.3 9.2 %shard_map.104 = (bf16[128,2048]{1,0:T(8,128)(2,1)}, bf16[128,2048]{1,0:T(8,128)(2,1)}, bf16[128,2048]{1,0:T(8,128)(2,1)}, bf16[2,32,2,4,8,128]{5,4,3,2,1,0:T(8,128)(2,1)}) custom-call(bf16[128,2048]{1,0:T(8,128)(2,1)} %bitcast.10, bf16[128,2048]{1,0:T(8,128)(2,1)} %bitcast.12, bf16[128,2048]{1,0:T(8,128)(2,1)} %bitcast.14, bf16[128,2048]{1,0:T(8,128)(2,1)} %bitcast.16, ...), custom_call_target="tpu_custom_call" | custom-call | tf_op jit(solution)/shard_map/pallas_call | solution.py:148
  91.5 10.8 %all_to_all.27.in_ref = bf16[2,32,2,4,8,128]{5,4,3,2,1,0:T(8,128)(2,1)} all-to-all(bf16[2,32,2,4,8,128]{5,4,3,2,1,0:T(8,128)(2,1)} %get-tuple-element.17), channel_id=1, replica_groups={{0,32},{64,96},{128,160},{192,224},{256,288},{320,352},{384,416},{448,4..., dimensions={0} | all-to-all | bytes 2097152 | tf_op jit(solution)/shard_map/all_to_all | solution.py:119
  102.3 2.2 %shard_map.105 = bf16[32,2,4,8,128]{4,3,2,1,0:T(8,128)(2,1)} custom-call(bf16[2,32,2,4,8,128]{5,4,3,2,1,0:T(8,128)(2,1)} %all_to_all.27.in_ref), custom_call_target="tpu_custom_call" | custom-call | tf_op jit(solution)/shard_map/pallas_call | solution.py:115
  104.5 22.0 %all_to_all.28.in_ref = bf16[32,2,4,8,128]{4,3,2,1,0:T(8,128)(2,1)} all-to-all(bf16[32,2,4,8,128]{4,3,2,1,0:T(8,128)(2,1)} %shard_map.105), channel_id=1, replica_groups=mesh['dp'=16,'context'=32] {'context'}, dimensions={0} | all-to-all | bytes 1048576 | tf_op jit(solution)/shard_map/all_to_all | solution.py:119
  126.5 1.7 %shard_map.106 = bf16[2,4,8,128]{3,2,1,0:T(8,128)(2,1)} custom-call(bf16[32,2,4,8,128]{4,3,2,1,0:T(8,128)(2,1)} %all_to_all.28.in_ref), custom_call_target="tpu_custom_call" | custom-call | tf_op jit(solution)/shard_map/pallas_call | solution.py:115
  128.3 13.5 %all_to_all.29.in_ref = bf16[8,8,128]{2,1,0:T(8,128)(2,1)} all-to-all(bf16[8,8,128]{2,1,0:T(8,128)(2,1)} %bitcast.17), channel_id=1, replica_groups={{0,64,128,192,256,320,384,448},{32,96,160,224,288,352,416,480},{1,65,12..., dimensions={0} | all-to-all | bytes 32768 | tf_op jit(solution)/shard_map/all_to_all | solution.py:119
  141.8 1.3 shard_map.107

commit v2 on v1

v2 whole, which is shorter than its diff:
```python
import functools

import jax
import jax.numpy as jnp
import numpy as np
from jax import lax
from jax.experimental import pallas as pl
from jax.experimental.pallas import tpu as pltpu
from jax.sharding import Mesh, PartitionSpec as P

F32 = jnp.float32
BF16 = jnp.bfloat16
GROUP = 8
PAD = 8
VMEM = pltpu.CompilerParams(vmem_limit_bytes=20 << 20)
DP = ("y_hi", "y_lo", "core")
CONTEXT = ("outer", "inner", "x")
NEAR = ("inner", "x")
FIRST, SECOND = ("y_lo", "core", "inner", "x"), ("y_hi", "outer")


def dot(a, b, contract, precision=None):
    return lax.dot_general(
        a, b, ((contract[:1], contract[1:]), ((), ())), precision=precision, preferred_element_type=F32
    )


def causal_mask(length):
    t = lax.broadcasted_iota(jnp.int32, (length, length), 0)
    s = lax.broadcasted_iota(jnp.int32, (length, length), 1)
    return t >= s


def running_columns(gates):
    lower = jnp.where(causal_mask(gates.shape[1]), 1.0, 0.0).astype(F32)
    return dot(lower, gates, (1, 1), lax.Precision.HIGHEST)


def running_rows(gates):
    lower = jnp.where(causal_mask(gates.shape[1]), 1.0, 0.0).astype(F32)
    return dot(gates, lower, (1, 1), lax.Precision.HIGHEST)


def states_kernel(key_scale, q_ref, k_ref, v_ref, g_ref, gates_ref, mq_ref, mk_ref, fq_ref, fk_ref, out_ref):
    width = mq_ref.shape[1]
    length = q_ref.shape[0]
    columns = running_columns(gates_ref[...])
    for j in range(GROUP):
        lanes = slice(j * width, (j + 1) * width)
        run = columns[:, j : j + 1]
        closing = run[length - 1 : length]
        fq = dot(q_ref[:, lanes], mq_ref[j], (1, 0)).astype(BF16)
        fk = (dot(k_ref[:, lanes], mk_ref[j], (1, 0)) * key_scale).astype(BF16)
        fq_ref[:, lanes] = fq
        fk_ref[:, lanes] = fk
        fk_end = (fk.astype(F32) * jnp.exp(closing - run)).astype(BF16)
        fq_start = (fq.astype(F32) * jnp.exp(run)).astype(BF16)
        out_ref[j, 0:width] = dot(fk_end, v_ref[:, lanes], (0, 0)).astype(BF16)
        out_ref[j, width : 2 * width] = dot(fq_start, g_ref[:, lanes], (0, 0)).astype(BF16)
        out_ref[j, 2 * width :] = jnp.broadcast_to(closing, (PAD, width)).astype(BF16)


def inside_kernel(key_scale, v_ref, g_ref, fq_ref, fk_ref, gates_ref, qb_ref, kb_ref, vg_ref):
    length = v_ref.shape[0]
    width = v_ref.shape[1] // GROUP
    causal = causal_mask(length)
    columns = running_columns(gates_ref[...])
    rows = running_rows(gates_ref[...])
    for j in range(GROUP):
        lanes = slice(j * width, (j + 1) * width)
        within = jnp.exp(jnp.where(causal, columns[:, j : j + 1] - rows[j : j + 1], -1e30))
        v, g, fq, fk = v_ref[:, lanes], g_ref[:, lanes], fq_ref[:, lanes], fk_ref[:, lanes]
        scores = (dot(fq, fk, (1, 1)) * within).astype(BF16)
        grad_scores = (dot(g, v, (1, 1)) * within).astype(BF16)
        qb_ref[:, lanes] = dot(grad_scores, fk, (1, 0))
        kb_ref[:, lanes] = dot(grad_scores, fq, (0, 0))
        vg_ref[:, lanes] = dot(scores, g, (0, 0))


def over(decay, value):
    rows, width = value.shape
    return (decay[None] * value.reshape(rows // PAD, PAD, width)).reshape(rows, width)


def totals_kernel(in_ref, out_ref):
    near, heads, width = in_ref.shape[0], in_ref.shape[1], in_ref.shape[3]
    mine = lax.axis_index("outer")
    for h in range(heads):
        ahead = jnp.zeros((width, width), F32)
        back = jnp.zeros((width, width), F32)
        log = jnp.zeros((PAD, width), F32)
        for r in range(near):
            b = near - 1 - r
            ahead = over(jnp.exp(in_ref[r, h, 2 * width :].astype(F32)), ahead) + in_ref[r, h, 0:width].astype(F32)
            back = over(jnp.exp(in_ref[b, h, 2 * width :].astype(F32)), back) + in_ref[
                b, h, width : 2 * width
            ].astype(F32)
            log = log + in_ref[r, h, 2 * width :].astype(F32)
        coarse = log.astype(BF16)
        fine = (log - coarse.astype(F32)).astype(BF16)
        for o in range(out_ref.shape[0]):
            out_ref[o, h, 0:width] = jnp.where(o > mine, ahead, back).astype(BF16)
            out_ref[o, h, width : width + PAD] = coarse
            out_ref[o, h, width + PAD :] = fine


def spread_kernel(in_ref, totals_ref, out_ref):
    near, heads, width = in_ref.shape[0], in_ref.shape[1], in_ref.shape[3]
    groups = totals_ref.shape[0]
    mine = lax.axis_index("outer")

    def total(o, h):
        log = totals_ref[o, h, width : width + PAD].astype(F32) + totals_ref[o, h, width + PAD :].astype(F32)
        return jnp.exp(log), totals_ref[o, h, 0:width].astype(F32)

    for h in range(heads):
        ahead = jnp.zeros((width, width), F32)
        back = jnp.zeros((width, width), F32)
        for o in range(groups):
            decay, value = total(o, h)
            ahead = jnp.where(o < mine, over(decay, ahead) + value, ahead)
            b = groups - 1 - o
            decay, value = total(b, h)
            back = jnp.where(b > mine, over(decay, back) + value, back)
        for r in range(near):
            b = near - 1 - r
            out_ref[r, h, 0:width] = ahead.astype(BF16)
            out_ref[b, h, width : 2 * width] = back.astype(BF16)
            if r < near - 1:
                ahead = over(jnp.exp(in_ref[r, h, 2 * width :].astype(F32)), ahead) + in_ref[r, h, 0:width].astype(F32)
                back = over(jnp.exp(in_ref[b, h, 2 * width :].astype(F32)), back) + in_ref[
                    b, h, width : 2 * width
                ].astype(F32)


def backs_kernel(
    key_scale, map_scale, q_ref, k_ref, v_ref, g_ref, gates_ref, qbi_ref, kbi_ref, in_ref, qb_ref, kb_ref, maps_ref
):
    length = q_ref.shape[0]
    width = q_ref.shape[1] // GROUP
    columns = running_columns(gates_ref[...])
    for j in range(GROUP):
        lanes = slice(j * width, (j + 1) * width)
        run = columns[:, j : j + 1]
        start = jnp.exp(run)
        end = jnp.exp(run[length - 1 : length] - run)
        state_in, grad_in = in_ref[j, 0:width], in_ref[j, width:]
        query_back = (qbi_ref[:, lanes] + dot(g_ref[:, lanes], state_in, (1, 1)) * start).astype(BF16)
        key_back = ((kbi_ref[:, lanes] + dot(v_ref[:, lanes], grad_in, (1, 1)) * end) * key_scale).astype(BF16)
        qb_ref[:, lanes] = query_back
        kb_ref[:, lanes] = key_back
        for m, (x, back) in enumerate(((q_ref[:, lanes], query_back), (k_ref[:, lanes], key_back))):
            part = dot(x, back, (0, 0)) * map_scale
            for b in range(width // 8):
                to = (j // 2) * 8 + b % 8
                maps_ref[to, m, 0, (j % 2) * 2 + b // 8] = part[8 * b : 8 * b + 8].astype(BF16)


def grads_kernel(fk_ref, gates_ref, mq_ref, mk_ref, qb_ref, kb_ref, vgi_ref, in_ref, qg_ref, kg_ref, vg_ref):
    width = mq_ref.shape[1]
    length = fk_ref.shape[0]
    columns = running_columns(gates_ref[...])
    for j in range(GROUP):
        lanes = slice(j * width, (j + 1) * width)
        run = columns[:, j : j + 1]
        end = jnp.exp(run[length - 1 : length] - run)
        vg_ref[:, lanes] = (vgi_ref[:, lanes] + dot(fk_ref[:, lanes], in_ref[j, width:], (1, 0)) * end).astype(BF16)
        qg_ref[:, lanes] = dot(qb_ref[:, lanes], mq_ref[j], (1, 1)).astype(BF16)
        kg_ref[:, lanes] = dot(kb_ref[:, lanes], mk_ref[j], (1, 1)).astype(BF16)


def sum_kernel(in_ref, out_ref):
    out_ref[...] = jnp.sum(in_ref[...].astype(F32), axis=0).astype(out_ref.dtype)


def add_up(value, dtype):
    out_shape = jax.ShapeDtypeStruct(value.shape[1:], dtype)
    return pl.pallas_call(sum_kernel, out_shape=out_shape, compiler_params=VMEM)(value)


def exchange(value, axes):
    return lax.all_to_all(value, axes, 0, 0, tiled=True)


def per_device(queries, keys, values, out_grad, log_gates, query_map, key_map):
    heads, width = query_map.shape[0], query_map.shape[1]
    length = queries.shape[1]
    near, outer = lax.axis_size(NEAR), lax.axis_size("outer")
    key_scale = width ** (-0.5) / 16.0
    map_scale = (lax.axis_size(DP) * lax.axis_size(CONTEXT) * length) ** (-0.5)
    steps = heads // GROUP
    share = heads // near
    q, k, v, g = (x.reshape(length, heads * width) for x in (queries, keys, values, out_grad))
    gates = log_gates.reshape(heads, length)
    wide = pl.BlockSpec((length, GROUP * width), lambda i: (0, i))
    gate_spec = pl.BlockSpec((GROUP, length), lambda i: (i, 0))
    map_spec = pl.BlockSpec((GROUP, width, width), lambda i: (i, 0, 0))
    wide_shape = jax.ShapeDtypeStruct((length, heads * width), BF16)
    sum_shape = jax.ShapeDtypeStruct((length, heads * width), F32)
    flops = 2 * length * width * width * heads
    fq, fk, sent = pl.pallas_call(
        functools.partial(states_kernel, key_scale),
        grid=(steps,),
        in_specs=[wide, wide, wide, wide, gate_spec, map_spec, map_spec],
        out_specs=[wide, wide, pl.BlockSpec((GROUP, 2 * width + PAD, width), lambda i: (i, 0, 0))],
        out_shape=[wide_shape, wide_shape, jax.ShapeDtypeStruct((heads, 2 * width + PAD, width), BF16)],
        cost_estimate=pl.CostEstimate(flops=4 * flops, bytes_accessed=6 << 20, transcendentals=0),
    )(q, k, v, g, gates, query_map, key_map)
    received = exchange(sent.reshape(near, share, 2 * width + PAD, width), NEAR)
    inside = pl.pallas_call(
        functools.partial(inside_kernel, key_scale),
        grid=(steps,),
        in_specs=[wide] * 4 + [gate_spec],
        out_specs=[wide] * 3,
        out_shape=[sum_shape] * 3,
        cost_estimate=pl.CostEstimate(flops=5 * flops, bytes_accessed=6 << 20, transcendentals=1 << 18),
    )(v, g, fq, fk, gates)
    totals = pl.pallas_call(
        totals_kernel,
        out_shape=jax.ShapeDtypeStruct((outer, share, width + 2 * PAD, width), BF16),
        compiler_params=VMEM,
    )(received)
    totals = exchange(totals, "outer")
    spread = pl.pallas_call(
        spread_kernel,
        out_shape=jax.ShapeDtypeStruct((near, share, 2 * width, width), BF16),
        compiler_params=VMEM,
    )(received, totals)
    carried = exchange(spread, NEAR).reshape(heads, 2 * width, width)
    carried_spec = pl.BlockSpec((GROUP, 2 * width, width), lambda i: (i, 0, 0))
    query_back, key_back, maps = pl.pallas_call(
        functools.partial(backs_kernel, key_scale, map_scale),
        grid=(steps,),
        in_specs=[wide] * 4 + [gate_spec] + [wide] * 2 + [carried_spec],
        out_specs=[wide] * 2 + [pl.BlockSpec((32, 2, 1, 4, 8, width), lambda i: (0, 0, i, 0, 0, 0))],
        out_shape=[wide_shape] * 2 + [jax.ShapeDtypeStruct((32, 2, steps, 4, 8, width), BF16)],
        cost_estimate=pl.CostEstimate(flops=4 * flops, bytes_accessed=7 << 20, transcendentals=0),
    )(q, k, v, g, gates, inside[0], inside[1], carried)
    maps = exchange(maps.reshape(32, 16, 8, width), FIRST)
    query_grad, key_grad, value_grad = pl.pallas_call(
        grads_kernel,
        grid=(steps,),
        in_specs=[wide, gate_spec, map_spec, map_spec] + [wide] * 3 + [carried_spec],
        out_specs=[wide] * 3,
        out_shape=[wide_shape] * 3,
        cost_estimate=pl.CostEstimate(flops=3 * flops, bytes_accessed=6 << 20, transcendentals=0),
    )(fk, gates, query_map, key_map, query_back, key_back, inside[2], carried)
    maps = exchange(add_up(maps, BF16), SECOND)
    map_grads = add_up(maps, F32)
    whole = queries.shape
    return query_grad.reshape(whole), key_grad.reshape(whole), value_grad.reshape(whole), map_grads


def solution(mesh):
    fine = Mesh(np.asarray(mesh.devices).reshape(4, 2, 2, 4, 2, 4), DP + CONTEXT)
    split = P(DP, CONTEXT, None)
    return jax.shard_map(
        per_device,
        mesh=fine,
        in_specs=(split, split, split, split, P(DP, None, CONTEXT), P(), P()),
        out_specs=(split, split, split, P(DP + CONTEXT, None)),
        check_vma=False,
    )
```

time: 145 us -> 116 us (0.80)
  blocking collectives: 119 us -> 65.1 us
  starting transfers between devices: 0 us -> 11.7 us
  waiting for transfers between devices: 0 us -> 10.9 us
  Pallas kernels: 23.2 us -> 25.8 us
    all_to_all x5 -> x3, blocking collectives: 119 us -> 65.1 us  [exchange(): return lax.all_to_all(value, axes, 0, 0, tiled=True)]
    all_to_all x0 -> x2, starting transfers between devices: none -> 11.7 us  [exchange(): return lax.all_to_all(value, axes, 0, 0, tiled=True)]
    all_to_all x0 -> x2, waiting for transfers between devices: none -> 10.9 us  [exchange(): return lax.all_to_all(value, axes, 0, 0, tiled=True)]
    pallas_call x5 -> x7, Pallas kernels: 16.9 us -> 19.6 us  [the longest x1 6.55 us: per_device(): pl.pallas_call(functools.partial(inside_kernel, key_scale), grid=(steps,)...]
  transfers between devices with their start and end apart: 0 -> 2, of which waited for: 0 -> 2; matrix products, arithmetic and copies ran while one was open for 0% -> 0% of each run, Pallas kernels for 0% -> 9%
where the time goes in v2:
time: 116 us; the launch traced here: 115 us
  blocking collectives  65.1 us (56%)
  Pallas kernels  25.8 us (22%)
  starting transfers between devices  11.7 us (10%)
  waiting for transfers between devices  10.9 us (9%)
    all_to_all x3, blocking collectives, exchange(): return lax.all_to_all(value, axes, 0, 0, tiled=True)  65.1 us
    all_to_all x2, starting transfers between devices, exchange(): return lax.all_to_all(value, axes, 0, 0, tiled=True)  11.7 us
    all_to_all x2, waiting for transfers between devices, exchange(): return lax.all_to_all(value, axes, 0, 0, tiled=True)  10.9 us
    pallas_call x1, Pallas kernels, per_device(): pl.pallas_call(functools.partial(inside_kernel, key_scale), grid=(steps,)...  6.55 us
    pallas_call x1, Pallas kernels, per_device(): pl.pallas_call(functools.partial(states_kernel, key_scale), grid=(steps,)...  6.2 us
    pallas_call x1, Pallas kernels, per_device(): pl.pallas_call(functools.partial(backs_kernel, key_scale, map_scale), gri...  6.15 us
    pallas_call x1, Pallas kernels, per_device(): pl.pallas_call(grads_kernel, grid=(steps,), in_specs=[wide, gate_spec, ma...  3.85 us
  transfers between devices with their start and end apart: 2, of which 2 were waited for; matrix products, arithmetic and copies ran while one was open for 0% of the time, Pallas kernels for 9%

profile of v2, /device:TPU:1, one launch (start us, length us, event | category | flops | bytes accessed | tf_op | source)
XLA Modules:
  0.0 115.2 jit_solution(8593518643972164897)
XLA Ops:
  0.6 6.2 %shard_map.102 = (bf16[128,2048]{1,0:T(8,128)(2,1)}, bf16[128,2048]{1,0:T(8,128)(2,1)}, bf16[16,264,128]{2,1,0:T(8,128)(2,1)}) custom-call(bf16[128,2048]{1,0:T(8,128)(2,1)} %bitcast.19, bf16[128,2048]{1,0:T(8,128)(2,1)} %bitcast.21, bf16[128,2048]{1,0:T(8,128)(2,1)} %bitcast.13, bf16[128,2048]{1,0:T(8,128)(2,1)} %bitcast.16, f32[16,128]{1,0:T(8,128)} %bitcast.25, ...), custom_call_target="tpu_custom_call" | custom-call | flops 268435456 | bytes 6291456 | tf_op jit(solution)/shard_map/pallas_call | solution.py:201
  6.8 19.1 %all_to_all.25.in_ref = bf16[8,2,264,128]{3,2,1,0:T(8,128)(2,1)S(1)} all-to-all(bf16[8,2,264,128]{3,2,1,0:T(8,128)(2,1)} %bitcast.23), channel_id=1, replica_groups=mesh['y_hi'=4,'y_lo'=2,'core'=2,'outer'=4,'inner'=2,'x'=4] {'inner','x'}, dimensions={0} | all-to-all | bytes 2162688 | tf_op jit(solution)/shard_map/all_to_all | solution.py:182
  25.9 0.2 shard_map.104
  26.2 20.1 %all_to_all.26.totals_ref = bf16[4,2,144,128]{3,2,1,0:T(8,128)(2,1)S(1)} all-to-all(bf16[4,2,144,128]{3,2,1,0:T(8,128)(2,1)S(1)} %shard_map.104), channel_id=1, replica_groups=mesh['y_hi'=4,'y_lo'=2,'core'=2,'outer'=4,'inner'=2,'x'=4] {'outer'}, dimensions={0} | all-to-all | bytes 589824 | tf_op jit(solution)/shard_map/all_to_all | solution.py:182
  46.2 1.4 %shard_map.105 = bf16[8,2,256,128]{3,2,1,0:T(8,128)(2,1)} custom-call(bf16[8,2,264,128]{3,2,1,0:T(8,128)(2,1)S(1)} %all_to_all.25.in_ref, bf16[4,2,144,128]{3,2,1,0:T(8,128)(2,1)S(1)} %all_to_all.26.totals_ref), custom_call_target="tpu_custom_call" | custom-call | tf_op jit(solution)/shard_map/pallas_call | solution.py:224
  47.6 3.6 %all-to-all-start.2 = ((bf16[8,2,256,128]{3,2,1,0:T(8,128)(2,1)}), bf16[8,2,256,128]{3,2,1,0:T(8,128)(2,1)S(1)}, u32[]{:S(2)}, u32[]{:S(2)}) async-start(bf16[8,2,256,128]{3,2,1,0:T(8,128)(2,1)} %shard_map.105), calls=%async_computation.2 | async-start | bytes 2097152 | tf_op jit(solution)/shard_map/all_to_all | solution.py:182
  51.2 6.6 %shard_map.103 = (f32[128,2048]{1,0:T(8,128)}, f32[128,2048]{1,0:T(8,128)}, f32[128,2048]{1,0:T(8,128)}) custom-call(bf16[128,2048]{1,0:T(8,128)(2,1)} %bitcast.14, bf16[128,2048]{1,0:T(8,128)(2,1)} %bitcast.17, bf16[128,2048]{1,0:T(8,128)(2,1)} %get-tuple-element.17.fq_ref, bf16[128,2048]{1,0:T(8,128)(2,1)} %get-tuple-element.16.fk_ref, f32[16,128]{1,0:T(8,128)} %bitcast.26), custom_call_target="tpu_custom_call" | custom-call | flops 335544320 | bytes 6291456 | tf_op jit(solution)/shard_map/pallas_call | solution.py:210
  57.8 3.5 %all-to-all-done.2 = bf16[8,2,256,128]{3,2,1,0:T(8,128)(2,1)S(1)} async-done(((bf16[8,2,256,128]{3,2,1,0:T(8,128)(2,1)}), bf16[8,2,256,128]{3,2,1,0:T(8,128)(2,1)S(1)}, u32[]{:S(2)}, u32[]{:S(2)}) %all-to-all-start.2) | async-done | bytes 1048608 | tf_op jit(solution)/shard_map/all_to_all | solution.py:182
  61.2 0.0 copy-start
  61.2 1.0 copy-done
  62.3 6.2 %shard_map.106 = (bf16[128,2048]{1,0:T(8,128)(2,1)}, bf16[128,2048]{1,0:T(8,128)(2,1)}, bf16[32,2,2,4,8,128]{5,4,3,2,1,0:T(8,128)(2,1)}) custom-call(bf16[128,2048]{1,0:T(8,128)(2,1)} %bitcast.20, bf16[128,2048]{1,0:T(8,128)(2,1)} %bitcast.22, bf16[128,2048]{1,0:T(8,128)(2,1)} %bitcast.15, bf16[128,2048]{1,0:T(8,128)(2,1)} %bitcast.18, f32[16,128]{1,0:T(8,128)} %bitcast.27, ...), custom_call_target="tpu_custom_call" | custom-call | flops 268435456 | bytes 7340032 | tf_op jit(solution)/shard_map/pallas_call | solution.py:231
  68.4 25.9 %all_to_all.27.in_ref = bf16[32,16,8,128]{3,2,1,0:T(8,128)(2,1)S(1)} all-to-all(bf16[32,16,8,128]{3,2,1,0:T(8,128)(2,1)} %bitcast.24), channel_id=1, replica_groups=mesh['y_hi'=4,'y_lo'=2,'core'=2,'outer'=4,'inner'=2,'x'=4] {'y_lo','core..., dimensions={0} | all-to-all | bytes 2097152 | tf_op jit(solution)/shard_map/all_to_all | solution.py:182
  94.4 0.8 shard_map.108
  95.1 8.2 %all-to-all-start.4 = ((bf16[16,8,128]{2,1,0:T(8,128)(2,1)}), bf16[16,8,128]{2,1,0:T(8,128)(2,1)S(1)}, u32[]{:S(2)}, u32[]{:S(2)}) async-start(bf16[16,8,128]{2,1,0:T(8,128)(2,1)} %shard_map.108), calls=%async_computation.4 | async-start | bytes 65536 | tf_op jit(solution)/shard_map/all_to_all | solution.py:182
  103.3 3.8 %shard_map.107 = (bf16[128,2048]{1,0:T(8,128)(2,1)}, bf16[128,2048]{1,0:T(8,128)(2,1)}, bf16[128,2048]{1,0:T(8,128)(2,1)}) custom-call(bf16[128,2048]{1,0:T(8,128)(2,1)} %get-tuple-element.16.fk_ref, f32[16,128]{1,0:T(8,128)} %bitcast.28, bf16[16,128,128]{2,1,0:T(8,128)(2,1)} %mq_ref.3, bf16[16,128,128]{2,1,0:T(8,128)(2,1)} %mk_ref.3, ...), custom_call_target="tpu_custom_call" | custom-call | flops 201326592 | bytes 6291456 | tf_op jit(solution)/shard_map/pallas_call | solution.py:240
  107.2 7.4 %all-to-all-done.4.in_ref = bf16[16,8,128]{2,1,0:T(8,128)(2,1)S(1)} async-done(((bf16[16,8,128]{2,1,0:T(8,128)(2,1)}), bf16[16,8,128]{2,1,0:T(8,128)(2,1)S(1)}, u32[]{:S(2)}, u32[]{:S(2)}) %all-to-all-start.4) | async-done | bytes 32800 | tf_op jit(solution)/shard_map/all_to_all | solution.py:182
  114.6 0.6 shard_map.109
Async XLA Ops:
  47.6 13.6 %all-to-all-start.2 = ((bf16[8,2,256,128]{3,2,1,0:T(8,128)(2,1)}), bf16[8,2,256,128]{3,2,1,0:T(8,128)(2,1)S(1)}, u32[]{:S(2)}, u32[]{:S(2)}) async-start(bf16[8,2,256,128]{3,2,1,0:T(8,128)(2,1)} %shard_map.105), calls=%async_computation.2 | async-start | bytes 2097152 | tf_op jit(solution)/shard_map/all_to_all | solution.py:182
  61.2 1.0 copy-start
  95.1 19.5 %all-to-all-start.4 = ((bf16[16,8,128]{2,1,0:T(8,128)(2,1)}), bf16[16,8,128]{2,1,0:T(8,128)(2,1)S(1)}, u32[]{:S(2)}, u32[]{:S(2)}) async-start(bf16[16,8,128]{2,1,0:T(8,128)(2,1)} %shard_map.108), calls=%async_computation.4 | async-start | bytes 65536 | tf_op jit(solution)/shard_map/all_to_all | solution.py:182

commit v3 on v2

v3 whole, which is shorter than its diff:
```python
import functools

import jax
import jax.numpy as jnp
import numpy as np
from jax import lax
from jax.experimental import pallas as pl
from jax.experimental.pallas import tpu as pltpu
from jax.sharding import Mesh, PartitionSpec as P

F32 = jnp.float32
BF16 = jnp.bfloat16
GROUP = 8
PAD = 8
DP = ("y", "core")
CONTEXT = ("outer", "inner", "x")
NEAR = ("inner", "x")
VMEM = pltpu.CompilerParams(vmem_limit_bytes=20 << 20)


def dot(a, b, contract, precision=None):
    return lax.dot_general(
        a, b, ((contract[:1], contract[1:]), ((), ())), precision=precision, preferred_element_type=F32
    )


def place(head):
    return 2 * (head // 4) + head % 2, (head // 2) % 2


def map_row(bit, m, owner):
    return ((bit * 2 + m) * 8 + owner) * 16


def causal_mask(length):
    t = lax.broadcasted_iota(jnp.int32, (length, length), 0)
    s = lax.broadcasted_iota(jnp.int32, (length, length), 1)
    return t >= s


def running_columns(gates):
    lower = jnp.where(causal_mask(gates.shape[1]), 1.0, 0.0).astype(F32)
    return dot(lower, gates, (1, 1), lax.Precision.HIGHEST)


def running_rows(gates):
    lower = jnp.where(causal_mask(gates.shape[1]), 1.0, 0.0).astype(F32)
    return dot(gates, lower, (1, 1), lax.Precision.HIGHEST)


def products_kernel(q_ref, k_ref, v_ref, g_ref, gates_ref, out_ref):
    length = q_ref.shape[0]
    width = q_ref.shape[1] // GROUP
    columns = running_columns(gates_ref[...])
    for j in range(GROUP):
        lanes = slice(j * width, (j + 1) * width)
        owner, bit = place(j)
        run = columns[:, j : j + 1]
        closing = run[length - 1 : length]
        g_start = (g_ref[:, lanes].astype(F32) * jnp.exp(run)).astype(BF16)
        v_end = (v_ref[:, lanes].astype(F32) * jnp.exp(closing - run)).astype(BF16)
        to = 2 * owner + bit
        out_ref[to, 0:width] = dot(q_ref[:, lanes], g_start, (0, 0)).astype(BF16)
        out_ref[to, width : 2 * width] = dot(k_ref[:, lanes], v_end, (0, 0)).astype(BF16)
        out_ref[to, 2 * width :] = jnp.broadcast_to(closing, (PAD, width)).astype(BF16)


def inside_kernel(
    key_scale, map_scale, q_ref, k_ref, v_ref, g_ref, gates_ref, mq_ref, mk_ref, fk_ref, qb_ref, kb_ref, vg_ref, out_ref
):
    heads, width = mq_ref.shape[0], mq_ref.shape[1]
    causal = causal_mask(q_ref.shape[0])
    columns = running_columns(gates_ref[...])
    rows = running_rows(gates_ref[...])
    for j in range(heads):
        lanes = slice(j * width, (j + 1) * width)
        owner, bit = place(j)
        within = jnp.exp(jnp.where(causal, columns[:, j : j + 1] - rows[j : j + 1], -1e30))
        q, k, v, g = q_ref[:, lanes], k_ref[:, lanes], v_ref[:, lanes], g_ref[:, lanes]
        fq = dot(q, mq_ref[j], (1, 0)).astype(BF16)
        fk = (dot(k, mk_ref[j], (1, 0)) * key_scale).astype(BF16)
        scores = (dot(fq, fk, (1, 1)) * within).astype(BF16)
        grad_scores = (dot(g, v, (1, 1)) * within).astype(BF16)
        query_back = dot(grad_scores, fk, (1, 0))
        key_back = dot(grad_scores, fq, (0, 0)) * key_scale
        fk_ref[:, lanes] = fk
        qb_ref[:, lanes] = query_back
        kb_ref[:, lanes] = key_back
        vg_ref[:, lanes] = dot(scores, g, (0, 0))
        for m, (x, back) in enumerate(((q, query_back), (k, key_back))):
            part = dot(x, back.astype(BF16), (0, 0)) * map_scale
            at = map_row(bit, m, owner)
            for b in range(width // 8):
                to = at + (b // 8) * 8
                out_ref[b % 8, to : to + 8] = part[8 * b : 8 * b + 8].astype(BF16)


def over(decay, value):
    rows, width = value.shape
    return (decay[None] * value.reshape(rows // PAD, PAD, width)).reshape(rows, width)


def totals_kernel(key_scale, in_ref, mq_ref, mk_ref, blocks_ref, out_ref):
    near, heads, width = in_ref.shape[0], in_ref.shape[1], in_ref.shape[3]
    mine = lax.axis_index("outer")
    pair = lax.axis_index("inner") * 2 + lax.axis_index("x") // 2
    first = pair * 4 + lax.axis_index("x") % 2
    for h in range(heads):
        mq, mk = mq_ref[first + 2 * h], mk_ref[first + 2 * h]
        ahead = jnp.zeros((width, width), F32)
        back = jnp.zeros((width, width), F32)
        log = jnp.zeros((PAD, width), F32)
        for r in range(near):
            b = near - 1 - r
            state = dot(mk, in_ref[r, h, width : 2 * width], (0, 0)) * key_scale
            grad = dot(mq, in_ref[b, h, 0:width], (0, 0))
            blocks_ref[r, h, 0:width] = state.astype(BF16)
            blocks_ref[b, h, width:] = grad.astype(BF16)
            ahead = over(jnp.exp(in_ref[r, h, 2 * width :].astype(F32)), ahead) + state
            back = over(jnp.exp(in_ref[b, h, 2 * width :].astype(F32)), back) + grad
            log = log + in_ref[r, h, 2 * width :].astype(F32)
        coarse = log.astype(BF16)
        fine = (log - coarse.astype(F32)).astype(BF16)
        for o in range(out_ref.shape[0]):
            out_ref[o, h, 0:width] = jnp.where(o > mine, ahead, back).astype(BF16)
            out_ref[o, h, width : width + PAD] = coarse
            out_ref[o, h, width + PAD :] = fine


def spread_kernel(
    key_scale, map_scale, in_ref, blocks_ref, totals_ref, inside_ref, out_ref, states_ref, maps_ref, sems
):
    near, heads, width = in_ref.shape[0], in_ref.shape[1], in_ref.shape[3]
    groups = totals_ref.shape[0]
    mine = lax.axis_index("outer")

    def total(o, h):
        log = totals_ref[o, h, width : width + PAD].astype(F32) + totals_ref[o, h, width + PAD :].astype(F32)
        return jnp.exp(log), totals_ref[o, h, 0:width].astype(F32)

    for h in range(heads):
        ahead = jnp.zeros((width, width), F32)
        back = jnp.zeros((width, width), F32)
        for o in range(groups):
            decay, value = total(o, h)
            ahead = jnp.where(o < mine, over(decay, ahead) + value, ahead)
            b = groups - 1 - o
            decay, value = total(b, h)
            back = jnp.where(b > mine, over(decay, back) + value, back)
        sums = [jnp.zeros((width, width), F32), jnp.zeros((width, width), F32)]
        for r in range(near):
            b = near - 1 - r
            state_in, grad_in = ahead.astype(BF16), back.astype(BF16)
            states_ref[r, 2 * h * width : (2 * h + 1) * width] = state_in
            states_ref[b, (2 * h + 1) * width : (2 * h + 2) * width] = grad_in
            sums[0] = sums[0] + dot(in_ref[r, h, 0:width], state_in, (1, 1))
            sums[1] = sums[1] + dot(in_ref[b, h, width : 2 * width], grad_in, (1, 1))
            if r < near - 1:
                ahead = over(jnp.exp(in_ref[r, h, 2 * width :].astype(F32)), ahead) + blocks_ref[
                    r, h, 0:width
                ].astype(F32)
                back = over(jnp.exp(in_ref[b, h, 2 * width :].astype(F32)), back) + blocks_ref[b, h, width:].astype(F32)
        for m, scale in enumerate((map_scale, map_scale * key_scale)):
            part = sums[m] * scale
            for b in range(width // 8):
                to = ((h * 2 + m) * 2 + b // 8) * 8
                maps_ref[b % 8, to : to + 8] = part[8 * b : 8 * b + 8].astype(BF16)
    rows = 2 * heads * width
    start = rows + inside_rows(heads * near)
    copies = [
        pltpu.make_async_copy(states_ref, out_ref.at[:, 0:rows], sems.at[0]),
        pltpu.make_async_copy(maps_ref, out_ref.at[:, start : start + maps_ref.shape[1]], sems.at[1]),
    ]
    for copy in copies:
        copy.start()
    for copy in copies:
        copy.wait()


def inside_rows(heads):
    return heads * 2 * 16


def gather_kernel(inside_ref, carried_ref, out_ref):
    total = jnp.sum(inside_ref[...].astype(F32), axis=0)
    for r in range(inside_ref.shape[0]):
        for bit in range(2):
            for m in range(2):
                at, of = map_row(bit, m, r), (bit * 2 + m) * 16
                add = carried_ref[r, of : of + 16].astype(F32)
                out_ref[at : at + 16] = (total[at : at + 16] + add).astype(BF16)


def grads_kernel(
    key_scale, v_ref, g_ref, fk_ref, gates_ref, mq_ref, mk_ref, qb_ref, kb_ref, vgi_ref, in_ref, qg_ref, kg_ref, vg_ref
):
    width = mq_ref.shape[1]
    length = fk_ref.shape[0]
    columns = running_columns(gates_ref[...])
    for j in range(GROUP):
        lanes = slice(j * width, (j + 1) * width)
        owner, bit = place(j)
        run = columns[:, j : j + 1]
        start = jnp.exp(run)
        end = jnp.exp(run[length - 1 : length] - run)
        state_in = in_ref[owner, 2 * bit * width : (2 * bit + 1) * width]
        grad_in = in_ref[owner, (2 * bit + 1) * width : (2 * bit + 2) * width]
        query_back = (qb_ref[:, lanes] + dot(g_ref[:, lanes], state_in, (1, 1)) * start).astype(BF16)
        key_back = (kb_ref[:, lanes] + dot(v_ref[:, lanes], grad_in, (1, 1)) * (end * key_scale)).astype(BF16)
        vg_ref[:, lanes] = (vgi_ref[:, lanes] + dot(fk_ref[:, lanes], grad_in, (1, 0)) * end).astype(BF16)
        qg_ref[:, lanes] = dot(query_back, mq_ref[j], (1, 1)).astype(BF16)
        kg_ref[:, lanes] = dot(key_back, mk_ref[j], (1, 1)).astype(BF16)


def sum_kernel(in_ref, out_ref):
    out_ref[...] = jnp.sum(in_ref[...].astype(F32), axis=0).astype(out_ref.dtype)


def add_up(value, dtype):
    out_shape = jax.ShapeDtypeStruct(value.shape[1:], dtype)
    return pl.pallas_call(sum_kernel, out_shape=out_shape, compiler_params=VMEM)(value)


def exchange(value, axes):
    return lax.all_to_all(value, axes, 0, 0, tiled=True)


def per_device(queries, keys, values, out_grad, log_gates, query_map, key_map):
    heads, width = query_map.shape[0], query_map.shape[1]
    length = queries.shape[1]
    near, outer = lax.axis_size(NEAR), lax.axis_size("outer")
    key_scale = width ** (-0.5) / 16.0
    map_scale = (lax.axis_size(DP) * lax.axis_size(CONTEXT) * length) ** (-0.5)
    steps = heads // GROUP
    share = heads // near
    q, k, v, g = (x.reshape(length, heads * width) for x in (queries, keys, values, out_grad))
    gates = log_gates.reshape(heads, length)
    wide = pl.BlockSpec((length, GROUP * width), lambda i: (0, i))
    gate_spec = pl.BlockSpec((GROUP, length), lambda i: (i, 0))
    map_spec = pl.BlockSpec((GROUP, width, width), lambda i: (i, 0, 0))
    wide_shape = jax.ShapeDtypeStruct((length, heads * width), BF16)
    sum_shape = jax.ShapeDtypeStruct((length, heads * width), F32)
    flops = 2 * length * width * width * heads
    sent = pl.pallas_call(
        products_kernel,
        grid=(steps,),
        in_specs=[wide, wide, wide, wide, gate_spec],
        out_specs=pl.BlockSpec((GROUP, 2 * width + PAD, width), lambda i: (i, 0, 0)),
        out_shape=jax.ShapeDtypeStruct((heads, 2 * width + PAD, width), BF16),
        cost_estimate=pl.CostEstimate(flops=2 * flops, bytes_accessed=3 << 20, transcendentals=0),
    )(q, k, v, g, gates)
    received = exchange(sent.reshape(near, share, 2 * width + PAD, width), NEAR)
    rows = 2 * share * width
    payload = jax.ShapeDtypeStruct((near, rows + inside_rows(heads) + inside_rows(share), width), BF16)
    full = pl.BlockSpec((length, heads * width), lambda i: (0, 0))
    fk, query_inside, key_inside, value_inside, inside = pl.pallas_call(
        functools.partial(inside_kernel, key_scale, map_scale),
        grid=(1,),
        in_specs=[full] * 4
        + [pl.BlockSpec((heads, length), lambda i: (0, 0))]
        + [pl.BlockSpec((heads, width, width), lambda i: (0, 0, 0))] * 2,
        out_specs=[full] * 4 + [pl.BlockSpec((near, inside_rows(heads), width), lambda i: (0, 1, 0))],
        out_shape=[wide_shape] + [sum_shape] * 3 + [payload],
        cost_estimate=pl.CostEstimate(flops=9 * flops, bytes_accessed=8 << 20, transcendentals=1 << 18),
    )(q, k, v, g, gates, query_map, key_map)
    blocks, totals = pl.pallas_call(
        functools.partial(totals_kernel, key_scale),
        out_shape=[
            jax.ShapeDtypeStruct((near, share, 2 * width, width), BF16),
            jax.ShapeDtypeStruct((outer, share, width + 2 * PAD, width), BF16),
        ],
    )(received, query_map, key_map)
    totals = exchange(totals, "outer")
    whole = pl.BlockSpec(memory_space=pltpu.VMEM)
    spread = pl.pallas_call(
        functools.partial(spread_kernel, key_scale, map_scale),
        in_specs=[whole, whole, whole, pl.BlockSpec(memory_space=pl.ANY)],
        out_specs=pl.BlockSpec(memory_space=pl.ANY),
        out_shape=payload,
        scratch_shapes=[
            pltpu.VMEM((near, rows, width), BF16),
            pltpu.VMEM((near, inside_rows(share), width), BF16),
            pltpu.SemaphoreType.DMA((2,)),
        ],
        input_output_aliases={3: 0},
    )(received, blocks, totals, inside)
    carried = exchange(spread, NEAR)
    tail = (rows + inside_rows(heads)) // inside_rows(share)
    maps = pl.pallas_call(
        gather_kernel,
        grid=(1,),
        in_specs=[
            pl.BlockSpec((near, inside_rows(heads), width), lambda i: (0, 1, 0)),
            pl.BlockSpec((near, inside_rows(share), width), lambda i: (0, tail, 0)),
        ],
        out_specs=pl.BlockSpec((inside_rows(heads), width), lambda i: (0, 0)),
        out_shape=jax.ShapeDtypeStruct((inside_rows(heads), width), BF16),
    )(carried, carried)
    maps = exchange(maps.reshape(2, inside_rows(heads) // 2, width), "core")
    maps = exchange(add_up(maps, BF16).reshape(32, 8, width), ("y", "outer"))
    query_grad, key_grad, value_grad = pl.pallas_call(
        functools.partial(grads_kernel, key_scale),
        grid=(steps,),
        in_specs=[wide] * 3 + [gate_spec, map_spec, map_spec] + [wide] * 3
        + [pl.BlockSpec((near // steps, rows, width), lambda i: (i, 0, 0))],
        out_specs=[wide] * 3,
        out_shape=[wide_shape] * 3,
        cost_estimate=pl.CostEstimate(flops=5 * flops, bytes_accessed=8 << 20, transcendentals=0),
    )(v, g, fk, gates, query_map, key_map, query_inside, key_inside, value_inside, carried)
    map_grads = add_up(maps, F32)
    shape = queries.shape
    return query_grad.reshape(shape), key_grad.reshape(shape), value_grad.reshape(shape), map_grads


def solution(mesh):
    fine = Mesh(np.asarray(mesh.devices).reshape(8, 2, 4, 2, 4), DP + CONTEXT)
    split = P(DP, CONTEXT, None)
    return jax.shard_map(
        per_device,
        mesh=fine,
        in_specs=(split, split, split, split, P(DP, None, CONTEXT), P(), P()),
        out_specs=(split, split, split, P(DP + CONTEXT, None)),
        check_vma=False,
    )
```

time: 116 us -> 118 us (1.017)
  starting transfers between devices: 11.7 us -> 24.6 us
  blocking collectives: 65.1 us -> 56.9 us
  waiting for transfers between devices: 10.9 us -> 5.08 us
  Pallas kernels: 25.8 us -> 29.5 us
    all_to_all x2, starting transfers between devices: 11.7 us -> 24.6 us  [exchange(): return lax.all_to_all(value, axes, 0, 0, tiled=True)]
    all_to_all x3, blocking collectives: 65.1 us -> 56.9 us  [exchange(): return lax.all_to_all(value, axes, 0, 0, tiled=True)]
    all_to_all x2, waiting for transfers between devices: 10.9 us -> 5.08 us  [exchange(): return lax.all_to_all(value, axes, 0, 0, tiled=True)]
    pallas_call x6, Pallas kernels: 24.4 us -> 28.2 us  [the longest x1 9.98 us: per_device(): pl.pallas_call(functools.partial(inside_kernel, key_scale, map_scale), gr...]
  transfers between devices with their start and end apart: 2 -> 2, of which waited for: 2 -> 1; matrix products, arithmetic and copies ran while one was open for 0% -> 0% of each run, Pallas kernels for 9% -> 14%
where the time goes in v3:
time: 118 us; the launch traced here: 117 us
  blocking collectives  56.9 us (48%)
  Pallas kernels  29.5 us (25%)
  starting transfers between devices  24.6 us (21%)
  waiting for transfers between devices  5.08 us (4%)
    all_to_all x3, blocking collectives, exchange(): return lax.all_to_all(value, axes, 0, 0, tiled=True)  56.9 us
    all_to_all x2, starting transfers between devices, exchange(): return lax.all_to_all(value, axes, 0, 0, tiled=True)  24.6 us
    pallas_call x1, Pallas kernels, per_device(): pl.pallas_call(functools.partial(inside_kernel, key_scale, map_scale), gr...  9.98 us
    pallas_call x1, Pallas kernels, per_device(): pl.pallas_call(functools.partial(grads_kernel, key_scale), grid=(steps,),...  6.1 us
    all_to_all x2, waiting for transfers between devices, exchange(): return lax.all_to_all(value, axes, 0, 0, tiled=True)  5.08 us
    pallas_call x1, Pallas kernels, per_device(): pl.pallas_call(products_kernel, grid=(steps,), in_specs=[wide, wide, wide...  3.69 us
    pallas_call x1, Pallas kernels, per_device(): pl.pallas_call(functools.partial(spread_kernel, key_scale, map_scale), in...  3.32 us
    pallas_call x1, Pallas kernels, per_device(): pl.pallas_call(functools.partial(totals_kernel, key_scale), out_shape=[ja...  3.08 us
  transfers between devices with their start and end apart: 2, of which 1 were waited for; matrix products, arithmetic and copies ran while one was open for 0% of the time, Pallas kernels for 14%

profile of v3, /device:TPU:1, one launch (start us, length us, event | category | flops | bytes accessed | tf_op | source)
XLA Modules:
  0.0 117.4 jit_solution(10563031374721501135)
XLA Ops:
  0.6 3.7 %shard_map.103 = bf16[16,264,128]{2,1,0:T(8,128)(2,1)} custom-call(bf16[128,2048]{1,0:T(8,128)(2,1)} %bitcast.18, bf16[128,2048]{1,0:T(8,128)(2,1)} %bitcast.20, bf16[128,2048]{1,0:T(8,128)(2,1)} %bitcast.11, bf16[128,2048]{1,0:T(8,128)(2,1)} %bitcast.14, f32[16,128]{1,0:T(8,128)} %bitcast.23), custom_call_target="tpu_custom_call" | custom-call | flops 134217728 | bytes 3145728 | tf_op jit(solution)/shard_map/pallas_call | solution.py:244
  4.3 18.5 %all_to_all.25.in_ref = bf16[8,2,264,128]{3,2,1,0:T(8,128)(2,1)} all-to-all(bf16[8,2,264,128]{3,2,1,0:T(8,128)(2,1)} %bitcast.17), channel_id=1, replica_groups=mesh['y'=8,'core'=2,'outer'=4,'inner'=2,'x'=4] {'inner','x'}, dimensions={0} | all-to-all | bytes 2162688 | tf_op jit(solution)/shard_map/all_to_all | solution.py:225
  22.8 3.1 %shard_map.104 = (bf16[8,2,256,128]{3,2,1,0:T(8,128)(2,1)}, bf16[4,2,144,128]{3,2,1,0:T(8,128)(2,1)}) custom-call(bf16[8,2,264,128]{3,2,1,0:T(8,128)(2,1)} %all_to_all.25.in_ref, bf16[16,128,128]{2,1,0:T(8,128)(2,1)} %mq_ref.5, bf16[16,128,128]{2,1,0:T(8,128)(2,1)} %mk_ref.5), custom_call_target="tpu_custom_call" | custom-call | tf_op jit(solution)/shard_map/pallas_call | solution.py:266
  25.9 12.5 %all-to-all-start.1 = ((bf16[4,2,144,128]{3,2,1,0:T(8,128)(2,1)}), bf16[4,2,144,128]{3,2,1,0:T(8,128)(2,1)S(1)}, u32[]{:S(2)}, u32[]{:S(2)}) async-start(bf16[4,2,144,128]{3,2,1,0:T(8,128)(2,1)} %get-tuple-element.19), calls=%async_computation.1 | async-start | bytes 589824 | tf_op jit(solution)/shard_map/all_to_all | solution.py:225
  38.4 10.0 %shard_map.102 = (bf16[128,2048]{1,0:T(8,128)(2,1)}, f32[128,2048]{1,0:T(8,128)}, f32[128,2048]{1,0:T(8,128)}, f32[128,2048]{1,0:T(8,128)}, bf16[8,1088,128]{2,1,0:T(8,128)(2,1)}) custom-call(bf16[128,2048]{1,0:T(8,128)(2,1)} %bitcast.19, bf16[128,2048]{1,0:T(8,128)(2,1)} %bitcast.21, bf16[128,2048]{1,0:T(8,128)(2,1)} %bitcast.12, ...), custom_call_target="tpu_custom_call" | custom-call | flops 603979776 | bytes 8388608 | tf_op jit(solution)/shard_map/pallas_call | solution.py:256
  48.4 0.0 all-to-all-done.1.totals_ref
  48.4 0.0 copy-start
  48.4 0.7 copy-done
  49.1 3.3 %shard_map.105 = bf16[8,1088,128]{2,1,0:T(8,128)(2,1)} custom-call(bf16[8,2,264,128]{3,2,1,0:T(8,128)(2,1)} %all_to_all.25.in_ref, bf16[8,2,256,128]{3,2,1,0:T(8,128)(2,1)} %get-tuple-element.18.blocks_ref, bf16[4,2,144,128]{3,2,1,0:T(8,128)(2,1)} %copy-done, bf16[8,1088,128]{2,1,0:T(8,128)(2,1)} %get-tuple-element.20.inside_ref), custom_call_target="tpu_custom_call", output_to_operand_aliasing={{}: (3, {})} | custom-call | tf_op jit(solution)/shard_map/pallas_call | solution.py:275
  52.5 30.0 %all_to_all.26.in_ref.inside_ref.carried_ref = bf16[8,1088,128]{2,1,0:T(8,128)(2,1)} all-to-all(bf16[8,1088,128]{2,1,0:T(8,128)(2,1)} %shard_map.105), channel_id=1, replica_groups=mesh['y'=8,'core'=2,'outer'=4,'inner'=2,'x'=4] {'inner','x'}, dimensions={0} | all-to-all | bytes 4456448 | tf_op jit(solution)/shard_map/all_to_all | solution.py:225
  82.4 2.0 %shard_map.107 = bf16[512,128]{1,0:T(8,128)(2,1)} custom-call(bf16[8,1088,128]{2,1,0:T(8,128)(2,1)} %all_to_all.26.in_ref.inside_ref.carried_ref, bf16[8,1088,128]{2,1,0:T(8,128)(2,1)} %all_to_all.26.in_ref.inside_ref.carried_ref), custom_call_target="tpu_custom_call" | custom-call | tf_op jit(solution)/shard_map/pallas_call | solution.py:289
  84.5 8.4 %all_to_all.27.in_ref = bf16[2,256,128]{2,1,0:T(8,128)(2,1)S(1)} all-to-all(bf16[2,256,128]{2,1,0:T(8,128)(2,1)} %bitcast.22), channel_id=1, replica_groups=mesh['y'=8,'core'=2,'outer'=4,'inner'=2,'x'=4] {'core'}, dimensions={0} | all-to-all | bytes 262144 | tf_op jit(solution)/shard_map/all_to_all | solution.py:225
  92.9 0.6 shard_map.108
  93.5 12.1 %all-to-all-start.4 = ((bf16[32,8,128]{2,1,0:T(8,128)(2,1)}), bf16[32,8,128]{2,1,0:T(8,128)(2,1)S(1)}, u32[]{:S(2)}, u32[]{:S(2)}) async-start(bf16[32,8,128]{2,1,0:T(8,128)(2,1)} %bitcast.10), calls=%async_computation.4 | async-start | bytes 131072 | tf_op jit(solution)/shard_map/all_to_all | solution.py:225
  105.6 6.1 %shard_map.106 = (bf16[128,2048]{1,0:T(8,128)(2,1)}, bf16[128,2048]{1,0:T(8,128)(2,1)}, bf16[128,2048]{1,0:T(8,128)(2,1)}) custom-call(bf16[128,2048]{1,0:T(8,128)(2,1)} %bitcast.13, bf16[128,2048]{1,0:T(8,128)(2,1)} %bitcast.16, bf16[128,2048]{1,0:T(8,128)(2,1)} %get-tuple-element.14.fk_ref, f32[16,128]{1,0:T(8,128)} %bitcast.25, ...), custom_call_target="tpu_custom_call" | custom-call | flops 335544320 | bytes 8388608 | tf_op jit(solution)/shard_map/pallas_call | solution.py:301
  111.7 5.1 %all-to-all-done.4.in_ref = bf16[32,8,128]{2,1,0:T(8,128)(2,1)S(1)} async-done(((bf16[32,8,128]{2,1,0:T(8,128)(2,1)}), bf16[32,8,128]{2,1,0:T(8,128)(2,1)S(1)}, u32[]{:S(2)}, u32[]{:S(2)}) %all-to-all-start.4) | async-done | bytes 65568 | tf_op jit(solution)/shard_map/all_to_all | solution.py:225
  116.8 0.6 shard_map.109
Async XLA Ops:
  25.9 22.5 %all-to-all-start.1 = ((bf16[4,2,144,128]{3,2,1,0:T(8,128)(2,1)}), bf16[4,2,144,128]{3,2,1,0:T(8,128)(2,1)S(1)}, u32[]{:S(2)}, u32[]{:S(2)}) async-start(bf16[4,2,144,128]{3,2,1,0:T(8,128)(2,1)} %get-tuple-element.19), calls=%async_computation.1 | async-start | bytes 589824 | tf_op jit(solution)/shard_map/all_to_all | solution.py:225
  48.4 0.7 copy-start
  93.5 23.3 %all-to-all-start.4 = ((bf16[32,8,128]{2,1,0:T(8,128)(2,1)}), bf16[32,8,128]{2,1,0:T(8,128)(2,1)S(1)}, u32[]{:S(2)}, u32[]{:S(2)}) async-start(bf16[32,8,128]{2,1,0:T(8,128)(2,1)} %bitcast.10), calls=%async_computation.4 | async-start | bytes 131072 | tf_op jit(solution)/shard_map/all_to_all | solution.py:225

commit v4 on v3

--- a/solution.py
+++ b/solution.py
@@ -12,7 +12,7 @@
 BF16 = jnp.bfloat16
 GROUP = 8
 PAD = 8
-DP = ("y", "core")
+DP = ("y_hi", "y_lo", "core")
 CONTEXT = ("outer", "inner", "x")
 NEAR = ("inner", "x")
 VMEM = pltpu.CompilerParams(vmem_limit_bytes=20 << 20)
@@ -26,10 +26,6 @@
 
 def place(head):
     return 2 * (head // 4) + head % 2, (head // 2) % 2
-
-
-def map_row(bit, m, owner):
-    return ((bit * 2 + m) * 8 + owner) * 16
 
 
 def causal_mask(length):
@@ -69,12 +65,14 @@
     key_scale, map_scale, q_ref, k_ref, v_ref, g_ref, gates_ref, mq_ref, mk_ref, fk_ref, qb_ref, kb_ref, vg_ref, out_ref
 ):
     heads, width = mq_ref.shape[0], mq_ref.shape[1]
+    core, y_lo = lax.axis_index("core"), lax.axis_index("y_lo")
     causal = causal_mask(q_ref.shape[0])
     columns = running_columns(gates_ref[...])
     rows = running_rows(gates_ref[...])
     for j in range(heads):
         lanes = slice(j * width, (j + 1) * width)
         owner, bit = place(j)
+        side = 2 * lax.bitwise_xor(core, bit) + lax.bitwise_xor(y_lo, (owner // 2) % 2)
         within = jnp.exp(jnp.where(causal, columns[:, j : j + 1] - rows[j : j + 1], -1e30))
         q, k, v, g = q_ref[:, lanes], k_ref[:, lanes], v_ref[:, lanes], g_ref[:, lanes]
         fq = dot(q, mq_ref[j], (1, 0)).astype(BF16)
@@ -89,10 +87,10 @@
         vg_ref[:, lanes] = dot(scores, g, (0, 0))
         for m, (x, back) in enumerate(((q, query_back), (k, key_back))):
             part = dot(x, back.astype(BF16), (0, 0)) * map_scale
-            at = map_row(bit, m, owner)
+            at = ((m * 2 + owner // 4) * 2 + owner % 2) * 16
             for b in range(width // 8):
                 to = at + (b // 8) * 8
-                out_ref[b % 8, to : to + 8] = part[8 * b : 8 * b + 8].astype(BF16)
+                out_ref[side, b % 8, to : to + 8] = part[8 * b : 8 * b + 8].astype(BF16)
 
 
 def over(decay, value):
@@ -100,7 +98,8 @@
     return (decay[None] * value.reshape(rows // PAD, PAD, width)).reshape(rows, width)
 
 
-def totals_kernel(key_scale, in_ref, mq_ref, mk_ref, blocks_ref, out_ref):
+def totals_kernel(key_scale, in_ref, mq_ref, mk_ref, inside_ref, blocks_ref, out_ref):
+    del inside_ref
     near, heads, width = in_ref.shape[0], in_ref.shape[1], in_ref.shape[3]
     mine = lax.axis_index("outer")
     pair = lax.axis_index("inner") * 2 + lax.axis_index("x") // 2
@@ -166,7 +165,7 @@
                 to = ((h * 2 + m) * 2 + b // 8) * 8
                 maps_ref[b % 8, to : to + 8] = part[8 * b : 8 * b + 8].astype(BF16)
     rows = 2 * heads * width
-    start = rows + inside_rows(heads * near)
+    start = rows + inside_rows(heads * near) // 4
     copies = [
         pltpu.make_async_copy(states_ref, out_ref.at[:, 0:rows], sems.at[0]),
         pltpu.make_async_copy(maps_ref, out_ref.at[:, start : start + maps_ref.shape[1]], sems.at[1]),
@@ -181,14 +180,28 @@
     return heads * 2 * 16
 
 
+def halve_kernel(kept_ref, got_ref, keep_ref, send_ref):
+    keep_ref[...] = (kept_ref[0].astype(F32) + got_ref[0].astype(F32)).astype(BF16)
+    send_ref[...] = (kept_ref[1].astype(F32) + got_ref[1].astype(F32)).astype(BF16)
+
+
+def pair_kernel(kept_ref, got_ref, out_ref):
+    out_ref[...] = (kept_ref[...].astype(F32) + got_ref[...].astype(F32)).astype(BF16)
+
+
 def gather_kernel(inside_ref, carried_ref, out_ref):
-    total = jnp.sum(inside_ref[...].astype(F32), axis=0)
-    for r in range(inside_ref.shape[0]):
+    core, y_lo = lax.axis_index("core"), lax.axis_index("y_lo")
+    for r in range(carried_ref.shape[0]):
         for bit in range(2):
             for m in range(2):
-                at, of = map_row(bit, m, r), (bit * 2 + m) * 16
-                add = carried_ref[r, of : of + 16].astype(F32)
-                out_ref[at : at + 16] = (total[at : at + 16] + add).astype(BF16)
+                of, to = (bit * 2 + m) * 16, (r % 2) * 16
+                out_ref[bit, m, r // 4, (r // 2) % 2, to : to + 16] = carried_ref[r, of : of + 16]
+    total = jnp.sum(inside_ref[...].astype(F32), axis=0)
+    for m in range(2):
+        for high in range(2):
+            at = (m * 2 + high) * 32
+            here = out_ref[core, m, high, y_lo].astype(F32)
+            out_ref[core, m, high, y_lo] = (here + total[at : at + 32]).astype(BF16)
 
 
 def grads_kernel(
@@ -250,8 +263,7 @@
         cost_estimate=pl.CostEstimate(flops=2 * flops, bytes_accessed=3 << 20, transcendentals=0),
     )(q, k, v, g, gates)
     received = exchange(sent.reshape(near, share, 2 * width + PAD, width), NEAR)
-    rows = 2 * share * width
-    payload = jax.ShapeDtypeStruct((near, rows + inside_rows(heads) + inside_rows(share), width), BF16)
+    rows, quarter = 2 * share * width, inside_rows(heads) // 4
     full = pl.BlockSpec((length, heads * width), lambda i: (0, 0))
     fk, query_inside, key_inside, value_inside, inside = pl.pallas_call(
         functools.partial(inside_kernel, key_scale, map_scale),
@@ -259,19 +271,43 @@
         in_specs=[full] * 4
         + [pl.BlockSpec((heads, length), lambda i: (0, 0))]
         + [pl.BlockSpec((heads, width, width), lambda i: (0, 0, 0))] * 2,
-        out_specs=[full] * 4 + [pl.BlockSpec((near, inside_rows(heads), width), lambda i: (0, 1, 0))],
-        out_shape=[wide_shape] + [sum_shape] * 3 + [payload],
+        out_specs=[full] * 4 + [pl.BlockSpec((4, near, quarter, width), lambda i: (0, 0, 0, 0))],
+        out_shape=[wide_shape] + [sum_shape] * 3 + [jax.ShapeDtypeStruct((4, near, quarter, width), BF16)],
         cost_estimate=pl.CostEstimate(flops=9 * flops, bytes_accessed=8 << 20, transcendentals=1 << 18),
     )(q, k, v, g, gates, query_map, key_map)
+    swap = [(0, 1), (1, 0)]
+    got = lax.ppermute(inside[2:], "core", swap)
+    part = jax.ShapeDtypeStruct((near, quarter, width), BF16)
+    half = pl.BlockSpec((2, near, quarter, width), lambda i: (0, 0, 0, 0))
+    whole_part = pl.BlockSpec((near, quarter, width), lambda i: (0, 0, 0))
+    keep, send = pl.pallas_call(
+        halve_kernel,
+        grid=(1,),
+        in_specs=[half, half],
+        out_specs=[whole_part] * 2,
+        out_shape=[part, part],
+        compiler_params=VMEM,
+    )(inside, got)
+    got = lax.ppermute(send, "y_lo", swap)
+    payload = jax.ShapeDtypeStruct((near, rows + quarter + inside_rows(share), width), BF16)
+    mixed = pl.pallas_call(
+        pair_kernel,
+        grid=(1,),
+        in_specs=[whole_part] * 2,
+        out_specs=pl.BlockSpec((near, quarter, width), lambda i: (0, rows // quarter, 0)),
+        out_shape=payload,
+        compiler_params=VMEM,
+    )(keep, got)
+    whole = pl.BlockSpec(memory_space=pltpu.VMEM)
     blocks, totals = pl.pallas_call(
         functools.partial(totals_kernel, key_scale),
+        in_specs=[whole] * 3 + [pl.BlockSpec(memory_space=pl.ANY)],
         out_shape=[
             jax.ShapeDtypeStruct((near, share, 2 * width, width), BF16),
             jax.ShapeDtypeStruct((outer, share, width + 2 * PAD, width), BF16),
         ],
-    )(received, query_map, key_map)
+    )(received, query_map, key_map, inside)
     totals = exchange(totals, "outer")
-    whole = pl.BlockSpec(memory_space=pltpu.VMEM)
     spread = pl.pallas_call(
         functools.partial(spread_kernel, key_scale, map_scale),
         in_specs=[whole, whole, whole, pl.BlockSpec(memory_space=pl.ANY)],
@@ -283,21 +319,23 @@
             pltpu.SemaphoreType.DMA((2,)),
         ],
         input_output_aliases={3: 0},
-    )(received, blocks, totals, inside)
+        compiler_params=VMEM,
+    )(received, blocks, totals, mixed)
     carried = exchange(spread, NEAR)
-    tail = (rows + inside_rows(heads)) // inside_rows(share)
+    tail = (rows + quarter) // inside_rows(share)
     maps = pl.pallas_call(
         gather_kernel,
         grid=(1,),
         in_specs=[
-            pl.BlockSpec((near, inside_rows(heads), width), lambda i: (0, 1, 0)),
+            pl.BlockSpec((near, quarter, width), lambda i: (0, rows // quarter, 0)),
             pl.BlockSpec((near, inside_rows(share), width), lambda i: (0, tail, 0)),
         ],
-        out_specs=pl.BlockSpec((inside_rows(heads), width), lambda i: (0, 0)),
-        out_shape=jax.ShapeDtypeStruct((inside_rows(heads), width), BF16),
+        out_specs=pl.BlockSpec((2, 2, 2, 2, 32, width), lambda i: (0, 0, 0, 0, 0, 0)),
+        out_shape=jax.ShapeDtypeStruct((2, 2, 2, 2, 32, width), BF16),
+        compiler_params=VMEM,
     )(carried, carried)
     maps = exchange(maps.reshape(2, inside_rows(heads) // 2, width), "core")
-    maps = exchange(add_up(maps, BF16).reshape(32, 8, width), ("y", "outer"))
+    maps = exchange(add_up(maps, BF16).reshape(32, 8, width), ("y_hi", "y_lo", "outer"))
     query_grad, key_grad, value_grad = pl.pallas_call(
         functools.partial(grads_kernel, key_scale),
         grid=(steps,),
@@ -313,7 +351,7 @@
 
 
 def solution(mesh):
-    fine = Mesh(np.asarray(mesh.devices).reshape(8, 2, 4, 2, 4), DP + CONTEXT)
+    fine = Mesh(np.asarray(mesh.devices).reshape(4, 2, 2, 4, 2, 4), DP + CONTEXT)
     split = P(DP, CONTEXT, None)
     return jax.shard_map(
         per_device,

time: 118 us -> 106 us (0.90)
  blocking collectives: 56.9 us -> 30.2 us
  starting transfers between devices: 24.6 us -> 34.3 us
  waiting for transfers between devices: 5.08 us -> 10.6 us
  Pallas kernels: 29.5 us -> 25.5 us
  local copies, waits for them, and re-layouts: 0.71 us -> 4.32 us
    all_to_all x3 -> x2, blocking collectives: 56.9 us -> 30.2 us  [exchange(): return lax.all_to_all(value, axes, 0, 0, tiled=True)]
    ppermute x0 -> x2, starting transfers between devices: none -> 9.14 us  [the longest x1 5.81 us: per_device(): got = lax.ppermute(inside[2:], 'core', swap)]
    ppermute x0 -> x2, waiting for transfers between devices: none -> 5.48 us  [the longest x1 5.48 us: per_device(): got = lax.ppermute(send, 'y_lo', swap)]
    unnamed x2 -> x10, local copies, waits for them, and re-layouts: 0.71 us -> 3.25 us
    pallas_call x1, Pallas kernels: 3.32 us -> 1.02 us  [per_device(): pl.pallas_call(functools.partial(spread_kernel, key_scale, map_scale), in...]
    pallas_call x2 -> x4, Pallas kernels: 5.11 us -> 3.42 us  [the longest x1 3.08 us: per_device(): pl.pallas_call(functools.partial(totals_kernel, key_scale), in_specs=[who...]
    all_to_all x2 -> x3, starting transfers between devices: 24.6 us -> 25.1 us  [exchange(): return lax.all_to_all(value, axes, 0, 0, tiled=True)]
    all_to_all x2 -> x3, waiting for transfers between devices: 5.08 us -> 5.08 us  [exchange(): return lax.all_to_all(value, axes, 0, 0, tiled=True)]
  transfers between devices with their start and end apart: 2 -> 5, of which waited for: 1 -> 2; matrix products, arithmetic and copies ran while one was open for 0% -> 1% of each run, Pallas kernels for 14% -> 18%
where the time goes in v4:
time: 106 us
  starting transfers between devices  34.3 us (32%)
  blocking collectives  30.2 us (28%)
  Pallas kernels  25.5 us (24%)
  waiting for transfers between devices  10.6 us (10%)
  local copies, waits for them, and re-layouts  4.32 us (4%)
    all_to_all x2, blocking collectives, exchange(): return lax.all_to_all(value, axes, 0, 0, tiled=True)  30.2 us
    all_to_all x3, starting transfers between devices, exchange(): return lax.all_to_all(value, axes, 0, 0, tiled=True)  25.1 us
    pallas_call x1, Pallas kernels, per_device(): pl.pallas_call(functools.partial(inside_kernel, key_scale, map_scale), gr...  10 us
    pallas_call x1, Pallas kernels, per_device(): pl.pallas_call(functools.partial(grads_kernel, key_scale), grid=(steps,),...  6.1 us
    ppermute x1, starting transfers between devices, per_device(): got = lax.ppermute(inside[2:], 'core', swap)  5.81 us
    ppermute x1, waiting for transfers between devices, per_device(): got = lax.ppermute(send, 'y_lo', swap)  5.48 us
    all_to_all x3, waiting for transfers between devices, exchange(): return lax.all_to_all(value, axes, 0, 0, tiled=True)  5.08 us
    pallas_call x1, Pallas kernels, per_device(): pl.pallas_call(products_kernel, grid=(steps,), in_specs=[wide, wide, wide...  3.73 us
  transfers between devices with their start and end apart: 5, of which 2 were waited for; matrix products, arithmetic and copies ran while one was open for 1% of the time, Pallas kernels for 18%

profile of v4, /device:TPU:1, one launch (start us, length us, event | category | flops | bytes accessed | tf_op | source)
XLA Modules:
  0.0 105.6 jit_solution(11482472129310619838)
XLA Ops:
  0.6 3.7 %shard_map.103 = bf16[16,264,128]{2,1,0:T(8,128)(2,1)} custom-call(bf16[128,2048]{1,0:T(8,128)(2,1)} %bitcast.19, bf16[128,2048]{1,0:T(8,128)(2,1)} %bitcast.21, bf16[128,2048]{1,0:T(8,128)(2,1)} %bitcast.12, bf16[128,2048]{1,0:T(8,128)(2,1)} %bitcast.15, f32[16,128]{1,0:T(8,128)} %bitcast.23), custom_call_target="tpu_custom_call" | custom-call | flops 134217728 | bytes 3145728 | tf_op jit(solution)/shard_map/pallas_call | solution.py:257
  4.4 6.6 %all-to-all-start = ((bf16[8,2,264,128]{3,2,1,0:T(8,128)(2,1)}), bf16[8,2,264,128]{3,2,1,0:T(8,128)(2,1)S(1)}, u32[]{:S(2)}, u32[]{:S(2)}) async-start(bf16[8,2,264,128]{3,2,1,0:T(8,128)(2,1)} %bitcast.18), calls=%async_computation | async-start | bytes 2162688 | tf_op jit(solution)/shard_map/all_to_all | solution.py:238
  11.0 10.0 %shard_map.102 = (bf16[128,2048]{1,0:T(8,128)(2,1)}, f32[128,2048]{1,0:T(8,128)}, f32[128,2048]{1,0:T(8,128)}, f32[128,2048]{1,0:T(8,128)}, bf16[4,8,128,128]{3,2,1,0:T(8,128)(2,1)}) custom-call(bf16[128,2048]{1,0:T(8,128)(2,1)} %bitcast.20, bf16[128,2048]{1,0:T(8,128)(2,1)} %bitcast.22, bf16[128,2048]{1,0:T(8,128)(2,1)} %bitcast.13, ...), custom_call_target="tpu_custom_call" | custom-call | flops 603979776 | bytes 8388608 | tf_op jit(solution)/shard_map/pallas_call | solution.py:268
  21.0 1.1 %slice.3 = bf16[2,8,128,128]{3,2,1,0:T(8,128)(2,1)S(1)} slice(bf16[4,8,128,128]{3,2,1,0:T(8,128)(2,1)} %get-tuple-element.20.inside_ref.kept_ref), slice={[2:4], [0:8], [0:128], [0:128]} | slice | bytes 1048576 | tf_op jit(solution)/shard_map/slice | solution.py:279
  22.1 0.0 copy-start.3
  22.1 5.8 %collective-permute-start = (bf16[2,8,128,128]{3,2,1,0:T(8,128)(2,1)S(1)}, bf16[2,8,128,128]{3,2,1,0:T(8,128)(2,1)S(1)}, u32[]{:S(2)}, u32[]{:S(2)}) collective-permute-start(bf16[2,8,128,128]{3,2,1,0:T(8,128)(2,1)S(1)} %slice.3), channel_id=1, source_target_pairs={{0,32},{32,0},{1,33},{33,1},{2,34},{34,2},{3,35},{35,3},{4,36},{36... | collective-permute-start | bytes 1572872 | tf_op jit(solution)/shard_map/ppermute | solution.py:279
  27.9 0.0 all-to-all-done.in_ref
  27.9 0.0 copy-start.1
  27.9 1.0 copy-done.1
  29.0 3.1 %shard_map.104 = (bf16[8,2,256,128]{3,2,1,0:T(8,128)(2,1)}, bf16[4,2,144,128]{3,2,1,0:T(8,128)(2,1)}) custom-call(bf16[8,2,264,128]{3,2,1,0:T(8,128)(2,1)} %copy-done.1, bf16[16,128,128]{2,1,0:T(8,128)(2,1)} %mq_ref.5, bf16[16,128,128]{2,1,0:T(8,128)(2,1)} %mk_ref.5, bf16[4,8,128,128]{3,2,1,0:T(8,128)(2,1)} %get-tuple-element.20.inside_ref.kept_ref), custom_call_target="tpu_custom_call" | custom-call | tf_op jit(solution)/shard_map/pallas_call | solution.py:302
  32.0 7.5 %all-to-all-start.1 = ((bf16[4,2,144,128]{3,2,1,0:T(8,128)(2,1)}), bf16[4,2,144,128]{3,2,1,0:T(8,128)(2,1)S(1)}, u32[]{:S(2)}, u32[]{:S(2)}) async-start(bf16[4,2,144,128]{3,2,1,0:T(8,128)(2,1)} %get-tuple-element.22), calls=%async_computation.1 | async-start | bytes 589824 | tf_op jit(solution)/shard_map/all_to_all | solution.py:238
  39.5 0.0 copy-start.2
  39.5 0.0 collective-permute-done.got_ref
  39.5 0.0 copy-done.3
  39.5 0.1 shard_map.105
  39.7 3.3 %collective-permute-start.1 = (bf16[8,128,128]{2,1,0:T(8,128)(2,1)S(1)}, bf16[8,128,128]{2,1,0:T(8,128)(2,1)S(1)}, u32[]{:S(2)}, u32[]{:S(2)}) collective-permute-start(bf16[8,128,128]{2,1,0:T(8,128)(2,1)S(1)} %get-tuple-element.24), channel_id=1, source_target_pairs={{0,64},{64,0},{1,65},{65,1},{2,66},{66,2},{3,67},{67,3},{4,68},{68... | collective-permute-start | bytes 786440 | tf_op jit(solution)/shard_map/ppermute | solution.py:291
  43.0 5.5 %collective-permute-done.1.got_ref = bf16[8,128,128]{2,1,0:T(8,128)(2,1)S(1)} collective-permute-done((bf16[8,128,128]{2,1,0:T(8,128)(2,1)S(1)}, bf16[8,128,128]{2,1,0:T(8,128)(2,1)S(1)}, u32[]{:S(2)}, u32[]{:S(2)}) %collective-permute-start.1) | collective-permute-done | bytes 262176 | tf_op jit(solution)/shard_map/ppermute | solution.py:291
  48.5 0.1 shard_map.106.inside_ref
  48.6 0.0 all-to-all-done.1.totals_ref
  48.6 0.0 copy-done.2
  48.6 0.0 copy-start.4
  48.7 1.2 %copy-done.4 = bf16[8,2,256,128]{3,2,1,0:T(8,128)(2,1)S(1)} copy-done((bf16[8,2,256,128]{3,2,1,0:T(8,128)(2,1)S(1)}, bf16[8,2,256,128]{3,2,1,0:T(8,128)(2,1)}, u32[]{:S(2)}) %copy-start.4) | copy-done | bytes 1048600
  49.9 1.0 shard_map.107
  50.9 23.4 %all_to_all.25.in_ref.inside_ref.carried_ref = bf16[8,704,128]{2,1,0:T(8,128)(2,1)S(1)} all-to-all(bf16[8,704,128]{2,1,0:T(8,128)(2,1)S(1)} %shard_map.107), channel_id=1, replica_groups=mesh['y_hi'=4,'y_lo'=2,'core'=2,'outer'=4,'inner'=2,'x'=4] {'inner','x'}, dimensions={0} | all-to-all | bytes 2883584 | tf_op jit(solution)/shard_map/all_to_all | solution.py:238
  74.3 0.0 copy-start
  74.3 0.1 shard_map.109
  74.4 1.0 copy-done
  75.4 6.8 %all_to_all.26.in_ref = bf16[2,256,128]{2,1,0:T(8,128)(2,1)S(1)} all-to-all(bf16[2,256,128]{2,1,0:T(8,128)(2,1)S(1)} %bitcast.11), channel_id=1, replica_groups=mesh['y_hi'=4,'y_lo'=2,'core'=2,'outer'=4,'inner'=2,'x'=4] {'core'}, dimensions={0} | all-to-all | bytes 262144 | tf_op jit(solution)/shard_map/all_to_all | solution.py:238
  82.2 0.6 shard_map.110
  82.9 11.0 %all-to-all-start.4 = ((bf16[32,8,128]{2,1,0:T(8,128)(2,1)}), bf16[32,8,128]{2,1,0:T(8,128)(2,1)S(1)}, u32[]{:S(2)}, u32[]{:S(2)}) async-start(bf16[32,8,128]{2,1,0:T(8,128)(2,1)} %bitcast.10), calls=%async_computation.4 | async-start | bytes 131072 | tf_op jit(solution)/shard_map/all_to_all | solution.py:238
  93.8 6.1 %shard_map.108 = (bf16[128,2048]{1,0:T(8,128)(2,1)}, bf16[128,2048]{1,0:T(8,128)(2,1)}, bf16[128,2048]{1,0:T(8,128)(2,1)}) custom-call(bf16[128,2048]{1,0:T(8,128)(2,1)} %bitcast.14, bf16[128,2048]{1,0:T(8,128)(2,1)} %bitcast.17, bf16[128,2048]{1,0:T(8,128)(2,1)} %get-tuple-element.16.fk_ref, f32[16,128]{1,0:T(8,128)} %bitcast.25, ...), custom_call_target="tpu_custom_call" | custom-call | flops 335544320 | bytes 8388608 | tf_op jit(solution)/shard_map/pallas_call | solution.py:339
  99.9 5.1 %all-to-all-done.4.in_ref = bf16[32,8,128]{2,1,0:T(8,128)(2,1)S(1)} async-done(((bf16[32,8,128]{2,1,0:T(8,128)(2,1)}), bf16[32,8,128]{2,1,0:T(8,128)(2,1)S(1)}, u32[]{:S(2)}, u32[]{:S(2)}) %all-to-all-start.4) | async-done | bytes 65568 | tf_op jit(solution)/shard_map/all_to_all | solution.py:238
  105.0 0.6 shard_map.111
Async XLA Ops:
  4.4 23.6 %all-to-all-start = ((bf16[8,2,264,128]{3,2,1,0:T(8,128)(2,1)}), bf16[8,2,264,128]{3,2,1,0:T(8,128)(2,1)S(1)}, u32[]{:S(2)}, u32[]{:S(2)}) async-start(bf16[8,2,264,128]{3,2,1,0:T(8,128)(2,1)} %bitcast.18), calls=%async_computation | async-start | bytes 2162688 | tf_op jit(solution)/shard_map/all_to_all | solution.py:238
  22.1 17.4 %copy-start.3 = (bf16[4,8,128,128]{3,2,1,0:T(8,128)(2,1)S(1)}, bf16[4,8,128,128]{3,2,1,0:T(8,128)(2,1)}, u32[]{:S(2)}) copy-start(bf16[4,8,128,128]{3,2,1,0:T(8,128)(2,1)} %get-tuple-element.20.inside_ref.kept_ref) | copy-start | bytes 3145732
  22.1 17.4 %collective-permute-start = (bf16[2,8,128,128]{3,2,1,0:T(8,128)(2,1)S(1)}, bf16[2,8,128,128]{3,2,1,0:T(8,128)(2,1)S(1)}, u32[]{:S(2)}, u32[]{:S(2)}) collective-permute-start(bf16[2,8,128,128]{3,2,1,0:T(8,128)(2,1)S(1)} %slice.3), channel_id=1, source_target_pairs={{0,32},{32,0},{1,33},{33,1},{2,34},{34,2},{3,35},{35,3},{4,36},{36... | collective-permute-start | bytes 1572872 | tf_op jit(solution)/shard_map/ppermute | solution.py:279
  27.9 1.0 copy-start.1
  32.0 16.6 %all-to-all-start.1 = ((bf16[4,2,144,128]{3,2,1,0:T(8,128)(2,1)}), bf16[4,2,144,128]{3,2,1,0:T(8,128)(2,1)S(1)}, u32[]{:S(2)}, u32[]{:S(2)}) async-start(bf16[4,2,144,128]{3,2,1,0:T(8,128)(2,1)} %get-tuple-element.22), calls=%async_computation.1 | async-start | bytes 589824 | tf_op jit(solution)/shard_map/all_to_all | solution.py:238
  39.5 9.1 %copy-start.2 = (bf16[8,2,264,128]{3,2,1,0:T(8,128)(2,1)S(1)}, bf16[8,2,264,128]{3,2,1,0:T(8,128)(2,1)}, u32[]{:S(2)}) copy-start(bf16[8,2,264,128]{3,2,1,0:T(8,128)(2,1)} %copy-done.1) | copy-start | bytes 3244036
  39.7 8.8 %collective-permute-start.1 = (bf16[8,128,128]{2,1,0:T(8,128)(2,1)S(1)}, bf16[8,128,128]{2,1,0:T(8,128)(2,1)S(1)}, u32[]{:S(2)}, u32[]{:S(2)}) collective-permute-start(bf16[8,128,128]{2,1,0:T(8,128)(2,1)S(1)} %get-tuple-element.24), channel_id=1, source_target_pairs={{0,64},{64,0},{1,65},{65,1},{2,66},{66,2},{3,67},{67,3},{4,68},{68... | collective-permute-start | bytes 786440 | tf_op jit(solution)/shard_map/ppermute | solution.py:291
  48.6 1.2 %copy-start.4 = (bf16[8,2,256,128]{3,2,1,0:T(8,128)(2,1)S(1)}, bf16[8,2,256,128]{3,2,1,0:T(8,128)(2,1)}, u32[]{:S(2)}) copy-start(bf16[8,2,256,128]{3,2,1,0:T(8,128)(2,1)} %get-tuple-element.21.blocks_ref) | copy-start | bytes 3145732
  74.3 1.1 %copy-start = (bf16[8,704,128]{2,1,0:T(8,128)(2,1)}, bf16[8,704,128]{2,1,0:T(8,128)(2,1)S(1)}, u32[]{:S(2)}) copy-start(bf16[8,704,128]{2,1,0:T(8,128)(2,1)S(1)} %all_to_all.25.in_ref.inside_ref.carried_ref) | copy-start | bytes 4325380
  82.9 22.1 %all-to-all-start.4 = ((bf16[32,8,128]{2,1,0:T(8,128)(2,1)}), bf16[32,8,128]{2,1,0:T(8,128)(2,1)S(1)}, u32[]{:S(2)}, u32[]{:S(2)}) async-start(bf16[32,8,128]{2,1,0:T(8,128)(2,1)} %bitcast.10), calls=%async_computation.4 | async-start | bytes 131072 | tf_op jit(solution)/shard_map/all_to_all | solution.py:238

commit v5 on v4

--- a/solution.py
+++ b/solution.py
@@ -61,36 +61,50 @@
         out_ref[to, 2 * width :] = jnp.broadcast_to(closing, (PAD, width)).astype(BF16)
 
 
+def owned_heads():
+    x = lax.axis_index("x")
+    return (lax.axis_index("inner") * 2 + x // 2) * 4 + x % 2
+
+
 def inside_kernel(
-    key_scale, map_scale, q_ref, k_ref, v_ref, g_ref, gates_ref, mq_ref, mk_ref, fk_ref, qb_ref, kb_ref, vg_ref, out_ref
+    key_scale, map_scale, q_ref, k_ref, v_ref, g_ref, gates_ref, mq_ref, mk_ref,
+    fq_ref, fk_ref, qb_ref, kb_ref, keep_ref, send_ref, own_ref,
 ):
     heads, width = mq_ref.shape[0], mq_ref.shape[1]
     core, y_lo = lax.axis_index("core"), lax.axis_index("y_lo")
+    first = owned_heads()
+    for bit in range(2):
+        own_ref[0, bit] = mq_ref[first + 2 * bit]
+        own_ref[1, bit] = mk_ref[first + 2 * bit]
     causal = causal_mask(q_ref.shape[0])
     columns = running_columns(gates_ref[...])
     rows = running_rows(gates_ref[...])
     for j in range(heads):
         lanes = slice(j * width, (j + 1) * width)
         owner, bit = place(j)
-        side = 2 * lax.bitwise_xor(core, bit) + lax.bitwise_xor(y_lo, (owner // 2) % 2)
         within = jnp.exp(jnp.where(causal, columns[:, j : j + 1] - rows[j : j + 1], -1e30))
         q, k, v, g = q_ref[:, lanes], k_ref[:, lanes], v_ref[:, lanes], g_ref[:, lanes]
         fq = dot(q, mq_ref[j], (1, 0)).astype(BF16)
         fk = (dot(k, mk_ref[j], (1, 0)) * key_scale).astype(BF16)
-        scores = (dot(fq, fk, (1, 1)) * within).astype(BF16)
         grad_scores = (dot(g, v, (1, 1)) * within).astype(BF16)
         query_back = dot(grad_scores, fk, (1, 0))
         key_back = dot(grad_scores, fq, (0, 0)) * key_scale
+        fq_ref[:, lanes] = fq
         fk_ref[:, lanes] = fk
         qb_ref[:, lanes] = query_back
         kb_ref[:, lanes] = key_back
-        vg_ref[:, lanes] = dot(scores, g, (0, 0))
-        for m, (x, back) in enumerate(((q, query_back), (k, key_back))):
-            part = dot(x, back.astype(BF16), (0, 0)) * map_scale
-            at = ((m * 2 + owner // 4) * 2 + owner % 2) * 16
-            for b in range(width // 8):
-                to = at + (b // 8) * 8
-                out_ref[side, b % 8, to : to + 8] = part[8 * b : 8 * b + 8].astype(BF16)
+        parts = [dot(x, back.astype(BF16), (0, 0)) * map_scale for x, back in ((q, query_back), (k, key_back))]
+        side = lax.bitwise_xor(y_lo, (owner // 2) % 2)
+
+        def store(ref, parts=parts, side=side, owner=owner):
+            for m in range(2):
+                at = ((m * 2 + owner // 4) * 2 + owner % 2) * 16
+                for b in range(width // 8):
+                    to = at + (b // 8) * 8
+                    ref[side, b % 8, to : to + 8] = parts[m][8 * b : 8 * b + 8].astype(BF16)
+
+        pl.when(core == bit)(functools.partial(store, keep_ref))
+        pl.when(core != bit)(functools.partial(store, send_ref))
 
 
 def over(decay, value):
@@ -98,25 +112,29 @@
     return (decay[None] * value.reshape(rows // PAD, PAD, width)).reshape(rows, width)
 
 
-def totals_kernel(key_scale, in_ref, mq_ref, mk_ref, inside_ref, blocks_ref, out_ref):
-    del inside_ref
+def decay_of(ref, r, h, width):
+    return jnp.exp(ref[r, h, 2 * width :].astype(F32))
+
+
+def block_state(key_scale, in_ref, own_ref, r, h, width):
+    return dot(own_ref[1, h], in_ref[r, h, width : 2 * width], (0, 0)) * key_scale
+
+
+def block_grad(in_ref, own_ref, r, h, width):
+    return dot(own_ref[0, h], in_ref[r, h, 0:width], (0, 0))
+
+
+def totals_kernel(key_scale, in_ref, own_ref, out_ref):
     near, heads, width = in_ref.shape[0], in_ref.shape[1], in_ref.shape[3]
     mine = lax.axis_index("outer")
-    pair = lax.axis_index("inner") * 2 + lax.axis_index("x") // 2
-    first = pair * 4 + lax.axis_index("x") % 2
     for h in range(heads):
-        mq, mk = mq_ref[first + 2 * h], mk_ref[first + 2 * h]
         ahead = jnp.zeros((width, width), F32)
         back = jnp.zeros((width, width), F32)
         log = jnp.zeros((PAD, width), F32)
         for r in range(near):
             b = near - 1 - r
-            state = dot(mk, in_ref[r, h, width : 2 * width], (0, 0)) * key_scale
-            grad = dot(mq, in_ref[b, h, 0:width], (0, 0))
-            blocks_ref[r, h, 0:width] = state.astype(BF16)
-            blocks_ref[b, h, width:] = grad.astype(BF16)
-            ahead = over(jnp.exp(in_ref[r, h, 2 * width :].astype(F32)), ahead) + state
-            back = over(jnp.exp(in_ref[b, h, 2 * width :].astype(F32)), back) + grad
+            ahead = over(decay_of(in_ref, r, h, width), ahead) + block_state(key_scale, in_ref, own_ref, r, h, width)
+            back = over(decay_of(in_ref, b, h, width), back) + block_grad(in_ref, own_ref, b, h, width)
             log = log + in_ref[r, h, 2 * width :].astype(F32)
         coarse = log.astype(BF16)
         fine = (log - coarse.astype(F32)).astype(BF16)
@@ -127,7 +145,7 @@
 
 
 def spread_kernel(
-    key_scale, map_scale, in_ref, blocks_ref, totals_ref, inside_ref, out_ref, states_ref, maps_ref, sems
+    key_scale, map_scale, in_ref, own_ref, totals_ref, inside_ref, out_ref, states_ref, maps_ref, sems
 ):
     near, heads, width = in_ref.shape[0], in_ref.shape[1], in_ref.shape[3]
     groups = totals_ref.shape[0]
@@ -155,10 +173,9 @@
             sums[0] = sums[0] + dot(in_ref[r, h, 0:width], state_in, (1, 1))
             sums[1] = sums[1] + dot(in_ref[b, h, width : 2 * width], grad_in, (1, 1))
             if r < near - 1:
-                ahead = over(jnp.exp(in_ref[r, h, 2 * width :].astype(F32)), ahead) + blocks_ref[
-                    r, h, 0:width
-                ].astype(F32)
-                back = over(jnp.exp(in_ref[b, h, 2 * width :].astype(F32)), back) + blocks_ref[b, h, width:].astype(F32)
+                state = block_state(key_scale, in_ref, own_ref, r, h, width)
+                ahead = over(decay_of(in_ref, r, h, width), ahead) + state
+                back = over(decay_of(in_ref, b, h, width), back) + block_grad(in_ref, own_ref, b, h, width)
         for m, scale in enumerate((map_scale, map_scale * key_scale)):
             part = sums[m] * scale
             for b in range(width // 8):
@@ -205,22 +222,27 @@
 
 
 def grads_kernel(
-    key_scale, v_ref, g_ref, fk_ref, gates_ref, mq_ref, mk_ref, qb_ref, kb_ref, vgi_ref, in_ref, qg_ref, kg_ref, vg_ref
+    key_scale, v_ref, g_ref, fq_ref, fk_ref, gates_ref, mq_ref, mk_ref, qb_ref, kb_ref, in_ref, qg_ref, kg_ref, vg_ref
 ):
     width = mq_ref.shape[1]
     length = fk_ref.shape[0]
+    causal = causal_mask(length)
     columns = running_columns(gates_ref[...])
+    rows = running_rows(gates_ref[...])
     for j in range(GROUP):
         lanes = slice(j * width, (j + 1) * width)
         owner, bit = place(j)
         run = columns[:, j : j + 1]
+        within = jnp.exp(jnp.where(causal, run - rows[j : j + 1], -1e30))
         start = jnp.exp(run)
         end = jnp.exp(run[length - 1 : length] - run)
         state_in = in_ref[owner, 2 * bit * width : (2 * bit + 1) * width]
         grad_in = in_ref[owner, (2 * bit + 1) * width : (2 * bit + 2) * width]
-        query_back = (qb_ref[:, lanes] + dot(g_ref[:, lanes], state_in, (1, 1)) * start).astype(BF16)
+        g, fk = g_ref[:, lanes], fk_ref[:, lanes]
+        scores = (dot(fq_ref[:, lanes], fk, (1, 1)) * within).astype(BF16)
+        query_back = (qb_ref[:, lanes] + dot(g, state_in, (1, 1)) * start).astype(BF16)
         key_back = (kb_ref[:, lanes] + dot(v_ref[:, lanes], grad_in, (1, 1)) * (end * key_scale)).astype(BF16)
-        vg_ref[:, lanes] = (vgi_ref[:, lanes] + dot(fk_ref[:, lanes], grad_in, (1, 0)) * end).astype(BF16)
+        vg_ref[:, lanes] = (dot(scores, g, (0, 0)) + dot(fk, grad_in, (1, 0)) * end).astype(BF16)
         qg_ref[:, lanes] = dot(query_back, mq_ref[j], (1, 1)).astype(BF16)
         kg_ref[:, lanes] = dot(key_back, mk_ref[j], (1, 1)).astype(BF16)
 
@@ -265,20 +287,22 @@
     received = exchange(sent.reshape(near, share, 2 * width + PAD, width), NEAR)
     rows, quarter = 2 * share * width, inside_rows(heads) // 4
     full = pl.BlockSpec((length, heads * width), lambda i: (0, 0))
-    fk, query_inside, key_inside, value_inside, inside = pl.pallas_call(
+    half = pl.BlockSpec((2, near, quarter, width), lambda i: (0, 0, 0, 0))
+    half_shape = jax.ShapeDtypeStruct((2, near, quarter, width), BF16)
+    fq, fk, query_inside, key_inside, keep, send, own = pl.pallas_call(
         functools.partial(inside_kernel, key_scale, map_scale),
         grid=(1,),
         in_specs=[full] * 4
         + [pl.BlockSpec((heads, length), lambda i: (0, 0))]
         + [pl.BlockSpec((heads, width, width), lambda i: (0, 0, 0))] * 2,
-        out_specs=[full] * 4 + [pl.BlockSpec((4, near, quarter, width), lambda i: (0, 0, 0, 0))],
-        out_shape=[wide_shape] + [sum_shape] * 3 + [jax.ShapeDtypeStruct((4, near, quarter, width), BF16)],
-        cost_estimate=pl.CostEstimate(flops=9 * flops, bytes_accessed=8 << 20, transcendentals=1 << 18),
+        out_specs=[full] * 4 + [half, half, pl.BlockSpec((2, share, width, width), lambda i: (0, 0, 0, 0))],
+        out_shape=[wide_shape] * 2 + [sum_shape] * 2 + [half_shape] * 2
+        + [jax.ShapeDtypeStruct((2, share, width, width), BF16)],
+        cost_estimate=pl.CostEstimate(flops=7 * flops, bytes_accessed=8 << 20, transcendentals=1 << 18),
     )(q, k, v, g, gates, query_map, key_map)
     swap = [(0, 1), (1, 0)]
-    got = lax.ppermute(inside[2:], "core", swap)
+    got = lax.ppermute(send, "core", swap)
     part = jax.ShapeDtypeStruct((near, quarter, width), BF16)
-    half = pl.BlockSpec((2, near, quarter, width), lambda i: (0, 0, 0, 0))
     whole_part = pl.BlockSpec((near, quarter, width), lambda i: (0, 0, 0))
     keep, send = pl.pallas_call(
         halve_kernel,
@@ -287,7 +311,7 @@
         out_specs=[whole_part] * 2,
         out_shape=[part, part],
         compiler_params=VMEM,
-    )(inside, got)
+    )(keep, got)
     got = lax.ppermute(send, "y_lo", swap)
     payload = jax.ShapeDtypeStruct((near, rows + quarter + inside_rows(share), width), BF16)
     mixed = pl.pallas_call(
@@ -299,14 +323,12 @@
         compiler_params=VMEM,
     )(keep, got)
     whole = pl.BlockSpec(memory_space=pltpu.VMEM)
-    blocks, totals = pl.pallas_call(
+    totals = pl.pallas_call(
         functools.partial(totals_kernel, key_scale),
-        in_specs=[whole] * 3 + [pl.BlockSpec(memory_space=pl.ANY)],
-        out_shape=[
-            jax.ShapeDtypeStruct((near, share, 2 * width, width), BF16),
-            jax.ShapeDtypeStruct((outer, share, width + 2 * PAD, width), BF16),
-        ],
-    )(received, query_map, key_map, inside)
+        in_specs=[whole] * 2,
+        out_shape=jax.ShapeDtypeStruct((outer, share, width + 2 * PAD, width), BF16),
+        compiler_params=VMEM,
+    )(received, own)
     totals = exchange(totals, "outer")
     spread = pl.pallas_call(
         functools.partial(spread_kernel, key_scale, map_scale),
@@ -320,7 +342,7 @@
         ],
         input_output_aliases={3: 0},
         compiler_params=VMEM,
-    )(received, blocks, totals, mixed)
+    )(received, own, totals, mixed)
     carried = exchange(spread, NEAR)
     tail = (rows + quarter) // inside_rows(share)
     maps = pl.pallas_call(
@@ -339,12 +361,12 @@
     query_grad, key_grad, value_grad = pl.pallas_call(
         functools.partial(grads_kernel, key_scale),
         grid=(steps,),
-        in_specs=[wide] * 3 + [gate_spec, map_spec, map_spec] + [wide] * 3
+        in_specs=[wide] * 4 + [gate_spec, map_spec, map_spec] + [wide] * 2
         + [pl.BlockSpec((near // steps, rows, width), lambda i: (i, 0, 0))],
         out_specs=[wide] * 3,
         out_shape=[wide_shape] * 3,
-        cost_estimate=pl.CostEstimate(flops=5 * flops, bytes_accessed=8 << 20, transcendentals=0),
-    )(v, g, fk, gates, query_map, key_map, query_inside, key_inside, value_inside, carried)
+        cost_estimate=pl.CostEstimate(flops=7 * flops, bytes_accessed=8 << 20, transcendentals=0),
+    )(v, g, fq, fk, gates, query_map, key_map, query_inside, key_inside, carried)
     map_grads = add_up(maps, F32)
     shape = queries.shape
     return query_grad.reshape(shape), key_grad.reshape(shape), value_grad.reshape(shape), map_grads

time: 106 us -> 106 us (level)
  Pallas kernels: 25.5 us -> 28.3 us
  local copies, waits for them, and re-layouts: 4.32 us -> 1.93 us
  starting transfers between devices: 34.3 us -> 33 us
    pallas_call x1, Pallas kernels: 10 us -> 12.1 us  [per_device(): pl.pallas_call(functools.partial(inside_kernel, key_scale, map_scale), gr...]
    pallas_call x1, Pallas kernels: 3.08 us -> 1.2 us  [per_device(): pl.pallas_call(functools.partial(totals_kernel, key_scale), in_specs=[who...]
    pallas_call x1, Pallas kernels: 1.02 us -> 2.88 us  [per_device(): pl.pallas_call(functools.partial(spread_kernel, key_scale, map_scale), in...]
    unnamed x10 -> x8, local copies, waits for them, and re-layouts: 3.25 us -> 1.93 us
    slice x1 -> x0, local copies, waits for them, and re-layouts: 1.08 us -> none  [per_device(): got = lax.ppermute(inside[2:], 'core', swap)]
  transfers between devices with their start and end apart: 5 -> 5, of which waited for: 2 -> 2; matrix products, arithmetic and copies ran while one was open for 1% -> 0% of each run, Pallas kernels for 18% -> 19%
where the time goes in v5:
time: 106 us; the launch traced here: 105 us
  starting transfers between devices  33 us (31%)
  blocking collectives  31.2 us (29%)
  Pallas kernels  28.3 us (27%)
  waiting for transfers between devices  9.86 us (9%)
  local copies, waits for them, and re-layouts  1.93 us (2%)
    all_to_all x2, blocking collectives, exchange(): return lax.all_to_all(value, axes, 0, 0, tiled=True)  31.2 us
    all_to_all x3, starting transfers between devices, exchange(): return lax.all_to_all(value, axes, 0, 0, tiled=True)  24.1 us
    pallas_call x1, Pallas kernels, per_device(): pl.pallas_call(functools.partial(inside_kernel, key_scale, map_scale), gr...  12.1 us
    pallas_call x1, Pallas kernels, per_device(): pl.pallas_call(functools.partial(grads_kernel, key_scale), grid=(steps,),...  6.79 us
    ppermute x1, starting transfers between devices, per_device(): got = lax.ppermute(send, 'core', swap)  5.66 us
    ppermute x1, waiting for transfers between devices, per_device(): got = lax.ppermute(send, 'y_lo', swap)  5.48 us
    all_to_all x3, waiting for transfers between devices, exchange(): return lax.all_to_all(value, axes, 0, 0, tiled=True)  4.38 us
    pallas_call x1, Pallas kernels, per_device(): pl.pallas_call(products_kernel, grid=(steps,), in_specs=[wide, wide, wide...  3.7 us
  transfers between devices with their start and end apart: 5, of which 2 were waited for; matrix products, arithmetic and copies ran while one was open for 0% of the time, Pallas kernels for 19%

profile of v5, /device:TPU:1, one launch (start us, length us, event | category | flops | bytes accessed | tf_op | source)
XLA Modules:
  0.0 105.0 jit_solution(15599977288507079964)
XLA Ops:
  0.6 3.7 %shard_map.103 = bf16[16,264,128]{2,1,0:T(8,128)(2,1)} custom-call(bf16[128,2048]{1,0:T(8,128)(2,1)} %bitcast.19, bf16[128,2048]{1,0:T(8,128)(2,1)} %bitcast.21, bf16[128,2048]{1,0:T(8,128)(2,1)} %bitcast.12, bf16[128,2048]{1,0:T(8,128)(2,1)} %bitcast.15, f32[16,128]{1,0:T(8,128)} %bitcast.23), custom_call_target="tpu_custom_call" | custom-call | flops 134217728 | bytes 3145728 | tf_op jit(solution)/shard_map/pallas_call | solution.py:279
  4.3 6.6 %all-to-all-start = ((bf16[8,2,264,128]{3,2,1,0:T(8,128)(2,1)}), bf16[8,2,264,128]{3,2,1,0:T(8,128)(2,1)S(1)}, u32[]{:S(2)}, u32[]{:S(2)}) async-start(bf16[8,2,264,128]{3,2,1,0:T(8,128)(2,1)} %bitcast.18), calls=%async_computation | async-start | bytes 2162688 | tf_op jit(solution)/shard_map/all_to_all | solution.py:260
  11.0 12.1 %shard_map.102 = (bf16[128,2048]{1,0:T(8,128)(2,1)}, bf16[128,2048]{1,0:T(8,128)(2,1)}, f32[128,2048]{1,0:T(8,128)}, f32[128,2048]{1,0:T(8,128)}, bf16[2,8,128,1...) custom-call(bf16[128,2048]{1,0:T(8,128)(2,1)} %bitcast.20, ...), custom_call_target="tpu_custom_call" | custom-call | flops 469762048 | bytes 8388608 | tf_op jit(solution)/shard_map/pallas_call | solution.py:292
  23.1 5.7 %collective-permute-start = (bf16[2,8,128,128]{3,2,1,0:T(8,128)(2,1)}, bf16[2,8,128,128]{3,2,1,0:T(8,128)(2,1)S(1)}, u32[]{:S(2)}, u32[]{:S(2)}) collective-permute-start(bf16[2,8,128,128]{3,2,1,0:T(8,128)(2,1)} %get-tuple-element.22), channel_id=1, source_target_pairs={{0,32},{32,0},{1,33},{33,1},{2,34},{34,2},{3,35},{35,3},{4,36},{36... | collective-permute-start | bytes 1572872 | tf_op jit(solution)/shard_map/ppermute | solution.py:304
  28.8 0.0 all-to-all-done.in_ref
  28.8 0.0 copy-start.1
  28.8 0.9 copy-done.1
  29.7 0.0 copy-start.3
  29.7 1.2 %shard_map.104 = bf16[4,2,144,128]{3,2,1,0:T(8,128)(2,1)} custom-call(bf16[8,2,264,128]{3,2,1,0:T(8,128)(2,1)S(1)} %all-to-all-done.in_ref, bf16[2,2,128,128]{3,2,1,0:T(8,128)(2,1)S(1)} %copy-done.1), custom_call_target="tpu_custom_call" | custom-call | tf_op jit(solution)/shard_map/pallas_call | solution.py:326
  30.9 6.6 %all-to-all-start.1 = ((bf16[4,2,144,128]{3,2,1,0:T(8,128)(2,1)}), bf16[4,2,144,128]{3,2,1,0:T(8,128)(2,1)S(1)}, u32[]{:S(2)}, u32[]{:S(2)}) async-start(bf16[4,2,144,128]{3,2,1,0:T(8,128)(2,1)} %shard_map.104), calls=%async_computation.1 | async-start | bytes 589824 | tf_op jit(solution)/shard_map/all_to_all | solution.py:260
  37.5 0.0 collective-permute-done.got_ref
  37.5 0.0 copy-done.3
  37.5 0.0 copy-start.2
  37.5 0.1 shard_map.105
  37.7 3.2 %collective-permute-start.1 = (bf16[8,128,128]{2,1,0:T(8,128)(2,1)S(1)}, bf16[8,128,128]{2,1,0:T(8,128)(2,1)S(1)}, u32[]{:S(2)}, u32[]{:S(2)}) collective-permute-start(bf16[8,128,128]{2,1,0:T(8,128)(2,1)S(1)} %get-tuple-element.24), channel_id=1, source_target_pairs={{0,64},{64,0},{1,65},{65,1},{2,66},{66,2},{3,67},{67,3},{4,68},{68... | collective-permute-start | bytes 786440 | tf_op jit(solution)/shard_map/ppermute | solution.py:315
  40.9 5.5 %collective-permute-done.1.got_ref = bf16[8,128,128]{2,1,0:T(8,128)(2,1)S(1)} collective-permute-done((bf16[8,128,128]{2,1,0:T(8,128)(2,1)S(1)}, bf16[8,128,128]{2,1,0:T(8,128)(2,1)S(1)}, u32[]{:S(2)}, u32[]{:S(2)}) %collective-permute-start.1) | collective-permute-done | bytes 262176 | tf_op jit(solution)/shard_map/ppermute | solution.py:315
  46.4 0.1 shard_map.106.inside_ref
  46.5 0.0 all-to-all-done.1.totals_ref
  46.5 0.0 copy-done.2
  46.5 2.9 %shard_map.107 = bf16[8,704,128]{2,1,0:T(8,128)(2,1)S(1)} custom-call(bf16[8,2,264,128]{3,2,1,0:T(8,128)(2,1)S(1)} %all-to-all-done.in_ref, bf16[2,2,128,128]{3,2,1,0:T(8,128)(2,1)S(1)} %copy-done.2, bf16[4,2,144,128]{3,2,1,0:T(8,128)(2,1)S(1)} %all-to-all-done.1.totals_ref, ...), custom_call_target="tpu_custom_call", output_to_operand_aliasing={{}: (3, {})} | custom-call | tf_op jit(solution)/shard_map/pallas_call | solution.py:333
  49.4 24.6 %all_to_all.25.in_ref.inside_ref.carried_ref = bf16[8,704,128]{2,1,0:T(8,128)(2,1)S(1)} all-to-all(bf16[8,704,128]{2,1,0:T(8,128)(2,1)S(1)} %shard_map.107), channel_id=1, replica_groups=mesh['y_hi'=4,'y_lo'=2,'core'=2,'outer'=4,'inner'=2,'x'=4] {'inner','x'}, dimensions={0} | all-to-all | bytes 2883584 | tf_op jit(solution)/shard_map/all_to_all | solution.py:260
  74.0 0.0 copy-start
  74.0 0.1 shard_map.109
  74.1 1.0 copy-done
  75.1 6.6 %all_to_all.26.in_ref = bf16[2,256,128]{2,1,0:T(8,128)(2,1)S(1)} all-to-all(bf16[2,256,128]{2,1,0:T(8,128)(2,1)S(1)} %bitcast.11), channel_id=1, replica_groups=mesh['y_hi'=4,'y_lo'=2,'core'=2,'outer'=4,'inner'=2,'x'=4] {'core'}, dimensions={0} | all-to-all | bytes 262144 | tf_op jit(solution)/shard_map/all_to_all | solution.py:260
  81.7 0.6 shard_map.110
  82.4 10.8 %all-to-all-start.4 = ((bf16[32,8,128]{2,1,0:T(8,128)(2,1)}), bf16[32,8,128]{2,1,0:T(8,128)(2,1)S(1)}, u32[]{:S(2)}, u32[]{:S(2)}) async-start(bf16[32,8,128]{2,1,0:T(8,128)(2,1)} %bitcast.10), calls=%async_computation.4 | async-start | bytes 131072 | tf_op jit(solution)/shard_map/all_to_all | solution.py:260
  93.2 6.8 %shard_map.108 = (bf16[128,2048]{1,0:T(8,128)(2,1)}, bf16[128,2048]{1,0:T(8,128)(2,1)}, bf16[128,2048]{1,0:T(8,128)(2,1)}) custom-call(bf16[128,2048]{1,0:T(8,128)(2,1)} %bitcast.14, bf16[128,2048]{1,0:T(8,128)(2,1)} %bitcast.17, bf16[128,2048]{1,0:T(8,128)(2,1)} %get-tuple-element.16.fq_ref, bf16[128,2048]{1,0:T(8,128)(2,1)} %get-tuple-element.17.fk_ref, ...), custom_call_target="tpu_custom_call" | custom-call | flops 469762048 | bytes 8388608 | tf_op jit(solution)/shard_map/pallas_call | solution.py:361
  100.0 4.4 %all-to-all-done.4.in_ref = bf16[32,8,128]{2,1,0:T(8,128)(2,1)S(1)} async-done(((bf16[32,8,128]{2,1,0:T(8,128)(2,1)}), bf16[32,8,128]{2,1,0:T(8,128)(2,1)S(1)}, u32[]{:S(2)}, u32[]{:S(2)}) %all-to-all-start.4) | async-done | bytes 65568 | tf_op jit(solution)/shard_map/all_to_all | solution.py:260
  104.4 0.6 shard_map.111
Async XLA Ops:
  4.3 24.5 %all-to-all-start = ((bf16[8,2,264,128]{3,2,1,0:T(8,128)(2,1)}), bf16[8,2,264,128]{3,2,1,0:T(8,128)(2,1)S(1)}, u32[]{:S(2)}, u32[]{:S(2)}) async-start(bf16[8,2,264,128]{3,2,1,0:T(8,128)(2,1)} %bitcast.18), calls=%async_computation | async-start | bytes 2162688 | tf_op jit(solution)/shard_map/all_to_all | solution.py:260
  23.1 14.4 %collective-permute-start = (bf16[2,8,128,128]{3,2,1,0:T(8,128)(2,1)}, bf16[2,8,128,128]{3,2,1,0:T(8,128)(2,1)S(1)}, u32[]{:S(2)}, u32[]{:S(2)}) collective-permute-start(bf16[2,8,128,128]{3,2,1,0:T(8,128)(2,1)} %get-tuple-element.22), channel_id=1, source_target_pairs={{0,32},{32,0},{1,33},{33,1},{2,34},{34,2},{3,35},{35,3},{4,36},{36... | collective-permute-start | bytes 1572872 | tf_op jit(solution)/shard_map/ppermute | solution.py:304
  28.8 0.9 copy-start.1
  29.7 7.8 %copy-start.3 = (bf16[2,8,128,128]{3,2,1,0:T(8,128)(2,1)S(1)}, bf16[2,8,128,128]{3,2,1,0:T(8,128)(2,1)}, u32[]{:S(2)}) copy-start(bf16[2,8,128,128]{3,2,1,0:T(8,128)(2,1)} %get-tuple-element.21.kept_ref) | copy-start | bytes 1572868
  30.9 15.6 %all-to-all-start.1 = ((bf16[4,2,144,128]{3,2,1,0:T(8,128)(2,1)}), bf16[4,2,144,128]{3,2,1,0:T(8,128)(2,1)S(1)}, u32[]{:S(2)}, u32[]{:S(2)}) async-start(bf16[4,2,144,128]{3,2,1,0:T(8,128)(2,1)} %shard_map.104), calls=%async_computation.1 | async-start | bytes 589824 | tf_op jit(solution)/shard_map/all_to_all | solution.py:260
  37.5 9.0 %copy-start.2 = (bf16[2,2,128,128]{3,2,1,0:T(8,128)(2,1)S(1)}, bf16[2,2,128,128]{3,2,1,0:T(8,128)(2,1)}, u32[]{:S(2)}) copy-start(bf16[2,2,128,128]{3,2,1,0:T(8,128)(2,1)} %get-tuple-element.20.own_ref) | copy-start | bytes 393220
  37.7 8.7 %collective-permute-start.1 = (bf16[8,128,128]{2,1,0:T(8,128)(2,1)S(1)}, bf16[8,128,128]{2,1,0:T(8,128)(2,1)S(1)}, u32[]{:S(2)}, u32[]{:S(2)}) collective-permute-start(bf16[8,128,128]{2,1,0:T(8,128)(2,1)S(1)} %get-tuple-element.24), channel_id=1, source_target_pairs={{0,64},{64,0},{1,65},{65,1},{2,66},{66,2},{3,67},{67,3},{4,68},{68... | collective-permute-start | bytes 786440 | tf_op jit(solution)/shard_map/ppermute | solution.py:315
  74.0 1.1 %copy-start = (bf16[8,704,128]{2,1,0:T(8,128)(2,1)}, bf16[8,704,128]{2,1,0:T(8,128)(2,1)S(1)}, u32[]{:S(2)}) copy-start(bf16[8,704,128]{2,1,0:T(8,128)(2,1)S(1)} %all_to_all.25.in_ref.inside_ref.carried_ref) | copy-start | bytes 4325380
  82.4 22.0 %all-to-all-start.4 = ((bf16[32,8,128]{2,1,0:T(8,128)(2,1)}), bf16[32,8,128]{2,1,0:T(8,128)(2,1)S(1)}, u32[]{:S(2)}, u32[]{:S(2)}) async-start(bf16[32,8,128]{2,1,0:T(8,128)(2,1)} %bitcast.10), calls=%async_computation.4 | async-start | bytes 131072 | tf_op jit(solution)/shard_map/all_to_all | solution.py:260

commit v6 on v5

--- a/solution.py
+++ b/solution.py
@@ -68,14 +68,9 @@
 
 def inside_kernel(
     key_scale, map_scale, q_ref, k_ref, v_ref, g_ref, gates_ref, mq_ref, mk_ref,
-    fq_ref, fk_ref, qb_ref, kb_ref, keep_ref, send_ref, own_ref,
+    fq_ref, fk_ref, qb_ref, kb_ref, keep_ref, send_ref, maps_ref, sems,
 ):
     heads, width = mq_ref.shape[0], mq_ref.shape[1]
-    core, y_lo = lax.axis_index("core"), lax.axis_index("y_lo")
-    first = owned_heads()
-    for bit in range(2):
-        own_ref[0, bit] = mq_ref[first + 2 * bit]
-        own_ref[1, bit] = mk_ref[first + 2 * bit]
     causal = causal_mask(q_ref.shape[0])
     columns = running_columns(gates_ref[...])
     rows = running_rows(gates_ref[...])
@@ -93,18 +88,22 @@
         fk_ref[:, lanes] = fk
         qb_ref[:, lanes] = query_back
         kb_ref[:, lanes] = key_back
-        parts = [dot(x, back.astype(BF16), (0, 0)) * map_scale for x, back in ((q, query_back), (k, key_back))]
-        side = lax.bitwise_xor(y_lo, (owner // 2) % 2)
-
-        def store(ref, parts=parts, side=side, owner=owner):
-            for m in range(2):
-                at = ((m * 2 + owner // 4) * 2 + owner % 2) * 16
-                for b in range(width // 8):
-                    to = at + (b // 8) * 8
-                    ref[side, b % 8, to : to + 8] = parts[m][8 * b : 8 * b + 8].astype(BF16)
-
-        pl.when(core == bit)(functools.partial(store, keep_ref))
-        pl.when(core != bit)(functools.partial(store, send_ref))
+        for m, (x, back) in enumerate(((q, query_back), (k, key_back))):
+            part = dot(x, back.astype(BF16), (0, 0)) * map_scale
+            at = ((m * 2 + owner // 4) * 2 + owner % 2) * 16
+            for b in range(width // 8):
+                to = at + (b // 8) * 8
+                maps_ref[bit, (owner // 2) % 2, b % 8, to : to + 8] = part[8 * b : 8 * b + 8].astype(BF16)
+    core, y_lo = lax.axis_index("core"), lax.axis_index("y_lo")
+    copies = []
+    for side in range(2):
+        along = lax.bitwise_xor(y_lo, side)
+        copies.append(pltpu.make_async_copy(maps_ref.at[core, along], keep_ref.at[side], sems.at[2 * side]))
+        copies.append(pltpu.make_async_copy(maps_ref.at[1 - core, along], send_ref.at[side], sems.at[2 * side + 1]))
+    for copy in copies:
+        copy.start()
+    for copy in copies:
+        copy.wait()
 
 
 def over(decay, value):
@@ -116,25 +115,27 @@
     return jnp.exp(ref[r, h, 2 * width :].astype(F32))
 
 
-def block_state(key_scale, in_ref, own_ref, r, h, width):
-    return dot(own_ref[1, h], in_ref[r, h, width : 2 * width], (0, 0)) * key_scale
-
-
-def block_grad(in_ref, own_ref, r, h, width):
-    return dot(own_ref[0, h], in_ref[r, h, 0:width], (0, 0))
-
-
-def totals_kernel(key_scale, in_ref, own_ref, out_ref):
+def block_state(key_scale, in_ref, map_ref, head, r, h, width):
+    return dot(map_ref[head], in_ref[r, h, width : 2 * width], (0, 0)) * key_scale
+
+
+def block_grad(in_ref, map_ref, head, r, h, width):
+    return dot(map_ref[head], in_ref[r, h, 0:width], (0, 0))
+
+
+def totals_kernel(key_scale, in_ref, mq_ref, mk_ref, out_ref):
     near, heads, width = in_ref.shape[0], in_ref.shape[1], in_ref.shape[3]
     mine = lax.axis_index("outer")
     for h in range(heads):
+        head = owned_heads() + 2 * h
         ahead = jnp.zeros((width, width), F32)
         back = jnp.zeros((width, width), F32)
         log = jnp.zeros((PAD, width), F32)
         for r in range(near):
             b = near - 1 - r
-            ahead = over(decay_of(in_ref, r, h, width), ahead) + block_state(key_scale, in_ref, own_ref, r, h, width)
-            back = over(decay_of(in_ref, b, h, width), back) + block_grad(in_ref, own_ref, b, h, width)
+            state = block_state(key_scale, in_ref, mk_ref, head, r, h, width)
+            ahead = over(decay_of(in_ref, r, h, width), ahead) + state
+            back = over(decay_of(in_ref, b, h, width), back) + block_grad(in_ref, mq_ref, head, b, h, width)
             log = log + in_ref[r, h, 2 * width :].astype(F32)
         coarse = log.astype(BF16)
         fine = (log - coarse.astype(F32)).astype(BF16)
@@ -144,12 +145,19 @@
             out_ref[o, h, width + PAD :] = fine
 
 
-def spread_kernel(
-    key_scale, map_scale, in_ref, own_ref, totals_ref, inside_ref, out_ref, states_ref, maps_ref, sems
-):
+def blocks_kernel(key_scale, in_ref, mq_ref, mk_ref, out_ref):
+    near, heads, width = in_ref.shape[0], in_ref.shape[1], in_ref.shape[3]
+    for h in range(heads):
+        head = owned_heads() + 2 * h
+        for r in range(near):
+            out_ref[r, h, 0:width] = block_state(key_scale, in_ref, mk_ref, head, r, h, width).astype(BF16)
+            out_ref[r, h, width:] = block_grad(in_ref, mq_ref, head, r, h, width).astype(BF16)
+
+
+def spread_kernel(key_scale, map_scale, in_ref, blocks_ref, totals_ref, states_ref, maps_ref):
     near, heads, width = in_ref.shape[0], in_ref.shape[1], in_ref.shape[3]
     groups = totals_ref.shape[0]
-    mine = lax.axis_index("outer")
+    mine, core = lax.axis_index("outer"), lax.axis_index("core")
 
     def total(o, h):
         log = totals_ref[o, h, width : width + PAD].astype(F32) + totals_ref[o, h, width + PAD :].astype(F32)
@@ -173,28 +181,14 @@
             sums[0] = sums[0] + dot(in_ref[r, h, 0:width], state_in, (1, 1))
             sums[1] = sums[1] + dot(in_ref[b, h, width : 2 * width], grad_in, (1, 1))
             if r < near - 1:
-                state = block_state(key_scale, in_ref, own_ref, r, h, width)
-                ahead = over(decay_of(in_ref, r, h, width), ahead) + state
-                back = over(decay_of(in_ref, b, h, width), back) + block_grad(in_ref, own_ref, b, h, width)
+                ahead = over(decay_of(in_ref, r, h, width), ahead) + blocks_ref[r, h, 0:width].astype(F32)
+                back = over(decay_of(in_ref, b, h, width), back) + blocks_ref[b, h, width:].astype(F32)
+        side = lax.bitwise_xor(core, h)
         for m, scale in enumerate((map_scale, map_scale * key_scale)):
             part = sums[m] * scale
             for b in range(width // 8):
-                to = ((h * 2 + m) * 2 + b // 8) * 8
-                maps_ref[b % 8, to : to + 8] = part[8 * b : 8 * b + 8].astype(BF16)
-    rows = 2 * heads * width
-    start = rows + inside_rows(heads * near) // 4
-    copies = [
-        pltpu.make_async_copy(states_ref, out_ref.at[:, 0:rows], sems.at[0]),
-        pltpu.make_async_copy(maps_ref, out_ref.at[:, start : start + maps_ref.shape[1]], sems.at[1]),
-    ]
-    for copy in copies:
-        copy.start()
-    for copy in copies:
-        copy.wait()
-
-
-def inside_rows(heads):
-    return heads * 2 * 16
+                to = (m * 2 + b // 8) * 8
+                maps_ref[side, b % 8, to : to + 8] = part[8 * b : 8 * b + 8].astype(BF16)
 
 
 def halve_kernel(kept_ref, got_ref, keep_ref, send_ref):
@@ -202,23 +196,25 @@
     send_ref[...] = (kept_ref[1].astype(F32) + got_ref[1].astype(F32)).astype(BF16)
 
 
-def pair_kernel(kept_ref, got_ref, out_ref):
-    out_ref[...] = (kept_ref[...].astype(F32) + got_ref[...].astype(F32)).astype(BF16)
-
-
-def gather_kernel(inside_ref, carried_ref, out_ref):
-    core, y_lo = lax.axis_index("core"), lax.axis_index("y_lo")
-    for r in range(carried_ref.shape[0]):
-        for bit in range(2):
-            for m in range(2):
-                of, to = (bit * 2 + m) * 16, (r % 2) * 16
-                out_ref[bit, m, r // 4, (r // 2) % 2, to : to + 16] = carried_ref[r, of : of + 16]
-    total = jnp.sum(inside_ref[...].astype(F32), axis=0)
+def pair_kernel(inside_ref, inside_got_ref, carried_ref, carried_got_ref, out_ref):
+    rows = inside_ref.shape[1]
+    out_ref[:, 0:rows] = (inside_ref[...].astype(F32) + inside_got_ref[...].astype(F32)).astype(BF16)
+    out_ref[:, rows:] = (carried_ref[0].astype(F32) + carried_got_ref[...].astype(F32)).astype(BF16)
+
+
+def gather_kernel(in_ref, out_ref):
+    y_lo = lax.axis_index("y_lo")
+    rows = in_ref.shape[1] - 32
+    for r in range(in_ref.shape[0]):
+        for m in range(2):
+            of, to = rows + m * 16, (r % 2) * 16
+            out_ref[m, r // 4, (r // 2) % 2, to : to + 16] = in_ref[r, of : of + 16]
+    total = jnp.sum(in_ref[:, 0:rows].astype(F32), axis=0)
     for m in range(2):
         for high in range(2):
             at = (m * 2 + high) * 32
-            here = out_ref[core, m, high, y_lo].astype(F32)
-            out_ref[core, m, high, y_lo] = (here + total[at : at + 32]).astype(BF16)
+            here = out_ref[m, high, y_lo].astype(F32)
+            out_ref[m, high, y_lo] = (here + total[at : at + 32]).astype(BF16)
 
 
 def grads_kernel(
@@ -285,79 +281,67 @@
         cost_estimate=pl.CostEstimate(flops=2 * flops, bytes_accessed=3 << 20, transcendentals=0),
     )(q, k, v, g, gates)
     received = exchange(sent.reshape(near, share, 2 * width + PAD, width), NEAR)
-    rows, quarter = 2 * share * width, inside_rows(heads) // 4
+    rows, quarter = 2 * share * width, heads * 8
     full = pl.BlockSpec((length, heads * width), lambda i: (0, 0))
-    half = pl.BlockSpec((2, near, quarter, width), lambda i: (0, 0, 0, 0))
     half_shape = jax.ShapeDtypeStruct((2, near, quarter, width), BF16)
-    fq, fk, query_inside, key_inside, keep, send, own = pl.pallas_call(
+    anywhere = pl.BlockSpec(memory_space=pl.ANY)
+    fq, fk, query_inside, key_inside, keep, send = pl.pallas_call(
         functools.partial(inside_kernel, key_scale, map_scale),
         grid=(1,),
         in_specs=[full] * 4
         + [pl.BlockSpec((heads, length), lambda i: (0, 0))]
         + [pl.BlockSpec((heads, width, width), lambda i: (0, 0, 0))] * 2,
-        out_specs=[full] * 4 + [half, half, pl.BlockSpec((2, share, width, width), lambda i: (0, 0, 0, 0))],
-        out_shape=[wide_shape] * 2 + [sum_shape] * 2 + [half_shape] * 2
-        + [jax.ShapeDtypeStruct((2, share, width, width), BF16)],
+        out_specs=[full] * 4 + [anywhere] * 2,
+        out_shape=[wide_shape] * 2 + [sum_shape] * 2 + [half_shape] * 2,
+        scratch_shapes=[pltpu.VMEM((2, 2, near, quarter, width), BF16), pltpu.SemaphoreType.DMA((4,))],
         cost_estimate=pl.CostEstimate(flops=7 * flops, bytes_accessed=8 << 20, transcendentals=1 << 18),
     )(q, k, v, g, gates, query_map, key_map)
+    received, keep = lax.optimization_barrier((received, keep))
     swap = [(0, 1), (1, 0)]
-    got = lax.ppermute(send, "core", swap)
+    whole = pl.BlockSpec(memory_space=pltpu.VMEM)
     part = jax.ShapeDtypeStruct((near, quarter, width), BF16)
-    whole_part = pl.BlockSpec((near, quarter, width), lambda i: (0, 0, 0))
     keep, send = pl.pallas_call(
-        halve_kernel,
-        grid=(1,),
-        in_specs=[half, half],
-        out_specs=[whole_part] * 2,
-        out_shape=[part, part],
-        compiler_params=VMEM,
-    )(keep, got)
-    got = lax.ppermute(send, "y_lo", swap)
-    payload = jax.ShapeDtypeStruct((near, rows + quarter + inside_rows(share), width), BF16)
-    mixed = pl.pallas_call(
-        pair_kernel,
-        grid=(1,),
-        in_specs=[whole_part] * 2,
-        out_specs=pl.BlockSpec((near, quarter, width), lambda i: (0, rows // quarter, 0)),
-        out_shape=payload,
-        compiler_params=VMEM,
-    )(keep, got)
-    whole = pl.BlockSpec(memory_space=pltpu.VMEM)
+        halve_kernel, in_specs=[whole] * 2, out_shape=[part] * 2, compiler_params=VMEM
+    )(keep, lax.ppermute(send, "core", swap))
     totals = pl.pallas_call(
         functools.partial(totals_kernel, key_scale),
-        in_specs=[whole] * 2,
+        in_specs=[whole] * 3,
         out_shape=jax.ShapeDtypeStruct((outer, share, width + 2 * PAD, width), BF16),
         compiler_params=VMEM,
-    )(received, own)
-    totals = exchange(totals, "outer")
-    spread = pl.pallas_call(
+    )(received, query_map, key_map)
+    blocks = pl.pallas_call(
+        functools.partial(blocks_kernel, key_scale),
+        in_specs=[whole] * 3,
+        out_shape=jax.ShapeDtypeStruct((near, share, 2 * width, width), BF16),
+        cost_estimate=pl.CostEstimate(flops=2 * flops, bytes_accessed=2 << 20, transcendentals=0),
+        compiler_params=VMEM,
+    )(received, query_map, key_map)
+    totals, send = lax.optimization_barrier((exchange(totals, "outer"), send))
+    inside_got = lax.ppermute(send, "y_lo", swap)
+    states, owned = pl.pallas_call(
         functools.partial(spread_kernel, key_scale, map_scale),
-        in_specs=[whole, whole, whole, pl.BlockSpec(memory_space=pl.ANY)],
-        out_specs=pl.BlockSpec(memory_space=pl.ANY),
-        out_shape=payload,
-        scratch_shapes=[
-            pltpu.VMEM((near, rows, width), BF16),
-            pltpu.VMEM((near, inside_rows(share), width), BF16),
-            pltpu.SemaphoreType.DMA((2,)),
+        in_specs=[whole] * 3,
+        out_shape=[
+            jax.ShapeDtypeStruct((near, rows, width), BF16),
+            jax.ShapeDtypeStruct((2, near, 32, width), BF16),
         ],
-        input_output_aliases={3: 0},
-        compiler_params=VMEM,
-    )(received, own, totals, mixed)
-    carried = exchange(spread, NEAR)
-    tail = (rows + quarter) // inside_rows(share)
+        compiler_params=VMEM,
+    )(received, blocks, totals)
+    carried = exchange(states, NEAR)
+    maps = pl.pallas_call(
+        pair_kernel,
+        in_specs=[whole] * 4,
+        out_shape=jax.ShapeDtypeStruct((near, quarter + 32, width), BF16),
+        compiler_params=VMEM,
+    )(keep, inside_got, owned, lax.ppermute(owned[1], "core", swap))
+    carried, maps = lax.optimization_barrier((carried, maps))
     maps = pl.pallas_call(
         gather_kernel,
-        grid=(1,),
-        in_specs=[
-            pl.BlockSpec((near, quarter, width), lambda i: (0, rows // quarter, 0)),
-            pl.BlockSpec((near, inside_rows(share), width), lambda i: (0, tail, 0)),
-        ],
-        out_specs=pl.BlockSpec((2, 2, 2, 2, 32, width), lambda i: (0, 0, 0, 0, 0, 0)),
-        out_shape=jax.ShapeDtypeStruct((2, 2, 2, 2, 32, width), BF16),
-        compiler_params=VMEM,
-    )(carried, carried)
-    maps = exchange(maps.reshape(2, inside_rows(heads) // 2, width), "core")
-    maps = exchange(add_up(maps, BF16).reshape(32, 8, width), ("y_hi", "y_lo", "outer"))
+        in_specs=[whole],
+        out_shape=jax.ShapeDtypeStruct((2, 2, 2, 32, width), BF16),
+        compiler_params=VMEM,
+    )(exchange(maps, NEAR))
+    maps = exchange(maps.reshape(32, 8, width), ("y_hi", "y_lo", "outer"))
     query_grad, key_grad, value_grad = pl.pallas_call(
         functools.partial(grads_kernel, key_scale),
         grid=(steps,),

time: 106 us -> 101 us (0.953)
  blocking collectives: 31.2 us -> 11.1 us
  starting transfers between devices: 33 us -> 42.3 us
  waiting for transfers between devices: 9.86 us -> 18.4 us
  Pallas kernels: 28.3 us -> 25.6 us
    all_to_all x2 -> x1, blocking collectives: 31.2 us -> 11.1 us  [exchange(): return lax.all_to_all(value, axes, 0, 0, tiled=True)]
    all_to_all x3 -> x4, waiting for transfers between devices: 4.38 us -> 16.9 us  [exchange(): return lax.all_to_all(value, axes, 0, 0, tiled=True)]
    all_to_all x3 -> x4, starting transfers between devices: 24.1 us -> 29.8 us  [exchange(): return lax.all_to_all(value, axes, 0, 0, tiled=True)]
    ppermute x2 -> x3, waiting for transfers between devices: 5.48 us -> 1.48 us  [the longest x1 0.88 us: per_device(): lax.ppermute(owned[1], 'core', swap)]
    ppermute x2 -> x3, starting transfers between devices: 8.87 us -> 12.5 us  [the longest x1 5.67 us: per_device(): lax.ppermute(send, 'core', swap)]
    pallas_call x1, Pallas kernels: 12.1 us -> 10.3 us  [per_device(): pl.pallas_call(functools.partial(inside_kernel, key_scale, map_scale), gr...]
    pallas_call x1, Pallas kernels: 2.88 us -> 1.65 us  [per_device(): pl.pallas_call(functools.partial(spread_kernel, key_scale, map_scale), in...]
  transfers between devices with their start and end apart: 5 -> 7, of which waited for: 2 -> 5; matrix products, arithmetic and copies ran while one was open for 0% -> 0% of each run, Pallas kernels for 19% -> 19%
where the time goes in v6:
time: 101 us; the launch traced here: 99.6 us
  starting transfers between devices  42.3 us (42%)
  Pallas kernels  25.6 us (25%)
  waiting for transfers between devices  18.4 us (18%)
  blocking collectives  11.1 us (11%)
  local copies, waits for them, and re-layouts  1.43 us (1%)
    all_to_all x4, starting transfers between devices, exchange(): return lax.all_to_all(value, axes, 0, 0, tiled=True)  29.8 us
    all_to_all x4, waiting for transfers between devices, exchange(): return lax.all_to_all(value, axes, 0, 0, tiled=True)  16.9 us
    all_to_all x1, blocking collectives, exchange(): return lax.all_to_all(value, axes, 0, 0, tiled=True)  11.1 us
    pallas_call x1, Pallas kernels, per_device(): pl.pallas_call(functools.partial(inside_kernel, key_scale, map_scale), gr...  10.3 us
    pallas_call x1, Pallas kernels, per_device(): pl.pallas_call(functools.partial(grads_kernel, key_scale), grid=(steps,),...  6.8 us
    ppermute x1, starting transfers between devices, per_device(): lax.ppermute(send, 'core', swap)  5.67 us
    pallas_call x1, Pallas kernels, per_device(): pl.pallas_call(products_kernel, grid=(steps,), in_specs=[wide, wide, wide...  3.69 us
    ppermute x1, starting transfers between devices, per_device(): lax.ppermute(owned[1], 'core', swap)  3.62 us
  transfers between devices with their start and end apart: 7, of which 5 were waited for; matrix products, arithmetic and copies ran while one was open for 0% of the time, Pallas kernels for 19%

profile of v6, /device:TPU:1, one launch (start us, length us, event | category | flops | bytes accessed | tf_op | source)
XLA Modules:
  0.0 99.6 jit_solution(1050037815187885848)
XLA Ops:
  0.6 3.7 %shard_map.103 = bf16[16,264,128]{2,1,0:T(8,128)(2,1)} custom-call(bf16[128,2048]{1,0:T(8,128)(2,1)} %bitcast.19, bf16[128,2048]{1,0:T(8,128)(2,1)} %bitcast.21, bf16[128,2048]{1,0:T(8,128)(2,1)} %bitcast.12, bf16[128,2048]{1,0:T(8,128)(2,1)} %bitcast.15, f32[16,128]{1,0:T(8,128)} %bitcast.23), custom_call_target="tpu_custom_call" | custom-call | flops 134217728 | bytes 3145728 | tf_op jit(solution)/shard_map/pallas_call | solution.py:275
  4.3 6.6 %all-to-all-start = ((bf16[8,2,264,128]{3,2,1,0:T(8,128)(2,1)}), bf16[8,2,264,128]{3,2,1,0:T(8,128)(2,1)S(1)}, u32[]{:S(2)}, u32[]{:S(2)}) async-start(bf16[8,2,264,128]{3,2,1,0:T(8,128)(2,1)} %bitcast.18), calls=%async_computation | async-start | bytes 2162688 | tf_op jit(solution)/shard_map/all_to_all | solution.py:256
  11.0 0.0 copy-start
  11.0 0.0 copy-start.1
  11.0 10.3 %shard_map.102 = (bf16[128,2048]{1,0:T(8,128)(2,1)}, bf16[128,2048]{1,0:T(8,128)(2,1)}, f32[128,2048]{1,0:T(8,128)}, f32[128,2048]{1,0:T(8,128)}, bf16[2,8,128,1...) custom-call(bf16[128,2048]{1,0:T(8,128)(2,1)} %bitcast.20, bf16[128,2048]{1,0:T(8,128)(2,1)} %bitcast.22, ...), custom_call_target="tpu_custom_call" | custom-call | flops 469762048 | bytes 8388608 | tf_op jit(solution)/shard_map/pallas_call | solution.py:288
  21.2 5.7 %collective-permute-start = (bf16[2,8,128,128]{3,2,1,0:T(8,128)(2,1)}, bf16[2,8,128,128]{3,2,1,0:T(8,128)(2,1)S(1)}, u32[]{:S(2)}, u32[]{:S(2)}) collective-permute-start(bf16[2,8,128,128]{3,2,1,0:T(8,128)(2,1)} %get-tuple-element.30), channel_id=1, source_target_pairs={{0,32},{32,0},{1,33},{33,1},{2,34},{34,2},{3,35},{35,3},{4,36},{36... | collective-permute-start | bytes 1572872 | tf_op jit(solution)/shard_map/ppermute | solution.py:305
  26.9 0.0 all-to-all-done.in_ref
  26.9 0.0 copy-done
  26.9 0.0 copy-done.1
  26.9 0.0 copy-start.2
  27.0 1.2 %shard_map.105 = bf16[4,2,144,128]{3,2,1,0:T(8,128)(2,1)} custom-call(bf16[8,2,264,128]{3,2,1,0:T(8,128)(2,1)S(1)} %all-to-all-done.in_ref, bf16[16,128,128]{2,1,0:T(8,128)(2,1)S(1)} %copy-done, bf16[16,128,128]{2,1,0:T(8,128)(2,1)S(1)} %copy-done.1), custom_call_target="tpu_custom_call" | custom-call | tf_op jit(solution)/shard_map/pallas_call | solution.py:306
  28.2 8.4 %all-to-all-start.1 = ((bf16[4,2,144,128]{3,2,1,0:T(8,128)(2,1)}), bf16[4,2,144,128]{3,2,1,0:T(8,128)(2,1)S(1)}, u32[]{:S(2)}, u32[]{:S(2)}) async-start(bf16[4,2,144,128]{3,2,1,0:T(8,128)(2,1)} %shard_map.105), calls=%async_computation.1 | async-start | bytes 589824 | tf_op jit(solution)/shard_map/all_to_all | solution.py:256
  36.6 0.0 collective-permute-done.got_ref
  36.6 0.0 copy-done.2
  36.6 0.1 shard_map.106
  36.8 0.0 copy-start.3
  36.8 0.7 copy-done.3
  37.5 0.0 copy-start.5
  37.5 0.7 copy-done.5
  38.2 0.5 shard_map.104.blocks_ref
  38.7 6.4 %all-to-all-done.1.totals_ref = bf16[4,2,144,128]{3,2,1,0:T(8,128)(2,1)S(1)} async-done(((bf16[4,2,144,128]{3,2,1,0:T(8,128)(2,1)}), bf16[4,2,144,128]{3,2,1,0:T(8,128)(2,1)S(1)}, u32[]{:S(2)}, u32[]{:S(2)}) %all-to-all-start.1) | async-done | bytes 294944 | tf_op jit(solution)/shard_map/all_to_all | solution.py:256
  45.1 1.7 %shard_map.107 = (bf16[8,512,128]{2,1,0:T(8,128)(2,1)}, bf16[2,8,32,128]{3,2,1,0:T(8,128)(2,1)S(1)}) custom-call(bf16[8,2,264,128]{3,2,1,0:T(8,128)(2,1)S(1)} %all-to-all-done.in_ref, bf16[8,2,256,128]{3,2,1,0:T(8,128)(2,1)S(1)} %shard_map.104.blocks_ref, bf16[4,2,144,128]{3,2,1,0:T(8,128)(2,1)S(1)} %all-to-all-done.1.totals_ref), custom_call_target="tpu_custom_call" | custom-call | tf_op jit(solution)/shard_map/pallas_call | solution.py:321
  46.8 0.0 copy-start.6
  46.8 0.0 copy-start.4
  46.8 6.9 %all-to-all-start.2 = ((bf16[8,512,128]{2,1,0:T(8,128)(2,1)}), bf16[8,512,128]{2,1,0:T(8,128)(2,1)S(1)}, u32[]{:S(2)}, u32[]{:S(2)}) async-start(bf16[8,512,128]{2,1,0:T(8,128)(2,1)} %get-tuple-element.33), calls=%async_computation.2 | async-start | bytes 2097152 | tf_op jit(solution)/shard_map/all_to_all | solution.py:256
  53.7 0.0 copy-done.6
  53.7 3.2 %collective-permute-start.1 = (bf16[8,128,128]{2,1,0:T(8,128)(2,1)S(1)}, bf16[8,128,128]{2,1,0:T(8,128)(2,1)S(1)}, u32[]{:S(2)}, u32[]{:S(2)}) collective-permute-start(bf16[8,128,128]{2,1,0:T(8,128)(2,1)S(1)} %copy-done.6), channel_id=1, source_target_pairs={{0,64},{64,0},{1,65},{65,1},{2,66},{66,2},{3,67},{67,3},{4,68},{68... | collective-permute-start | bytes 786440 | tf_op jit(solution)/shard_map/ppermute | solution.py:320
  56.9 3.6 %collective-permute-start.2 = (bf16[8,32,128]{2,1,0:T(8,128)(2,1)S(1)}, bf16[8,32,128]{2,1,0:T(8,128)(2,1)S(1)}, u32[]{:S(2)}, u32[]{:S(2)}) collective-permute-start(bf16[8,32,128]{2,1,0:T(8,128)(2,1)S(1)} %slice_bitcast_fusion), channel_id=1, source_target_pairs={{0,32},{32,0},{1,33},{33,1},{2,34},{34,2},{3,35},{35,3},{4,36},{36... | collective-permute-start | bytes 196616 | tf_op jit(solution)/shard_map/ppermute | solution.py:336
  60.5 0.9 collective-permute-done.2.carried_got_ref
  61.4 0.6 collective-permute-done.1.inside_got_ref
  62.0 0.0 copy-done.4
  62.0 0.1 shard_map.108
  62.1 6.0 %all-to-all-done.2.in_ref = bf16[8,512,128]{2,1,0:T(8,128)(2,1)S(1)} async-done(((bf16[8,512,128]{2,1,0:T(8,128)(2,1)}), bf16[8,512,128]{2,1,0:T(8,128)(2,1)S(1)}, u32[]{:S(2)}, u32[]{:S(2)}) %all-to-all-start.2) | async-done | bytes 1048608 | tf_op jit(solution)/shard_map/all_to_all | solution.py:256
  68.1 0.0 copy-start.7
  68.1 11.1 %all_to_all.25.in_ref = bf16[8,160,128]{2,1,0:T(8,128)(2,1)S(1)} all-to-all(bf16[8,160,128]{2,1,0:T(8,128)(2,1)S(1)} %shard_map.108), channel_id=1, replica_groups=mesh['y_hi'=4,'y_lo'=2,'core'=2,'outer'=4,'inner'=2,'x'=4] {'inner','x'}, dimensions={0} | all-to-all | bytes 655360 | tf_op jit(solution)/shard_map/all_to_all | solution.py:256
  79.2 0.7 shard_map.110
  79.9 7.8 %all-to-all-start.4 = ((bf16[32,8,128]{2,1,0:T(8,128)(2,1)}), bf16[32,8,128]{2,1,0:T(8,128)(2,1)S(1)}, u32[]{:S(2)}, u32[]{:S(2)}) async-start(bf16[32,8,128]{2,1,0:T(8,128)(2,1)} %bitcast.10), calls=%async_computation.4 | async-start | bytes 131072 | tf_op jit(solution)/shard_map/all_to_all | solution.py:256
  87.6 0.0 copy-done.7
  87.7 6.8 %shard_map.109 = (bf16[128,2048]{1,0:T(8,128)(2,1)}, bf16[128,2048]{1,0:T(8,128)(2,1)}, bf16[128,2048]{1,0:T(8,128)(2,1)}) custom-call(bf16[128,2048]{1,0:T(8,128)(2,1)} %bitcast.14, bf16[128,2048]{1,0:T(8,128)(2,1)} %bitcast.17, bf16[128,2048]{1,0:T(8,128)(2,1)} %get-tuple-element.23.fq_ref, bf16[128,2048]{1,0:T(8,128)(2,1)} %get-tuple-element.24.fk_ref, ...), custom_call_target="tpu_custom_call" | custom-call | flops 469762048 | bytes 8388608 | tf_op jit(solution)/shard_map/pallas_call | solution.py:345
  94.5 4.5 %all-to-all-done.4.in_ref = bf16[32,8,128]{2,1,0:T(8,128)(2,1)S(1)} async-done(((bf16[32,8,128]{2,1,0:T(8,128)(2,1)}), bf16[32,8,128]{2,1,0:T(8,128)(2,1)S(1)}, u32[]{:S(2)}, u32[]{:S(2)}) %all-to-all-start.4) | async-done | bytes 65568 | tf_op jit(solution)/shard_map/all_to_all | solution.py:256
  98.9 0.6 shard_map.111
  (1 shorter events, 0.0 us)
Async XLA Ops:
  4.3 22.6 %all-to-all-start = ((bf16[8,2,264,128]{3,2,1,0:T(8,128)(2,1)}), bf16[8,2,264,128]{3,2,1,0:T(8,128)(2,1)S(1)}, u32[]{:S(2)}, u32[]{:S(2)}) async-start(bf16[8,2,264,128]{3,2,1,0:T(8,128)(2,1)} %bitcast.18), calls=%async_computation | async-start | bytes 2162688 | tf_op jit(solution)/shard_map/all_to_all | solution.py:256
  11.0 16.0 %copy-start = (bf16[16,128,128]{2,1,0:T(8,128)(2,1)S(1)}, bf16[16,128,128]{2,1,0:T(8,128)(2,1)}, u32[]{:S(2)}) copy-start(bf16[16,128,128]{2,1,0:T(8,128)(2,1)} %mq_ref.7) | copy-start | bytes 1572868
  11.0 16.0 %copy-start.1 = (bf16[16,128,128]{2,1,0:T(8,128)(2,1)S(1)}, bf16[16,128,128]{2,1,0:T(8,128)(2,1)}, u32[]{:S(2)}) copy-start(bf16[16,128,128]{2,1,0:T(8,128)(2,1)} %mk_ref.7) | copy-start | bytes 1572868
  21.2 15.4 %collective-permute-start = (bf16[2,8,128,128]{3,2,1,0:T(8,128)(2,1)}, bf16[2,8,128,128]{3,2,1,0:T(8,128)(2,1)S(1)}, u32[]{:S(2)}, u32[]{:S(2)}) collective-permute-start(bf16[2,8,128,128]{3,2,1,0:T(8,128)(2,1)} %get-tuple-element.30), channel_id=1, source_target_pairs={{0,32},{32,0},{1,33},{33,1},{2,34},{34,2},{3,35},{35,3},{4,36},{36... | collective-permute-start | bytes 1572872 | tf_op jit(solution)/shard_map/ppermute | solution.py:305
  26.9 9.7 %copy-start.2 = (bf16[2,8,128,128]{3,2,1,0:T(8,128)(2,1)S(1)}, bf16[2,8,128,128]{3,2,1,0:T(8,128)(2,1)}, u32[]{:S(2)}) copy-start(bf16[2,8,128,128]{3,2,1,0:T(8,128)(2,1)} %get-tuple-element.29.kept_ref) | copy-start | bytes 1572868
  28.2 16.9 %all-to-all-start.1 = ((bf16[4,2,144,128]{3,2,1,0:T(8,128)(2,1)}), bf16[4,2,144,128]{3,2,1,0:T(8,128)(2,1)S(1)}, u32[]{:S(2)}, u32[]{:S(2)}) async-start(bf16[4,2,144,128]{3,2,1,0:T(8,128)(2,1)} %shard_map.105), calls=%async_computation.1 | async-start | bytes 589824 | tf_op jit(solution)/shard_map/all_to_all | solution.py:256
  36.8 0.7 copy-start.3
  37.5 0.7 copy-start.5
  46.8 6.9 %copy-start.6 = (bf16[8,128,128]{2,1,0:T(8,128)(2,1)S(1)}, bf16[8,128,128]{2,1,0:T(8,128)(2,1)}, u32[]{:S(2)}) copy-start(bf16[8,128,128]{2,1,0:T(8,128)(2,1)} %copy-done.5) | copy-start | bytes 786436
  46.8 15.2 %copy-start.4 = (bf16[8,128,128]{2,1,0:T(8,128)(2,1)S(1)}, bf16[8,128,128]{2,1,0:T(8,128)(2,1)}, u32[]{:S(2)}) copy-start(bf16[8,128,128]{2,1,0:T(8,128)(2,1)} %copy-done.3) | copy-start | bytes 786436
  46.8 21.3 %all-to-all-start.2 = ((bf16[8,512,128]{2,1,0:T(8,128)(2,1)}), bf16[8,512,128]{2,1,0:T(8,128)(2,1)S(1)}, u32[]{:S(2)}, u32[]{:S(2)}) async-start(bf16[8,512,128]{2,1,0:T(8,128)(2,1)} %get-tuple-element.33), calls=%async_computation.2 | async-start | bytes 2097152 | tf_op jit(solution)/shard_map/all_to_all | solution.py:256
  53.7 8.3 %collective-permute-start.1 = (bf16[8,128,128]{2,1,0:T(8,128)(2,1)S(1)}, bf16[8,128,128]{2,1,0:T(8,128)(2,1)S(1)}, u32[]{:S(2)}, u32[]{:S(2)}) collective-permute-start(bf16[8,128,128]{2,1,0:T(8,128)(2,1)S(1)} %copy-done.6), channel_id=1, source_target_pairs={{0,64},{64,0},{1,65},{65,1},{2,66},{66,2},{3,67},{67,3},{4,68},{68... | collective-permute-start | bytes 786440 | tf_op jit(solution)/shard_map/ppermute | solution.py:320
  56.9 4.5 %collective-permute-start.2 = (bf16[8,32,128]{2,1,0:T(8,128)(2,1)S(1)}, bf16[8,32,128]{2,1,0:T(8,128)(2,1)S(1)}, u32[]{:S(2)}, u32[]{:S(2)}) collective-permute-start(bf16[8,32,128]{2,1,0:T(8,128)(2,1)S(1)} %slice_bitcast_fusion), channel_id=1, source_target_pairs={{0,32},{32,0},{1,33},{33,1},{2,34},{34,2},{3,35},{35,3},{4,36},{36... | collective-permute-start | bytes 196616 | tf_op jit(solution)/shard_map/ppermute | solution.py:336
  68.1 19.6 %copy-start.7 = (bf16[8,512,128]{2,1,0:T(8,128)(2,1)}, bf16[8,512,128]{2,1,0:T(8,128)(2,1)S(1)}, u32[]{:S(2)}) copy-start(bf16[8,512,128]{2,1,0:T(8,128)(2,1)S(1)} %all-to-all-done.2.in_ref) | copy-start | bytes 3145732
  79.9 19.1 %all-to-all-start.4 = ((bf16[32,8,128]{2,1,0:T(8,128)(2,1)}), bf16[32,8,128]{2,1,0:T(8,128)(2,1)S(1)}, u32[]{:S(2)}, u32[]{:S(2)}) async-start(bf16[32,8,128]{2,1,0:T(8,128)(2,1)} %bitcast.10), calls=%async_computation.4 | async-start | bytes 131072 | tf_op jit(solution)/shard_map/all_to_all | solution.py:256

commit v7 on v6

--- a/solution.py
+++ b/solution.py
@@ -316,8 +316,8 @@
         cost_estimate=pl.CostEstimate(flops=2 * flops, bytes_accessed=2 << 20, transcendentals=0),
         compiler_params=VMEM,
     )(received, query_map, key_map)
-    totals, send = lax.optimization_barrier((exchange(totals, "outer"), send))
     inside_got = lax.ppermute(send, "y_lo", swap)
+    totals, inside_got = lax.optimization_barrier((exchange(totals, "outer"), inside_got))
     states, owned = pl.pallas_call(
         functools.partial(spread_kernel, key_scale, map_scale),
         in_specs=[whole] * 3,
@@ -335,13 +335,6 @@
         compiler_params=VMEM,
     )(keep, inside_got, owned, lax.ppermute(owned[1], "core", swap))
     carried, maps = lax.optimization_barrier((carried, maps))
-    maps = pl.pallas_call(
-        gather_kernel,
-        in_specs=[whole],
-        out_shape=jax.ShapeDtypeStruct((2, 2, 2, 32, width), BF16),
-        compiler_params=VMEM,
-    )(exchange(maps, NEAR))
-    maps = exchange(maps.reshape(32, 8, width), ("y_hi", "y_lo", "outer"))
     query_grad, key_grad, value_grad = pl.pallas_call(
         functools.partial(grads_kernel, key_scale),
         grid=(steps,),
@@ -351,6 +344,14 @@
         out_shape=[wide_shape] * 3,
         cost_estimate=pl.CostEstimate(flops=7 * flops, bytes_accessed=8 << 20, transcendentals=0),
     )(v, g, fq, fk, gates, query_map, key_map, query_inside, key_inside, carried)
+    maps, query_grad = lax.optimization_barrier((exchange(maps, NEAR), query_grad))
+    maps = pl.pallas_call(
+        gather_kernel,
+        in_specs=[whole],
+        out_shape=jax.ShapeDtypeStruct((2, 2, 2, 32, width), BF16),
+        compiler_params=VMEM,
+    )(maps)
+    maps = exchange(maps.reshape(32, 8, width), ("y_hi", "y_lo", "outer"))
     map_grads = add_up(maps, F32)
     shape = queries.shape
     return query_grad.reshape(shape), key_grad.reshape(shape), value_grad.reshape(shape), map_grads

time: 101 us -> 103 us (1.020)
  blocking collectives: 11.1 us -> 21.3 us
  starting transfers between devices: 42.3 us -> 37.4 us
  waiting for transfers between devices: 18.4 us -> 15.2 us
    all_to_all x1, blocking collectives: 11.1 us -> 21.3 us  [exchange(): return lax.all_to_all(value, axes, 0, 0, tiled=True)]
    all_to_all x4, waiting for transfers between devices: 16.9 us -> 9.35 us  [exchange(): return lax.all_to_all(value, axes, 0, 0, tiled=True)]
    all_to_all x4, starting transfers between devices: 29.8 us -> 25.1 us  [exchange(): return lax.all_to_all(value, axes, 0, 0, tiled=True)]
    ppermute x1, waiting for transfers between devices: 0.59 us -> 4.97 us  [per_device(): inside_got = lax.ppermute(send, 'y_lo', swap)]
  transfers between devices with their start and end apart: 7 -> 7, of which waited for: 5 -> 3; matrix products, arithmetic and copies ran while one was open for 0% -> 0% of each run, Pallas kernels for 19% -> 19%
where the time goes in v7:
time: 103 us; the launch traced here: 101 us
  starting transfers between devices  37.4 us (36%)
  Pallas kernels  25.7 us (25%)
  blocking collectives  21.3 us (21%)
  waiting for transfers between devices  15.2 us (15%)
    all_to_all x4, starting transfers between devices, exchange(): return lax.all_to_all(value, axes, 0, 0, tiled=True)  25.1 us
    all_to_all x1, blocking collectives, exchange(): return lax.all_to_all(value, axes, 0, 0, tiled=True)  21.3 us
    pallas_call x1, Pallas kernels, per_device(): pl.pallas_call(functools.partial(inside_kernel, key_scale, map_scale), gr...  10.3 us
    all_to_all x4, waiting for transfers between devices, exchange(): return lax.all_to_all(value, axes, 0, 0, tiled=True)  9.35 us
    pallas_call x1, Pallas kernels, per_device(): pl.pallas_call(functools.partial(grads_kernel, key_scale), grid=(steps,),...  6.81 us
    ppermute x1, starting transfers between devices, per_device(): lax.ppermute(send, 'core', swap)  5.67 us
    ppermute x1, waiting for transfers between devices, per_device(): inside_got = lax.ppermute(send, 'y_lo', swap)  4.97 us
    pallas_call x1, Pallas kernels, per_device(): pl.pallas_call(products_kernel, grid=(steps,), in_specs=[wide, wide, wide...  3.69 us
  transfers between devices with their start and end apart: 7, of which 3 were waited for; matrix products, arithmetic and copies ran while one was open for 0% of the time, Pallas kernels for 19%

profile of v7, /device:TPU:1, one launch (start us, length us, event | category | flops | bytes accessed | tf_op | source)
XLA Modules:
  0.0 101.1 jit_solution(274880283778171427)
XLA Ops:
  0.6 3.7 %shard_map.102 = bf16[16,264,128]{2,1,0:T(8,128)(2,1)} custom-call(bf16[128,2048]{1,0:T(8,128)(2,1)} %bitcast.20, bf16[128,2048]{1,0:T(8,128)(2,1)} %bitcast.22, bf16[128,2048]{1,0:T(8,128)(2,1)} %bitcast.13, bf16[128,2048]{1,0:T(8,128)(2,1)} %bitcast.16, f32[16,128]{1,0:T(8,128)} %bitcast.24), custom_call_target="tpu_custom_call" | custom-call | flops 134217728 | bytes 3145728 | tf_op jit(solution)/shard_map/pallas_call | solution.py:275
  4.3 6.6 %all-to-all-start = ((bf16[8,2,264,128]{3,2,1,0:T(8,128)(2,1)}), bf16[8,2,264,128]{3,2,1,0:T(8,128)(2,1)S(1)}, u32[]{:S(2)}, u32[]{:S(2)}) async-start(bf16[8,2,264,128]{3,2,1,0:T(8,128)(2,1)} %bitcast.19), calls=%async_computation | async-start | bytes 2162688 | tf_op jit(solution)/shard_map/all_to_all | solution.py:256
  11.0 0.0 copy-start
  11.0 0.0 copy-start.1
  11.0 10.3 %shard_map.103 = (bf16[128,2048]{1,0:T(8,128)(2,1)}, bf16[128,2048]{1,0:T(8,128)(2,1)}, f32[128,2048]{1,0:T(8,128)}, f32[128,2048]{1,0:T(8,128)}, bf16[2,8,128,1...) custom-call(bf16[128,2048]{1,0:T(8,128)(2,1)} %bitcast.21, bf16[128,2048]{1,0:T(8,128)(2,1)} %bitcast.23, ...), custom_call_target="tpu_custom_call" | custom-call | flops 469762048 | bytes 8388608 | tf_op jit(solution)/shard_map/pallas_call | solution.py:288
  21.2 5.7 %collective-permute-start = (bf16[2,8,128,128]{3,2,1,0:T(8,128)(2,1)}, bf16[2,8,128,128]{3,2,1,0:T(8,128)(2,1)S(1)}, u32[]{:S(2)}, u32[]{:S(2)}) collective-permute-start(bf16[2,8,128,128]{3,2,1,0:T(8,128)(2,1)} %get-tuple-element.28), channel_id=1, source_target_pairs={{0,32},{32,0},{1,33},{33,1},{2,34},{34,2},{3,35},{35,3},{4,36},{36... | collective-permute-start | bytes 1572872 | tf_op jit(solution)/shard_map/ppermute | solution.py:305
  26.9 0.0 all-to-all-done.in_ref
  26.9 0.0 copy-done
  26.9 0.0 copy-done.1
  26.9 0.0 copy-start.2
  27.0 1.2 %shard_map.105 = bf16[4,2,144,128]{3,2,1,0:T(8,128)(2,1)} custom-call(bf16[8,2,264,128]{3,2,1,0:T(8,128)(2,1)S(1)} %all-to-all-done.in_ref, bf16[16,128,128]{2,1,0:T(8,128)(2,1)S(1)} %copy-done, bf16[16,128,128]{2,1,0:T(8,128)(2,1)S(1)} %copy-done.1), custom_call_target="tpu_custom_call" | custom-call | tf_op jit(solution)/shard_map/pallas_call | solution.py:306
  28.2 8.4 %all-to-all-start.1 = ((bf16[4,2,144,128]{3,2,1,0:T(8,128)(2,1)}), bf16[4,2,144,128]{3,2,1,0:T(8,128)(2,1)S(1)}, u32[]{:S(2)}, u32[]{:S(2)}) async-start(bf16[4,2,144,128]{3,2,1,0:T(8,128)(2,1)} %shard_map.105), calls=%async_computation.1 | async-start | bytes 589824 | tf_op jit(solution)/shard_map/all_to_all | solution.py:256
  36.6 0.0 collective-permute-done.got_ref
  36.6 0.0 copy-done.2
  36.6 0.1 shard_map.106
  36.8 0.0 copy-start.3
  36.8 3.2 %collective-permute-start.1 = (bf16[8,128,128]{2,1,0:T(8,128)(2,1)S(1)}, bf16[8,128,128]{2,1,0:T(8,128)(2,1)S(1)}, u32[]{:S(2)}, u32[]{:S(2)}) collective-permute-start(bf16[8,128,128]{2,1,0:T(8,128)(2,1)S(1)} %get-tuple-element.29), channel_id=1, source_target_pairs={{0,64},{64,0},{1,65},{65,1},{2,66},{66,2},{3,67},{67,3},{4,68},{68... | collective-permute-start | bytes 786440 | tf_op jit(solution)/shard_map/ppermute | solution.py:319
  40.0 0.5 shard_map.104.blocks_ref
  40.5 0.0 copy-done.3
  40.5 5.0 %collective-permute-done.1.inside_got_ref = bf16[8,128,128]{2,1,0:T(8,128)(2,1)S(1)} collective-permute-done((bf16[8,128,128]{2,1,0:T(8,128)(2,1)S(1)}, bf16[8,128,128]{2,1,0:T(8,128)(2,1)S(1)}, u32[]{:S(2)}, u32[]{:S(2)}) %collective-permute-start.1) | collective-permute-done | bytes 262176 | tf_op jit(solution)/shard_map/ppermute | solution.py:319
  45.5 0.0 copy-start.5
  45.5 0.7 copy-done.5
  46.2 0.0 all-to-all-done.1.totals_ref
  46.2 1.7 %shard_map.107 = (bf16[8,512,128]{2,1,0:T(8,128)(2,1)}, bf16[2,8,32,128]{3,2,1,0:T(8,128)(2,1)S(1)}) custom-call(bf16[8,2,264,128]{3,2,1,0:T(8,128)(2,1)S(1)} %all-to-all-done.in_ref, bf16[8,2,256,128]{3,2,1,0:T(8,128)(2,1)S(1)} %shard_map.104.blocks_ref, bf16[4,2,144,128]{3,2,1,0:T(8,128)(2,1)S(1)} %all-to-all-done.1.totals_ref), custom_call_target="tpu_custom_call" | custom-call | tf_op jit(solution)/shard_map/pallas_call | solution.py:321
  47.8 0.0 copy-start.4
  47.9 0.0 copy-start.6
  47.9 5.8 %all-to-all-start.2 = ((bf16[8,512,128]{2,1,0:T(8,128)(2,1)}), bf16[8,512,128]{2,1,0:T(8,128)(2,1)S(1)}, u32[]{:S(2)}, u32[]{:S(2)}) async-start(bf16[8,512,128]{2,1,0:T(8,128)(2,1)} %get-tuple-element.31), calls=%async_computation.2 | async-start | bytes 2097152 | tf_op jit(solution)/shard_map/all_to_all | solution.py:256
  53.7 3.3 %collective-permute-start.2 = (bf16[8,32,128]{2,1,0:T(8,128)(2,1)S(1)}, bf16[8,32,128]{2,1,0:T(8,128)(2,1)S(1)}, u32[]{:S(2)}, u32[]{:S(2)}) collective-permute-start(bf16[8,32,128]{2,1,0:T(8,128)(2,1)S(1)} %slice_bitcast_fusion), channel_id=1, source_target_pairs={{0,32},{32,0},{1,33},{33,1},{2,34},{34,2},{3,35},{35,3},{4,36},{36... | collective-permute-start | bytes 196616 | tf_op jit(solution)/shard_map/ppermute | solution.py:336
  57.0 0.9 collective-permute-done.2.carried_got_ref
  57.9 0.0 copy-done.4
  57.9 0.0 copy-done.6
  57.9 0.8 shard_map.108
  58.7 9.3 %all-to-all-done.2.in_ref = bf16[8,512,128]{2,1,0:T(8,128)(2,1)S(1)} async-done(((bf16[8,512,128]{2,1,0:T(8,128)(2,1)}), bf16[8,512,128]{2,1,0:T(8,128)(2,1)S(1)}, u32[]{:S(2)}, u32[]{:S(2)}) %all-to-all-start.2) | async-done | bytes 1048608 | tf_op jit(solution)/shard_map/all_to_all | solution.py:256
  68.1 0.0 copy-start.7
  68.1 4.2 %all-to-all-start.3 = ((bf16[8,160,128]{2,1,0:T(8,128)(2,1)}), bf16[8,160,128]{2,1,0:T(8,128)(2,1)S(1)}, u32[]{:S(2)}, u32[]{:S(2)}) async-start(bf16[8,160,128]{2,1,0:T(8,128)(2,1)} %shard_map.108), calls=%async_computation.3 | async-start | bytes 655360 | tf_op jit(solution)/shard_map/all_to_all | solution.py:256
  72.3 0.0 copy-done.7
  72.3 6.8 %shard_map.109 = (bf16[128,2048]{1,0:T(8,128)(2,1)}, bf16[128,2048]{1,0:T(8,128)(2,1)}, bf16[128,2048]{1,0:T(8,128)(2,1)}) custom-call(bf16[128,2048]{1,0:T(8,128)(2,1)} %bitcast.15, bf16[128,2048]{1,0:T(8,128)(2,1)} %bitcast.18, bf16[128,2048]{1,0:T(8,128)(2,1)} %get-tuple-element.36.fq_ref, bf16[128,2048]{1,0:T(8,128)(2,1)} %get-tuple-element.37.fk_ref, ...), custom_call_target="tpu_custom_call" | custom-call | flops 469762048 | bytes 8388608 | tf_op jit(solution)/shard_map/pallas_call | solution.py:338
  79.1 0.0 all-to-all-done.3.in_ref
  79.2 21.3 %all_to_all.25.in_ref = bf16[32,8,128]{2,1,0:T(8,128)(2,1)S(1)} all-to-all(bf16[32,8,128]{2,1,0:T(8,128)(2,1)S(1)} %bitcast.12), channel_id=1, replica_groups=mesh['y_hi'=4,'y_lo'=2,'core'=2,'outer'=4,'inner'=2,'x'=4] {'y_hi','y_lo..., dimensions={0} | all-to-all | bytes 131072 | tf_op jit(solution)/shard_map/all_to_all | solution.py:256
  100.5 0.6 shard_map.111
  (2 shorter events, 0.1 us)
Async XLA Ops:
  4.3 22.6 %all-to-all-start = ((bf16[8,2,264,128]{3,2,1,0:T(8,128)(2,1)}), bf16[8,2,264,128]{3,2,1,0:T(8,128)(2,1)S(1)}, u32[]{:S(2)}, u32[]{:S(2)}) async-start(bf16[8,2,264,128]{3,2,1,0:T(8,128)(2,1)} %bitcast.19), calls=%async_computation | async-start | bytes 2162688 | tf_op jit(solution)/shard_map/all_to_all | solution.py:256
  11.0 16.0 %copy-start = (bf16[16,128,128]{2,1,0:T(8,128)(2,1)S(1)}, bf16[16,128,128]{2,1,0:T(8,128)(2,1)}, u32[]{:S(2)}) copy-start(bf16[16,128,128]{2,1,0:T(8,128)(2,1)} %mq_ref.7) | copy-start | bytes 1572868
  11.0 16.0 %copy-start.1 = (bf16[16,128,128]{2,1,0:T(8,128)(2,1)S(1)}, bf16[16,128,128]{2,1,0:T(8,128)(2,1)}, u32[]{:S(2)}) copy-start(bf16[16,128,128]{2,1,0:T(8,128)(2,1)} %mk_ref.7) | copy-start | bytes 1572868
  21.2 15.4 %collective-permute-start = (bf16[2,8,128,128]{3,2,1,0:T(8,128)(2,1)}, bf16[2,8,128,128]{3,2,1,0:T(8,128)(2,1)S(1)}, u32[]{:S(2)}, u32[]{:S(2)}) collective-permute-start(bf16[2,8,128,128]{3,2,1,0:T(8,128)(2,1)} %get-tuple-element.28), channel_id=1, source_target_pairs={{0,32},{32,0},{1,33},{33,1},{2,34},{34,2},{3,35},{35,3},{4,36},{36... | collective-permute-start | bytes 1572872 | tf_op jit(solution)/shard_map/ppermute | solution.py:305
  26.9 9.7 %copy-start.2 = (bf16[2,8,128,128]{3,2,1,0:T(8,128)(2,1)S(1)}, bf16[2,8,128,128]{3,2,1,0:T(8,128)(2,1)}, u32[]{:S(2)}) copy-start(bf16[2,8,128,128]{3,2,1,0:T(8,128)(2,1)} %get-tuple-element.27.kept_ref) | copy-start | bytes 1572868
  28.2 18.0 %all-to-all-start.1 = ((bf16[4,2,144,128]{3,2,1,0:T(8,128)(2,1)}), bf16[4,2,144,128]{3,2,1,0:T(8,128)(2,1)S(1)}, u32[]{:S(2)}, u32[]{:S(2)}) async-start(bf16[4,2,144,128]{3,2,1,0:T(8,128)(2,1)} %shard_map.105), calls=%async_computation.1 | async-start | bytes 589824 | tf_op jit(solution)/shard_map/all_to_all | solution.py:256
  36.8 3.7 %copy-start.3 = (bf16[8,128,128]{2,1,0:T(8,128)(2,1)}, bf16[8,128,128]{2,1,0:T(8,128)(2,1)S(1)}, u32[]{:S(2)}) copy-start(bf16[8,128,128]{2,1,0:T(8,128)(2,1)S(1)} %get-tuple-element.32.inside_ref) | copy-start | bytes 786436
  36.8 8.7 %collective-permute-start.1 = (bf16[8,128,128]{2,1,0:T(8,128)(2,1)S(1)}, bf16[8,128,128]{2,1,0:T(8,128)(2,1)S(1)}, u32[]{:S(2)}, u32[]{:S(2)}) collective-permute-start(bf16[8,128,128]{2,1,0:T(8,128)(2,1)S(1)} %get-tuple-element.29), channel_id=1, source_target_pairs={{0,64},{64,0},{1,65},{65,1},{2,66},{66,2},{3,67},{67,3},{4,68},{68... | collective-permute-start | bytes 786440 | tf_op jit(solution)/shard_map/ppermute | solution.py:319
  45.5 0.7 copy-start.5
  47.8 10.1 %copy-start.4 = (bf16[8,128,128]{2,1,0:T(8,128)(2,1)S(1)}, bf16[8,128,128]{2,1,0:T(8,128)(2,1)}, u32[]{:S(2)}) copy-start(bf16[8,128,128]{2,1,0:T(8,128)(2,1)} %copy-done.3) | copy-start | bytes 786436
  47.9 10.1 %copy-start.6 = (bf16[8,128,128]{2,1,0:T(8,128)(2,1)S(1)}, bf16[8,128,128]{2,1,0:T(8,128)(2,1)}, u32[]{:S(2)}) copy-start(bf16[8,128,128]{2,1,0:T(8,128)(2,1)} %copy-done.5) | copy-start | bytes 786436
  47.9 20.2 %all-to-all-start.2 = ((bf16[8,512,128]{2,1,0:T(8,128)(2,1)}), bf16[8,512,128]{2,1,0:T(8,128)(2,1)S(1)}, u32[]{:S(2)}, u32[]{:S(2)}) async-start(bf16[8,512,128]{2,1,0:T(8,128)(2,1)} %get-tuple-element.31), calls=%async_computation.2 | async-start | bytes 2097152 | tf_op jit(solution)/shard_map/all_to_all | solution.py:256
  53.7 4.2 %collective-permute-start.2 = (bf16[8,32,128]{2,1,0:T(8,128)(2,1)S(1)}, bf16[8,32,128]{2,1,0:T(8,128)(2,1)S(1)}, u32[]{:S(2)}, u32[]{:S(2)}) collective-permute-start(bf16[8,32,128]{2,1,0:T(8,128)(2,1)S(1)} %slice_bitcast_fusion), channel_id=1, source_target_pairs={{0,32},{32,0},{1,33},{33,1},{2,34},{34,2},{3,35},{35,3},{4,36},{36... | collective-permute-start | bytes 196616 | tf_op jit(solution)/shard_map/ppermute | solution.py:336
  68.1 4.2 %copy-start.7 = (bf16[8,512,128]{2,1,0:T(8,128)(2,1)}, bf16[8,512,128]{2,1,0:T(8,128)(2,1)S(1)}, u32[]{:S(2)}) copy-start(bf16[8,512,128]{2,1,0:T(8,128)(2,1)S(1)} %all-to-all-done.2.in_ref) | copy-start | bytes 3145732
  68.1 11.0 %all-to-all-start.3 = ((bf16[8,160,128]{2,1,0:T(8,128)(2,1)}), bf16[8,160,128]{2,1,0:T(8,128)(2,1)S(1)}, u32[]{:S(2)}, u32[]{:S(2)}) async-start(bf16[8,160,128]{2,1,0:T(8,128)(2,1)} %shard_map.108), calls=%async_computation.3 | async-start | bytes 655360 | tf_op jit(solution)/shard_map/all_to_all | solution.py:256

commit v8 on v7

--- a/solution.py
+++ b/solution.py
@@ -71,6 +71,7 @@
     fq_ref, fk_ref, qb_ref, kb_ref, keep_ref, send_ref, maps_ref, sems,
 ):
     heads, width = mq_ref.shape[0], mq_ref.shape[1]
+    step = pl.program_id(0)
     causal = causal_mask(q_ref.shape[0])
     columns = running_columns(gates_ref[...])
     rows = running_rows(gates_ref[...])
@@ -90,20 +91,22 @@
         kb_ref[:, lanes] = key_back
         for m, (x, back) in enumerate(((q, query_back), (k, key_back))):
             part = dot(x, back.astype(BF16), (0, 0)) * map_scale
-            at = ((m * 2 + owner // 4) * 2 + owner % 2) * 16
             for b in range(width // 8):
-                to = at + (b // 8) * 8
-                maps_ref[bit, (owner // 2) % 2, b % 8, to : to + 8] = part[8 * b : 8 * b + 8].astype(BF16)
-    core, y_lo = lax.axis_index("core"), lax.axis_index("y_lo")
-    copies = []
-    for side in range(2):
-        along = lax.bitwise_xor(y_lo, side)
-        copies.append(pltpu.make_async_copy(maps_ref.at[core, along], keep_ref.at[side], sems.at[2 * side]))
-        copies.append(pltpu.make_async_copy(maps_ref.at[1 - core, along], send_ref.at[side], sems.at[2 * side + 1]))
-    for copy in copies:
-        copy.start()
-    for copy in copies:
-        copy.wait()
+                to = (owner % 2) * 16 + (b // 8) * 8
+                maps_ref[bit, (owner // 2) % 2, b % 8, m, step, to : to + 8] = part[8 * b : 8 * b + 8].astype(BF16)
+
+    @pl.when(step == pl.num_programs(0) - 1)
+    def _():
+        core, y_lo = lax.axis_index("core"), lax.axis_index("y_lo")
+        copies = []
+        for side in range(2):
+            along = lax.bitwise_xor(y_lo, side)
+            for to, (ref, of) in enumerate(((keep_ref, core), (send_ref, 1 - core))):
+                copies.append(pltpu.make_async_copy(maps_ref.at[of, along], ref.at[side], sems.at[2 * side + to]))
+        for copy in copies:
+            copy.start()
+        for copy in copies:
+            copy.wait()
 
 
 def over(decay, value):
@@ -282,27 +285,22 @@
     )(q, k, v, g, gates)
     received = exchange(sent.reshape(near, share, 2 * width + PAD, width), NEAR)
     rows, quarter = 2 * share * width, heads * 8
-    full = pl.BlockSpec((length, heads * width), lambda i: (0, 0))
-    half_shape = jax.ShapeDtypeStruct((2, near, quarter, width), BF16)
+    half_shape = jax.ShapeDtypeStruct((2, near, 2, steps, 32, width), BF16)
     anywhere = pl.BlockSpec(memory_space=pl.ANY)
     fq, fk, query_inside, key_inside, keep, send = pl.pallas_call(
         functools.partial(inside_kernel, key_scale, map_scale),
-        grid=(1,),
-        in_specs=[full] * 4
-        + [pl.BlockSpec((heads, length), lambda i: (0, 0))]
-        + [pl.BlockSpec((heads, width, width), lambda i: (0, 0, 0))] * 2,
-        out_specs=[full] * 4 + [anywhere] * 2,
+        grid=(steps,),
+        in_specs=[wide] * 4 + [gate_spec, map_spec, map_spec],
+        out_specs=[wide] * 4 + [anywhere] * 2,
         out_shape=[wide_shape] * 2 + [sum_shape] * 2 + [half_shape] * 2,
-        scratch_shapes=[pltpu.VMEM((2, 2, near, quarter, width), BF16), pltpu.SemaphoreType.DMA((4,))],
+        scratch_shapes=[pltpu.VMEM((2, 2, near, 2, steps, 32, width), BF16), pltpu.SemaphoreType.DMA((4,))],
         cost_estimate=pl.CostEstimate(flops=7 * flops, bytes_accessed=8 << 20, transcendentals=1 << 18),
     )(q, k, v, g, gates, query_map, key_map)
+    keep, send = (x.reshape(2, near, quarter, width) for x in (keep, send))
     received, keep = lax.optimization_barrier((received, keep))
     swap = [(0, 1), (1, 0)]
     whole = pl.BlockSpec(memory_space=pltpu.VMEM)
     part = jax.ShapeDtypeStruct((near, quarter, width), BF16)
-    keep, send = pl.pallas_call(
-        halve_kernel, in_specs=[whole] * 2, out_shape=[part] * 2, compiler_params=VMEM
-    )(keep, lax.ppermute(send, "core", swap))
     totals = pl.pallas_call(
         functools.partial(totals_kernel, key_scale),
         in_specs=[whole] * 3,
@@ -316,8 +314,13 @@
         cost_estimate=pl.CostEstimate(flops=2 * flops, bytes_accessed=2 << 20, transcendentals=0),
         compiler_params=VMEM,
     )(received, query_map, key_map)
+    got = lax.ppermute(send, "core", swap)
+    keep, send = pl.pallas_call(
+        halve_kernel, in_specs=[whole] * 2, out_shape=[part] * 2, compiler_params=VMEM
+    )(keep, got)
+    totals = exchange(totals, "outer")
+    totals, send = lax.optimization_barrier((totals, send))
     inside_got = lax.ppermute(send, "y_lo", swap)
-    totals, inside_got = lax.optimization_barrier((exchange(totals, "outer"), inside_got))
     states, owned = pl.pallas_call(
         functools.partial(spread_kernel, key_scale, map_scale),
         in_specs=[whole] * 3,
@@ -360,6 +363,7 @@
 def solution(mesh):
     fine = Mesh(np.asarray(mesh.devices).reshape(4, 2, 2, 4, 2, 4), DP + CONTEXT)
     split = P(DP, CONTEXT, None)
+
     return jax.shard_map(
         per_device,
         mesh=fine,

time: 103 us -> 100 us (0.971)
  waiting for transfers between devices: 15.2 us -> 12.8 us
  blocking collectives: 21.3 us -> 19 us
  starting transfers between devices: 37.4 us -> 39.5 us
    ppermute x1, waiting for transfers between devices: 4.97 us -> 0.42 us  [per_device(): inside_got = lax.ppermute(send, 'y_lo', swap)]
    all_to_all x1, blocking collectives: 21.3 us -> 19 us  [exchange(): return lax.all_to_all(value, axes, 0, 0, tiled=True)]
    all_to_all x4, waiting for transfers between devices: 9.35 us -> 11.5 us  [exchange(): return lax.all_to_all(value, axes, 0, 0, tiled=True)]
    all_to_all x4, starting transfers between devices: 25.1 us -> 26.9 us  [exchange(): return lax.all_to_all(value, axes, 0, 0, tiled=True)]
  transfers between devices with their start and end apart: 7 -> 7, of which waited for: 3 -> 4; matrix products, arithmetic and copies ran while one was open for 0% -> 0% of each run, Pallas kernels for 19% -> 19%
where the time goes in v8:
time: 100 us; the launch traced here: 98.7 us
  starting transfers between devices  39.5 us (40%)
  Pallas kernels  25.2 us (25%)
  blocking collectives  19 us (19%)
  waiting for transfers between devices  12.8 us (13%)
  local copies, waits for them, and re-layouts  1.43 us (1%)
    all_to_all x4, starting transfers between devices, exchange(): return lax.all_to_all(value, axes, 0, 0, tiled=True)  26.9 us
    all_to_all x1, blocking collectives, exchange(): return lax.all_to_all(value, axes, 0, 0, tiled=True)  19 us
    all_to_all x4, waiting for transfers between devices, exchange(): return lax.all_to_all(value, axes, 0, 0, tiled=True)  11.5 us
    pallas_call x1, Pallas kernels, per_device(): pl.pallas_call(functools.partial(inside_kernel, key_scale, map_scale), gr...  9.67 us
    pallas_call x1, Pallas kernels, per_device(): pl.pallas_call(functools.partial(grads_kernel, key_scale), grid=(steps,),...  6.81 us
    ppermute x1, starting transfers between devices, per_device(): got = lax.ppermute(send, 'core', swap)  5.67 us
    ppermute x1, starting transfers between devices, per_device(): lax.ppermute(owned[1], 'core', swap)  3.71 us
    pallas_call x1, Pallas kernels, per_device(): pl.pallas_call(products_kernel, grid=(steps,), in_specs=[wide, wide, wide...  3.69 us
  transfers between devices with their start and end apart: 7, of which 4 were waited for; matrix products, arithmetic and copies ran while one was open for 0% of the time, Pallas kernels for 19%

profile of v8, /device:TPU:1, one launch (start us, length us, event | category | flops | bytes accessed | tf_op | source)
XLA Modules:
  0.0 98.7 jit_solution(2146635809549490511)
XLA Ops:
  0.6 3.7 %shard_map.102 = bf16[16,264,128]{2,1,0:T(8,128)(2,1)} custom-call(bf16[128,2048]{1,0:T(8,128)(2,1)} %bitcast.23, bf16[128,2048]{1,0:T(8,128)(2,1)} %bitcast.25, bf16[128,2048]{1,0:T(8,128)(2,1)} %bitcast.16, bf16[128,2048]{1,0:T(8,128)(2,1)} %bitcast.19, f32[16,128]{1,0:T(8,128)} %bitcast.27), custom_call_target="tpu_custom_call" | custom-call | flops 134217728 | bytes 3145728 | tf_op jit(solution)/shard_map/pallas_call | solution.py:278
  4.3 6.6 %all-to-all-start = ((bf16[8,2,264,128]{3,2,1,0:T(8,128)(2,1)}), bf16[8,2,264,128]{3,2,1,0:T(8,128)(2,1)S(1)}, u32[]{:S(2)}, u32[]{:S(2)}) async-start(bf16[8,2,264,128]{3,2,1,0:T(8,128)(2,1)} %bitcast.22), calls=%async_computation | async-start | bytes 2162688 | tf_op jit(solution)/shard_map/all_to_all | solution.py:259
  11.0 0.0 copy-start
  11.0 0.0 copy-start.1
  11.0 9.7 %shard_map.103 = (bf16[128,2048]{1,0:T(8,128)(2,1)}, bf16[128,2048]{1,0:T(8,128)(2,1)}, f32[128,2048]{1,0:T(8,128)}, f32[128,2048]{1,0:T(8,128)}, bf16[2,8,2,2,3...) custom-call(bf16[128,2048]{1,0:T(8,128)(2,1)} %bitcast.24, bf16[128,2048]{1,0:T(8,128)(2,1)} %bitcast.26, ...), custom_call_target="tpu_custom_call" | custom-call | flops 469762048 | bytes 8388608 | tf_op jit(solution)/shard_map/pallas_call | solution.py:290
  20.7 5.7 %collective-permute-start = (bf16[2,8,128,128]{3,2,1,0:T(8,128)(2,1)}, bf16[2,8,128,128]{3,2,1,0:T(8,128)(2,1)S(1)}, u32[]{:S(2)}, u32[]{:S(2)}) collective-permute-start(bf16[2,8,128,128]{3,2,1,0:T(8,128)(2,1)} %bitcast.33), channel_id=1, source_target_pairs={{0,32},{32,0},{1,33},{33,1},{2,34},{34,2},{3,35},{35,3},{4,36},{36... | collective-permute-start | bytes 1572872 | tf_op jit(solution)/shard_map/ppermute | solution.py:317
  26.3 0.0 all-to-all-done.in_ref
  26.3 0.0 copy-done
  26.4 0.0 copy-done.1
  26.4 0.0 copy-start.2
  26.4 1.2 %shard_map.105 = bf16[4,2,144,128]{3,2,1,0:T(8,128)(2,1)} custom-call(bf16[8,2,264,128]{3,2,1,0:T(8,128)(2,1)S(1)} %all-to-all-done.in_ref, bf16[16,128,128]{2,1,0:T(8,128)(2,1)S(1)} %copy-done, bf16[16,128,128]{2,1,0:T(8,128)(2,1)S(1)} %copy-done.1), custom_call_target="tpu_custom_call" | custom-call | tf_op jit(solution)/shard_map/pallas_call | solution.py:304
  27.6 9.0 %all-to-all-start.1 = ((bf16[4,2,144,128]{3,2,1,0:T(8,128)(2,1)}), bf16[4,2,144,128]{3,2,1,0:T(8,128)(2,1)S(1)}, u32[]{:S(2)}, u32[]{:S(2)}) async-start(bf16[4,2,144,128]{3,2,1,0:T(8,128)(2,1)} %shard_map.105), calls=%async_computation.1 | async-start | bytes 589824 | tf_op jit(solution)/shard_map/all_to_all | solution.py:259
  36.6 0.0 collective-permute-done.got_ref
  36.6 0.0 copy-done.2
  36.6 0.1 shard_map.106
  36.8 0.0 copy-start.3
  36.8 0.7 copy-done.3
  37.5 0.0 copy-start.5
  37.5 0.7 copy-done.5
  38.2 0.5 shard_map.104.blocks_ref
  38.7 6.4 %all-to-all-done.1.totals_ref = bf16[4,2,144,128]{3,2,1,0:T(8,128)(2,1)S(1)} async-done(((bf16[4,2,144,128]{3,2,1,0:T(8,128)(2,1)}), bf16[4,2,144,128]{3,2,1,0:T(8,128)(2,1)S(1)}, u32[]{:S(2)}, u32[]{:S(2)}) %all-to-all-start.1) | async-done | bytes 294944 | tf_op jit(solution)/shard_map/all_to_all | solution.py:259
  45.1 1.7 %shard_map.107 = (bf16[8,512,128]{2,1,0:T(8,128)(2,1)}, bf16[2,8,32,128]{3,2,1,0:T(8,128)(2,1)S(1)}) custom-call(bf16[8,2,264,128]{3,2,1,0:T(8,128)(2,1)S(1)} %all-to-all-done.in_ref, bf16[8,2,256,128]{3,2,1,0:T(8,128)(2,1)S(1)} %shard_map.104.blocks_ref, bf16[4,2,144,128]{3,2,1,0:T(8,128)(2,1)S(1)} %all-to-all-done.1.totals_ref), custom_call_target="tpu_custom_call" | custom-call | tf_op jit(solution)/shard_map/pallas_call | solution.py:324
  46.8 0.0 copy-start.6
  46.8 0.0 copy-start.4
  46.8 6.7 %all-to-all-start.2 = ((bf16[8,512,128]{2,1,0:T(8,128)(2,1)}), bf16[8,512,128]{2,1,0:T(8,128)(2,1)S(1)}, u32[]{:S(2)}, u32[]{:S(2)}) async-start(bf16[8,512,128]{2,1,0:T(8,128)(2,1)} %get-tuple-element.31), calls=%async_computation.2 | async-start | bytes 2097152 | tf_op jit(solution)/shard_map/all_to_all | solution.py:259
  53.5 0.0 copy-done.6
  53.5 3.2 %collective-permute-start.1 = (bf16[8,128,128]{2,1,0:T(8,128)(2,1)S(1)}, bf16[8,128,128]{2,1,0:T(8,128)(2,1)S(1)}, u32[]{:S(2)}, u32[]{:S(2)}) collective-permute-start(bf16[8,128,128]{2,1,0:T(8,128)(2,1)S(1)} %copy-done.6), channel_id=1, source_target_pairs={{0,64},{64,0},{1,65},{65,1},{2,66},{66,2},{3,67},{67,3},{4,68},{68... | collective-permute-start | bytes 786440 | tf_op jit(solution)/shard_map/ppermute | solution.py:323
  56.7 3.7 %collective-permute-start.2 = (bf16[8,32,128]{2,1,0:T(8,128)(2,1)S(1)}, bf16[8,32,128]{2,1,0:T(8,128)(2,1)S(1)}, u32[]{:S(2)}, u32[]{:S(2)}) collective-permute-start(bf16[8,32,128]{2,1,0:T(8,128)(2,1)S(1)} %slice_bitcast_fusion), channel_id=1, source_target_pairs={{0,32},{32,0},{1,33},{33,1},{2,34},{34,2},{3,35},{35,3},{4,36},{36... | collective-permute-start | bytes 196616 | tf_op jit(solution)/shard_map/ppermute | solution.py:339
  60.5 0.9 collective-permute-done.2.carried_got_ref
  61.3 0.4 collective-permute-done.1.inside_got_ref
  61.7 0.0 copy-done.4
  61.8 0.8 shard_map.108
  62.6 5.1 %all-to-all-done.2.in_ref = bf16[8,512,128]{2,1,0:T(8,128)(2,1)S(1)} async-done(((bf16[8,512,128]{2,1,0:T(8,128)(2,1)}), bf16[8,512,128]{2,1,0:T(8,128)(2,1)S(1)}, u32[]{:S(2)}, u32[]{:S(2)}) %all-to-all-start.2) | async-done | bytes 1048608 | tf_op jit(solution)/shard_map/all_to_all | solution.py:259
  67.6 0.0 copy-start.7
  67.6 4.5 %all-to-all-start.3 = ((bf16[8,160,128]{2,1,0:T(8,128)(2,1)}), bf16[8,160,128]{2,1,0:T(8,128)(2,1)S(1)}, u32[]{:S(2)}, u32[]{:S(2)}) async-start(bf16[8,160,128]{2,1,0:T(8,128)(2,1)} %shard_map.108), calls=%async_computation.3 | async-start | bytes 655360 | tf_op jit(solution)/shard_map/all_to_all | solution.py:259
  72.1 0.0 copy-done.7
  72.1 6.8 %shard_map.109 = (bf16[128,2048]{1,0:T(8,128)(2,1)}, bf16[128,2048]{1,0:T(8,128)(2,1)}, bf16[128,2048]{1,0:T(8,128)(2,1)}) custom-call(bf16[128,2048]{1,0:T(8,128)(2,1)} %bitcast.18, bf16[128,2048]{1,0:T(8,128)(2,1)} %bitcast.21, bf16[128,2048]{1,0:T(8,128)(2,1)} %get-tuple-element.36.fq_ref, bf16[128,2048]{1,0:T(8,128)(2,1)} %get-tuple-element.37.fk_ref, ...), custom_call_target="tpu_custom_call" | custom-call | flops 469762048 | bytes 8388608 | tf_op jit(solution)/shard_map/pallas_call | solution.py:341
  78.9 0.0 all-to-all-done.3.in_ref
  79.0 19.0 %all_to_all.25.in_ref = bf16[32,8,128]{2,1,0:T(8,128)(2,1)S(1)} all-to-all(bf16[32,8,128]{2,1,0:T(8,128)(2,1)S(1)} %bitcast.15), channel_id=1, replica_groups=mesh['y_hi'=4,'y_lo'=2,'core'=2,'outer'=4,'inner'=2,'x'=4] {'y_hi','y_lo..., dimensions={0} | all-to-all | bytes 131072 | tf_op jit(solution)/shard_map/all_to_all | solution.py:259
  98.0 0.6 shard_map.111
  (2 shorter events, 0.1 us)
Async XLA Ops:
  4.3 22.0 %all-to-all-start = ((bf16[8,2,264,128]{3,2,1,0:T(8,128)(2,1)}), bf16[8,2,264,128]{3,2,1,0:T(8,128)(2,1)S(1)}, u32[]{:S(2)}, u32[]{:S(2)}) async-start(bf16[8,2,264,128]{3,2,1,0:T(8,128)(2,1)} %bitcast.22), calls=%async_computation | async-start | bytes 2162688 | tf_op jit(solution)/shard_map/all_to_all | solution.py:259
  11.0 15.4 %copy-start = (bf16[16,128,128]{2,1,0:T(8,128)(2,1)S(1)}, bf16[16,128,128]{2,1,0:T(8,128)(2,1)}, u32[]{:S(2)}) copy-start(bf16[16,128,128]{2,1,0:T(8,128)(2,1)} %mq_ref.7) | copy-start | bytes 1572868
  11.0 15.4 %copy-start.1 = (bf16[16,128,128]{2,1,0:T(8,128)(2,1)S(1)}, bf16[16,128,128]{2,1,0:T(8,128)(2,1)}, u32[]{:S(2)}) copy-start(bf16[16,128,128]{2,1,0:T(8,128)(2,1)} %mk_ref.7) | copy-start | bytes 1572868
  20.7 16.0 %collective-permute-start = (bf16[2,8,128,128]{3,2,1,0:T(8,128)(2,1)}, bf16[2,8,128,128]{3,2,1,0:T(8,128)(2,1)S(1)}, u32[]{:S(2)}, u32[]{:S(2)}) collective-permute-start(bf16[2,8,128,128]{3,2,1,0:T(8,128)(2,1)} %bitcast.33), channel_id=1, source_target_pairs={{0,32},{32,0},{1,33},{33,1},{2,34},{34,2},{3,35},{35,3},{4,36},{36... | collective-permute-start | bytes 1572872 | tf_op jit(solution)/shard_map/ppermute | solution.py:317
  26.4 10.3 %copy-start.2 = (bf16[2,8,2,2,32,128]{5,4,3,2,1,0:T(8,128)(2,1)S(1)}, bf16[2,8,2,2,32,128]{5,4,3,2,1,0:T(8,128)(2,1)}, u32[]{:S(2)}) copy-start(bf16[2,8,2,2,32,128]{5,4,3,2,1,0:T(8,128)(2,1)} %get-tuple-element.25) | copy-start | bytes 1572868
  27.6 17.5 %all-to-all-start.1 = ((bf16[4,2,144,128]{3,2,1,0:T(8,128)(2,1)}), bf16[4,2,144,128]{3,2,1,0:T(8,128)(2,1)S(1)}, u32[]{:S(2)}, u32[]{:S(2)}) async-start(bf16[4,2,144,128]{3,2,1,0:T(8,128)(2,1)} %shard_map.105), calls=%async_computation.1 | async-start | bytes 589824 | tf_op jit(solution)/shard_map/all_to_all | solution.py:259
  36.8 0.7 copy-start.3
  37.5 0.7 copy-start.5
  46.8 6.7 %copy-start.6 = (bf16[8,128,128]{2,1,0:T(8,128)(2,1)S(1)}, bf16[8,128,128]{2,1,0:T(8,128)(2,1)}, u32[]{:S(2)}) copy-start(bf16[8,128,128]{2,1,0:T(8,128)(2,1)} %copy-done.5) | copy-start | bytes 786436
  46.8 15.0 %copy-start.4 = (bf16[8,128,128]{2,1,0:T(8,128)(2,1)S(1)}, bf16[8,128,128]{2,1,0:T(8,128)(2,1)}, u32[]{:S(2)}) copy-start(bf16[8,128,128]{2,1,0:T(8,128)(2,1)} %copy-done.3) | copy-start | bytes 786436
  46.8 20.8 %all-to-all-start.2 = ((bf16[8,512,128]{2,1,0:T(8,128)(2,1)}), bf16[8,512,128]{2,1,0:T(8,128)(2,1)S(1)}, u32[]{:S(2)}, u32[]{:S(2)}) async-start(bf16[8,512,128]{2,1,0:T(8,128)(2,1)} %get-tuple-element.31), calls=%async_computation.2 | async-start | bytes 2097152 | tf_op jit(solution)/shard_map/all_to_all | solution.py:259
  53.5 8.2 %collective-permute-start.1 = (bf16[8,128,128]{2,1,0:T(8,128)(2,1)S(1)}, bf16[8,128,128]{2,1,0:T(8,128)(2,1)S(1)}, u32[]{:S(2)}, u32[]{:S(2)}) collective-permute-start(bf16[8,128,128]{2,1,0:T(8,128)(2,1)S(1)} %copy-done.6), channel_id=1, source_target_pairs={{0,64},{64,0},{1,65},{65,1},{2,66},{66,2},{3,67},{67,3},{4,68},{68... | collective-permute-start | bytes 786440 | tf_op jit(solution)/shard_map/ppermute | solution.py:323
  56.7 4.6 %collective-permute-start.2 = (bf16[8,32,128]{2,1,0:T(8,128)(2,1)S(1)}, bf16[8,32,128]{2,1,0:T(8,128)(2,1)S(1)}, u32[]{:S(2)}, u32[]{:S(2)}) collective-permute-start(bf16[8,32,128]{2,1,0:T(8,128)(2,1)S(1)} %slice_bitcast_fusion), channel_id=1, source_target_pairs={{0,32},{32,0},{1,33},{33,1},{2,34},{34,2},{3,35},{35,3},{4,36},{36... | collective-permute-start | bytes 196616 | tf_op jit(solution)/shard_map/ppermute | solution.py:339
  67.6 4.5 %copy-start.7 = (bf16[8,512,128]{2,1,0:T(8,128)(2,1)}, bf16[8,512,128]{2,1,0:T(8,128)(2,1)S(1)}, u32[]{:S(2)}) copy-start(bf16[8,512,128]{2,1,0:T(8,128)(2,1)S(1)} %all-to-all-done.2.in_ref) | copy-start | bytes 3145732
  67.6 11.3 %all-to-all-start.3 = ((bf16[8,160,128]{2,1,0:T(8,128)(2,1)}), bf16[8,160,128]{2,1,0:T(8,128)(2,1)S(1)}, u32[]{:S(2)}, u32[]{:S(2)}) async-start(bf16[8,160,128]{2,1,0:T(8,128)(2,1)} %shard_map.108), calls=%async_computation.3 | async-start | bytes 655360 | tf_op jit(solution)/shard_map/all_to_all | solution.py:259

commit v9 on v8

--- a/solution.py
+++ b/solution.py
@@ -338,16 +338,28 @@
         compiler_params=VMEM,
     )(keep, inside_got, owned, lax.ppermute(owned[1], "core", swap))
     carried, maps = lax.optimization_barrier((carried, maps))
-    query_grad, key_grad, value_grad = pl.pallas_call(
-        functools.partial(grads_kernel, key_scale),
-        grid=(steps,),
-        in_specs=[wide] * 4 + [gate_spec, map_spec, map_spec] + [wide] * 2
-        + [pl.BlockSpec((near // steps, rows, width), lambda i: (i, 0, 0))],
-        out_specs=[wide] * 3,
-        out_shape=[wide_shape] * 3,
-        cost_estimate=pl.CostEstimate(flops=7 * flops, bytes_accessed=8 << 20, transcendentals=0),
-    )(v, g, fq, fk, gates, query_map, key_map, query_inside, key_inside, carried)
-    maps, query_grad = lax.optimization_barrier((exchange(maps, NEAR), query_grad))
+
+    def grads(part, carried, *written):
+        mine = pl.BlockSpec((length, GROUP * width), lambda i: (0, part))
+        maps_of = pl.BlockSpec((GROUP, width, width), lambda i: (part, 0, 0))
+
+        def kernel(*refs):
+            grads_kernel(key_scale, *refs[:10], *refs[10 + len(written) :])
+
+        return pl.pallas_call(
+            kernel,
+            grid=(1,),
+            in_specs=[mine] * 4 + [pl.BlockSpec((GROUP, length), lambda i: (part, 0)), maps_of, maps_of] + [mine] * 2
+            + [pl.BlockSpec((near // steps, rows, width), lambda i: (part, 0, 0))] + [anywhere] * len(written),
+            out_specs=[mine] * 3,
+            out_shape=[wide_shape] * 3,
+            input_output_aliases={10 + i: i for i in range(len(written))},
+            cost_estimate=pl.CostEstimate(flops=7 * flops // 2, bytes_accessed=4 << 20, transcendentals=0),
+        )(v, g, fq, fk, gates, query_map, key_map, query_inside, key_inside, carried, *written)
+
+    written = grads(0, carried)
+    maps, carried, *written = lax.optimization_barrier((exchange(maps, NEAR), carried, *written))
+    query_grad, key_grad, value_grad = grads(1, carried, *written)
     maps = pl.pallas_call(
         gather_kernel,
         in_specs=[whole],

time: 100 us -> 101 us (1.010)
  the two profiles are of different devices: /device:TPU:1 before, /device:TPU:8 now
where the time goes in v9:
time: 101 us
  starting transfers between devices  37.8 us (37%)
  waiting for transfers between devices  32.3 us (32%)
  Pallas kernels  28.3 us (28%)
  local copies, waits for them, and re-layouts  1.43 us (1%)
    all_to_all x5, starting transfers between devices, exchange(): return lax.all_to_all(value, axes, 0, 0, tiled=True)  31.6 us
    all_to_all x5, waiting for transfers between devices, exchange(): return lax.all_to_all(value, axes, 0, 0, tiled=True)  27.5 us
    pallas_call x1, Pallas kernels, per_device(): pl.pallas_call(functools.partial(inside_kernel, key_scale, map_scale), gr...  9.61 us
    pallas_call x2, Pallas kernels, grads(): pl.pallas_call(kernel, grid=(1,), in_specs=[mine] * 4 + [pl.BlockSpec((GR...  9.44 us
    pallas_call x1, Pallas kernels, per_device(): pl.pallas_call(products_kernel, grid=(steps,), in_specs=[wide, wide, wide...  3.69 us
    ppermute x1, waiting for transfers between devices, per_device(): inside_got = lax.ppermute(send, 'y_lo', swap)  3.55 us
    ppermute x1, starting transfers between devices, per_device(): inside_got = lax.ppermute(send, 'y_lo', swap)  2.36 us
  transfers between devices with their start and end apart: 8, of which 7 were waited for; matrix products, arithmetic and copies ran while one was open for 0% of the time, Pallas kernels for 22%

profile of v9, /device:TPU:8, one launch (start us, length us, event | category | flops | bytes accessed | tf_op | source)
XLA Modules:
  0.0 100.6 jit_solution(17458695023610398457)
XLA Ops:
  0.6 3.7 %shard_map.103 = bf16[16,264,128]{2,1,0:T(8,128)(2,1)} custom-call(bf16[128,2048]{1,0:T(8,128)(2,1)} %bitcast.24, bf16[128,2048]{1,0:T(8,128)(2,1)} %bitcast.26, bf16[128,2048]{1,0:T(8,128)(2,1)} %bitcast.15, bf16[128,2048]{1,0:T(8,128)(2,1)} %bitcast.19, f32[16,128]{1,0:T(8,128)} %bitcast.31), custom_call_target="tpu_custom_call" | custom-call | flops 134217728 | bytes 3145728 | tf_op jit(solution)/shard_map/pallas_call | solution.py:278
  4.3 6.1 %all-to-all-start = ((bf16[8,2,264,128]{3,2,1,0:T(8,128)(2,1)}), bf16[8,2,264,128]{3,2,1,0:T(8,128)(2,1)S(1)}, u32[]{:S(2)}, u32[]{:S(2)}) async-start(bf16[8,2,264,128]{3,2,1,0:T(8,128)(2,1)} %bitcast.23), calls=%async_computation | async-start | bytes 2162688 | tf_op jit(solution)/shard_map/all_to_all | solution.py:259
  10.4 0.0 copy-start
  10.4 0.0 copy-start.1
  10.4 9.6 %shard_map.102 = (bf16[128,2048]{1,0:T(8,128)(2,1)}, bf16[128,2048]{1,0:T(8,128)(2,1)}, f32[128,2048]{1,0:T(8,128)}, f32[128,2048]{1,0:T(8,128)}, bf16[2,8,2,2,3...) custom-call(bf16[128,2048]{1,0:T(8,128)(2,1)} %bitcast.25, bf16[128,2048]{1,0:T(8,128)(2,1)} %bitcast.27, ...), custom_call_target="tpu_custom_call" | custom-call | flops 469762048 | bytes 8388608 | tf_op jit(solution)/shard_map/pallas_call | solution.py:290
  20.1 1.9 %collective-permute-start = (bf16[2,8,128,128]{3,2,1,0:T(8,128)(2,1)}, bf16[2,8,128,128]{3,2,1,0:T(8,128)(2,1)S(1)}, u32[]{:S(2)}, u32[]{:S(2)}) collective-permute-start(bf16[2,8,128,128]{3,2,1,0:T(8,128)(2,1)} %bitcast.35), channel_id=1, source_target_pairs={{0,32},{32,0},{1,33},{33,1},{2,34},{34,2},{3,35},{35,3},{4,36},{36... | collective-permute-start | bytes 1572872 | tf_op jit(solution)/shard_map/ppermute | solution.py:317
  22.0 3.6 %all-to-all-done.in_ref = bf16[8,2,264,128]{3,2,1,0:T(8,128)(2,1)S(1)} async-done(((bf16[8,2,264,128]{3,2,1,0:T(8,128)(2,1)}), bf16[8,2,264,128]{3,2,1,0:T(8,128)(2,1)S(1)}, u32[]{:S(2)}, u32[]{:S(2)}) %all-to-all-start) | async-done | bytes 1081376 | tf_op jit(solution)/shard_map/all_to_all | solution.py:259
  25.6 0.0 copy-done
  25.6 0.0 copy-done.1
  25.6 0.0 copy-start.2
  25.6 1.2 %shard_map.105 = bf16[4,2,144,128]{3,2,1,0:T(8,128)(2,1)} custom-call(bf16[8,2,264,128]{3,2,1,0:T(8,128)(2,1)S(1)} %all-to-all-done.in_ref, bf16[16,128,128]{2,1,0:T(8,128)(2,1)S(1)} %copy-done, bf16[16,128,128]{2,1,0:T(8,128)(2,1)S(1)} %copy-done.1), custom_call_target="tpu_custom_call" | custom-call | tf_op jit(solution)/shard_map/pallas_call | solution.py:304
  26.8 9.4 %all-to-all-start.1 = ((bf16[4,2,144,128]{3,2,1,0:T(8,128)(2,1)}), bf16[4,2,144,128]{3,2,1,0:T(8,128)(2,1)S(1)}, u32[]{:S(2)}, u32[]{:S(2)}) async-start(bf16[4,2,144,128]{3,2,1,0:T(8,128)(2,1)} %shard_map.105), calls=%async_computation.1 | async-start | bytes 589824 | tf_op jit(solution)/shard_map/all_to_all | solution.py:259
  36.2 0.0 collective-permute-done.got_ref
  36.2 0.0 copy-done.2
  36.2 0.1 shard_map.106
  36.3 0.0 copy-start.3
  36.4 0.7 copy-done.3
  37.0 0.0 copy-start.5
  37.0 0.7 copy-done.5
  37.7 0.5 shard_map.104.blocks_ref
  38.2 9.6 %all-to-all-done.1.totals_ref = bf16[4,2,144,128]{3,2,1,0:T(8,128)(2,1)S(1)} async-done(((bf16[4,2,144,128]{3,2,1,0:T(8,128)(2,1)}), bf16[4,2,144,128]{3,2,1,0:T(8,128)(2,1)S(1)}, u32[]{:S(2)}, u32[]{:S(2)}) %all-to-all-start.1) | async-done | bytes 294944 | tf_op jit(solution)/shard_map/all_to_all | solution.py:259
  47.8 1.6 %shard_map.107 = (bf16[8,512,128]{2,1,0:T(8,128)(2,1)}, bf16[2,8,32,128]{3,2,1,0:T(8,128)(2,1)S(1)}) custom-call(bf16[8,2,264,128]{3,2,1,0:T(8,128)(2,1)S(1)} %all-to-all-done.in_ref, bf16[8,2,256,128]{3,2,1,0:T(8,128)(2,1)S(1)} %shard_map.104.blocks_ref, bf16[4,2,144,128]{3,2,1,0:T(8,128)(2,1)S(1)} %all-to-all-done.1.totals_ref), custom_call_target="tpu_custom_call" | custom-call | tf_op jit(solution)/shard_map/pallas_call | solution.py:324
  49.5 0.0 copy-start.6
  49.5 0.0 copy-start.4
  49.5 4.0 %all-to-all-start.2 = ((bf16[8,512,128]{2,1,0:T(8,128)(2,1)}), bf16[8,512,128]{2,1,0:T(8,128)(2,1)S(1)}, u32[]{:S(2)}, u32[]{:S(2)}) async-start(bf16[8,512,128]{2,1,0:T(8,128)(2,1)} %get-tuple-element.41), calls=%async_computation.2 | async-start | bytes 2097152 | tf_op jit(solution)/shard_map/all_to_all | solution.py:259
  53.5 0.0 copy-done.6
  53.5 2.4 %collective-permute-start.1 = (bf16[8,128,128]{2,1,0:T(8,128)(2,1)S(1)}, bf16[8,128,128]{2,1,0:T(8,128)(2,1)S(1)}, u32[]{:S(2)}, u32[]{:S(2)}) collective-permute-start(bf16[8,128,128]{2,1,0:T(8,128)(2,1)S(1)} %copy-done.6), channel_id=1, source_target_pairs={{0,64},{64,0},{1,65},{65,1},{2,66},{66,2},{3,67},{67,3},{4,68},{68... | collective-permute-start | bytes 786440 | tf_op jit(solution)/shard_map/ppermute | solution.py:323
  55.9 1.9 %collective-permute-start.2 = (bf16[8,32,128]{2,1,0:T(8,128)(2,1)S(1)}, bf16[8,32,128]{2,1,0:T(8,128)(2,1)S(1)}, u32[]{:S(2)}, u32[]{:S(2)}) collective-permute-start(bf16[8,32,128]{2,1,0:T(8,128)(2,1)S(1)} %slice_bitcast_fusion), channel_id=1, source_target_pairs={{0,32},{32,0},{1,33},{33,1},{2,34},{34,2},{3,35},{35,3},{4,36},{36... | collective-permute-start | bytes 196616 | tf_op jit(solution)/shard_map/ppermute | solution.py:339
  57.8 1.2 %collective-permute-done.2.carried_got_ref = bf16[8,32,128]{2,1,0:T(8,128)(2,1)S(1)} collective-permute-done((bf16[8,32,128]{2,1,0:T(8,128)(2,1)S(1)}, bf16[8,32,128]{2,1,0:T(8,128)(2,1)S(1)}, u32[]{:S(2)}, u32[]{:S(2)}) %collective-permute-start.2) | collective-permute-done | bytes 65568 | tf_op jit(solution)/shard_map/ppermute | solution.py:339
  59.0 3.6 %collective-permute-done.1.inside_got_ref = bf16[8,128,128]{2,1,0:T(8,128)(2,1)S(1)} collective-permute-done((bf16[8,128,128]{2,1,0:T(8,128)(2,1)S(1)}, bf16[8,128,128]{2,1,0:T(8,128)(2,1)S(1)}, u32[]{:S(2)}, u32[]{:S(2)}) %collective-permute-start.1) | collective-permute-done | bytes 262176 | tf_op jit(solution)/shard_map/ppermute | solution.py:323
  62.6 0.0 copy-done.4
  62.6 0.8 shard_map.108
  63.4 4.3 %all-to-all-done.2.refs_9_ = bf16[8,512,128]{2,1,0:T(8,128)(2,1)S(1)} async-done(((bf16[8,512,128]{2,1,0:T(8,128)(2,1)}), bf16[8,512,128]{2,1,0:T(8,128)(2,1)S(1)}, u32[]{:S(2)}, u32[]{:S(2)}) %all-to-all-start.2) | async-done | bytes 1048608 | tf_op jit(solution)/shard_map/all_to_all | solution.py:259
  67.7 0.0 copy-start.7
  67.7 3.6 %all-to-all-start.3 = ((bf16[8,160,128]{2,1,0:T(8,128)(2,1)}), bf16[8,160,128]{2,1,0:T(8,128)(2,1)S(1)}, u32[]{:S(2)}, u32[]{:S(2)}) async-start(bf16[8,160,128]{2,1,0:T(8,128)(2,1)} %shard_map.108), calls=%async_computation.3 | async-start | bytes 655360 | tf_op jit(solution)/shard_map/all_to_all | solution.py:259
  71.4 0.0 copy-done.7
  71.4 4.7 %shard_map.109 = (bf16[128,2048]{1,0:T(8,128)(2,1)}, bf16[128,2048]{1,0:T(8,128)(2,1)}, bf16[128,2048]{1,0:T(8,128)(2,1)}) custom-call(bf16[128,2048]{1,0:T(8,128)(2,1)} %bitcast.17, bf16[128,2048]{1,0:T(8,128)(2,1)} %bitcast.21, bf16[128,2048]{1,0:T(8,128)(2,1)} %get-tuple-element.31.refs_2_, bf16[128,2048]{1,0:T(8,128)(2,1)} %get-tuple-element.32.refs_3_, ...), custom_call_target="tpu_custom_call" | custom-call | flops 234881024 | bytes 4194304 | tf_op jit(solution)/shard_map/pallas_call | solution.py:349
  76.1 3.3 %all-to-all-done.3.in_ref = bf16[8,160,128]{2,1,0:T(8,128)(2,1)S(1)} async-done(((bf16[8,160,128]{2,1,0:T(8,128)(2,1)}), bf16[8,160,128]{2,1,0:T(8,128)(2,1)S(1)}, u32[]{:S(2)}, u32[]{:S(2)}) %all-to-all-start.3) | async-done | bytes 327712 | tf_op jit(solution)/shard_map/all_to_all | solution.py:259
  79.4 0.7 shard_map.111
  80.0 8.5 %all-to-all-start.4 = ((bf16[32,8,128]{2,1,0:T(8,128)(2,1)}), bf16[32,8,128]{2,1,0:T(8,128)(2,1)S(1)}, u32[]{:S(2)}, u32[]{:S(2)}) async-start(bf16[32,8,128]{2,1,0:T(8,128)(2,1)} %bitcast.12), calls=%async_computation.4 | async-start | bytes 131072 | tf_op jit(solution)/shard_map/all_to_all | solution.py:259
  88.5 4.7 %shard_map.110 = (bf16[128,2048]{1,0:T(8,128)(2,1)}, bf16[128,2048]{1,0:T(8,128)(2,1)}, bf16[128,2048]{1,0:T(8,128)(2,1)}) custom-call(bf16[128,2048]{1,0:T(8,128)(2,1)} %bitcast.18, bf16[128,2048]{1,0:T(8,128)(2,1)} %bitcast.22, bf16[128,2048]{1,0:T(8,128)(2,1)} %get-tuple-element.31.refs_2_, ...), custom_call_target="tpu_custom_call", output_to_operand_aliasing={{0}: (10, {}), {1}: (11, {}), {2}: (12, {})} | custom-call | flops 234881024 | bytes 4194304 | tf_op jit(solution)/shard_map/pallas_call | solution.py:349
  93.2 6.7 %all-to-all-done.4.in_ref = bf16[32,8,128]{2,1,0:T(8,128)(2,1)S(1)} async-done(((bf16[32,8,128]{2,1,0:T(8,128)(2,1)}), bf16[32,8,128]{2,1,0:T(8,128)(2,1)S(1)}, u32[]{:S(2)}, u32[]{:S(2)}) %all-to-all-start.4) | async-done | bytes 65568 | tf_op jit(solution)/shard_map/all_to_all | solution.py:259
  99.9 0.6 shard_map.112
  (1 shorter events, 0.0 us)
Async XLA Ops:
  4.3 21.3 %all-to-all-start = ((bf16[8,2,264,128]{3,2,1,0:T(8,128)(2,1)}), bf16[8,2,264,128]{3,2,1,0:T(8,128)(2,1)S(1)}, u32[]{:S(2)}, u32[]{:S(2)}) async-start(bf16[8,2,264,128]{3,2,1,0:T(8,128)(2,1)} %bitcast.23), calls=%async_computation | async-start | bytes 2162688 | tf_op jit(solution)/shard_map/all_to_all | solution.py:259
  10.4 15.2 %copy-start = (bf16[16,128,128]{2,1,0:T(8,128)(2,1)S(1)}, bf16[16,128,128]{2,1,0:T(8,128)(2,1)}, u32[]{:S(2)}) copy-start(bf16[16,128,128]{2,1,0:T(8,128)(2,1)} %refs_5_.3) | copy-start | bytes 1572868
  10.4 15.2 %copy-start.1 = (bf16[16,128,128]{2,1,0:T(8,128)(2,1)S(1)}, bf16[16,128,128]{2,1,0:T(8,128)(2,1)}, u32[]{:S(2)}) copy-start(bf16[16,128,128]{2,1,0:T(8,128)(2,1)} %refs_6_.3) | copy-start | bytes 1572868
  20.1 16.1 %collective-permute-start = (bf16[2,8,128,128]{3,2,1,0:T(8,128)(2,1)}, bf16[2,8,128,128]{3,2,1,0:T(8,128)(2,1)S(1)}, u32[]{:S(2)}, u32[]{:S(2)}) collective-permute-start(bf16[2,8,128,128]{3,2,1,0:T(8,128)(2,1)} %bitcast.35), channel_id=1, source_target_pairs={{0,32},{32,0},{1,33},{33,1},{2,34},{34,2},{3,35},{35,3},{4,36},{36... | collective-permute-start | bytes 1572872 | tf_op jit(solution)/shard_map/ppermute | solution.py:317
  25.6 10.6 %copy-start.2 = (bf16[2,8,2,2,32,128]{5,4,3,2,1,0:T(8,128)(2,1)S(1)}, bf16[2,8,2,2,32,128]{5,4,3,2,1,0:T(8,128)(2,1)}, u32[]{:S(2)}) copy-start(bf16[2,8,2,2,32,128]{5,4,3,2,1,0:T(8,128)(2,1)} %get-tuple-element.35) | copy-start | bytes 1572868
  26.8 21.0 %all-to-all-start.1 = ((bf16[4,2,144,128]{3,2,1,0:T(8,128)(2,1)}), bf16[4,2,144,128]{3,2,1,0:T(8,128)(2,1)S(1)}, u32[]{:S(2)}, u32[]{:S(2)}) async-start(bf16[4,2,144,128]{3,2,1,0:T(8,128)(2,1)} %shard_map.105), calls=%async_computation.1 | async-start | bytes 589824 | tf_op jit(solution)/shard_map/all_to_all | solution.py:259
  36.3 0.7 copy-start.3
  37.0 0.7 copy-start.5
  49.5 4.0 %copy-start.6 = (bf16[8,128,128]{2,1,0:T(8,128)(2,1)S(1)}, bf16[8,128,128]{2,1,0:T(8,128)(2,1)}, u32[]{:S(2)}) copy-start(bf16[8,128,128]{2,1,0:T(8,128)(2,1)} %copy-done.5) | copy-start | bytes 786436
  49.5 13.1 %copy-start.4 = (bf16[8,128,128]{2,1,0:T(8,128)(2,1)S(1)}, bf16[8,128,128]{2,1,0:T(8,128)(2,1)}, u32[]{:S(2)}) copy-start(bf16[8,128,128]{2,1,0:T(8,128)(2,1)} %copy-done.3) | copy-start | bytes 786436
  49.5 18.3 %all-to-all-start.2 = ((bf16[8,512,128]{2,1,0:T(8,128)(2,1)}), bf16[8,512,128]{2,1,0:T(8,128)(2,1)S(1)}, u32[]{:S(2)}, u32[]{:S(2)}) async-start(bf16[8,512,128]{2,1,0:T(8,128)(2,1)} %get-tuple-element.41), calls=%async_computation.2 | async-start | bytes 2097152 | tf_op jit(solution)/shard_map/all_to_all | solution.py:259
  53.5 9.1 %collective-permute-start.1 = (bf16[8,128,128]{2,1,0:T(8,128)(2,1)S(1)}, bf16[8,128,128]{2,1,0:T(8,128)(2,1)S(1)}, u32[]{:S(2)}, u32[]{:S(2)}) collective-permute-start(bf16[8,128,128]{2,1,0:T(8,128)(2,1)S(1)} %copy-done.6), channel_id=1, source_target_pairs={{0,64},{64,0},{1,65},{65,1},{2,66},{66,2},{3,67},{67,3},{4,68},{68... | collective-permute-start | bytes 786440 | tf_op jit(solution)/shard_map/ppermute | solution.py:323
  55.9 3.1 %collective-permute-start.2 = (bf16[8,32,128]{2,1,0:T(8,128)(2,1)S(1)}, bf16[8,32,128]{2,1,0:T(8,128)(2,1)S(1)}, u32[]{:S(2)}, u32[]{:S(2)}) collective-permute-start(bf16[8,32,128]{2,1,0:T(8,128)(2,1)S(1)} %slice_bitcast_fusion), channel_id=1, source_target_pairs={{0,32},{32,0},{1,33},{33,1},{2,34},{34,2},{3,35},{35,3},{4,36},{36... | collective-permute-start | bytes 196616 | tf_op jit(solution)/shard_map/ppermute | solution.py:339
  67.7 3.6 %copy-start.7 = (bf16[8,512,128]{2,1,0:T(8,128)(2,1)}, bf16[8,512,128]{2,1,0:T(8,128)(2,1)S(1)}, u32[]{:S(2)}) copy-start(bf16[8,512,128]{2,1,0:T(8,128)(2,1)S(1)} %all-to-all-done.2.refs_9_) | copy-start | bytes 3145732
  67.7 11.6 %all-to-all-start.3 = ((bf16[8,160,128]{2,1,0:T(8,128)(2,1)}), bf16[8,160,128]{2,1,0:T(8,128)(2,1)S(1)}, u32[]{:S(2)}, u32[]{:S(2)}) async-start(bf16[8,160,128]{2,1,0:T(8,128)(2,1)} %shard_map.108), calls=%async_computation.3 | async-start | bytes 655360 | tf_op jit(solution)/shard_map/all_to_all | solution.py:259
  80.0 19.9 %all-to-all-start.4 = ((bf16[32,8,128]{2,1,0:T(8,128)(2,1)}), bf16[32,8,128]{2,1,0:T(8,128)(2,1)S(1)}, u32[]{:S(2)}, u32[]{:S(2)}) async-start(bf16[32,8,128]{2,1,0:T(8,128)(2,1)} %bitcast.12), calls=%async_computation.4 | async-start | bytes 131072 | tf_op jit(solution)/shard_map/all_to_all | solution.py:259

commit v10 on v8

--- a/solution.py
+++ b/solution.py
@@ -220,28 +220,36 @@
             out_ref[m, high, y_lo] = (here + total[at : at + 32]).astype(BF16)
 
 
-def grads_kernel(
-    key_scale, v_ref, g_ref, fq_ref, fk_ref, gates_ref, mq_ref, mk_ref, qb_ref, kb_ref, in_ref, qg_ref, kg_ref, vg_ref
-):
-    width = mq_ref.shape[1]
-    length = fk_ref.shape[0]
-    causal = causal_mask(length)
+def values_kernel(g_ref, fq_ref, fk_ref, gates_ref, out_ref):
+    width = g_ref.shape[1] // GROUP
+    causal = causal_mask(g_ref.shape[0])
     columns = running_columns(gates_ref[...])
     rows = running_rows(gates_ref[...])
     for j in range(GROUP):
         lanes = slice(j * width, (j + 1) * width)
+        within = jnp.exp(jnp.where(causal, columns[:, j : j + 1] - rows[j : j + 1], -1e30))
+        scores = (dot(fq_ref[:, lanes], fk_ref[:, lanes], (1, 1)) * within).astype(BF16)
+        out_ref[:, lanes] = dot(scores, g_ref[:, lanes], (0, 0))
+
+
+def grads_kernel(
+    key_scale, v_ref, g_ref, vgi_ref, fk_ref, gates_ref, mq_ref, mk_ref, qb_ref, kb_ref, in_ref, qg_ref, kg_ref, vg_ref
+):
+    width = mq_ref.shape[1]
+    length = fk_ref.shape[0]
+    columns = running_columns(gates_ref[...])
+    for j in range(GROUP):
+        lanes = slice(j * width, (j + 1) * width)
         owner, bit = place(j)
         run = columns[:, j : j + 1]
-        within = jnp.exp(jnp.where(causal, run - rows[j : j + 1], -1e30))
         start = jnp.exp(run)
         end = jnp.exp(run[length - 1 : length] - run)
         state_in = in_ref[owner, 2 * bit * width : (2 * bit + 1) * width]
         grad_in = in_ref[owner, (2 * bit + 1) * width : (2 * bit + 2) * width]
         g, fk = g_ref[:, lanes], fk_ref[:, lanes]
-        scores = (dot(fq_ref[:, lanes], fk, (1, 1)) * within).astype(BF16)
         query_back = (qb_ref[:, lanes] + dot(g, state_in, (1, 1)) * start).astype(BF16)
         key_back = (kb_ref[:, lanes] + dot(v_ref[:, lanes], grad_in, (1, 1)) * (end * key_scale)).astype(BF16)
-        vg_ref[:, lanes] = (dot(scores, g, (0, 0)) + dot(fk, grad_in, (1, 0)) * end).astype(BF16)
+        vg_ref[:, lanes] = (vgi_ref[:, lanes] + dot(fk, grad_in, (1, 0)) * end).astype(BF16)
         qg_ref[:, lanes] = dot(query_back, mq_ref[j], (1, 1)).astype(BF16)
         kg_ref[:, lanes] = dot(key_back, mk_ref[j], (1, 1)).astype(BF16)
 
@@ -330,7 +338,15 @@
         ],
         compiler_params=VMEM,
     )(received, blocks, totals)
-    carried = exchange(states, NEAR)
+    value_inside = pl.pallas_call(
+        values_kernel,
+        grid=(steps,),
+        in_specs=[wide] * 3 + [gate_spec],
+        out_specs=wide,
+        out_shape=sum_shape,
+        cost_estimate=pl.CostEstimate(flops=2 * flops, bytes_accessed=3 << 20, transcendentals=1 << 18),
+    )(g, fq, fk, gates)
+    carried, value_inside = lax.optimization_barrier((exchange(states, NEAR), value_inside))
     maps = pl.pallas_call(
         pair_kernel,
         in_specs=[whole] * 4,
@@ -345,8 +361,8 @@
         + [pl.BlockSpec((near // steps, rows, width), lambda i: (i, 0, 0))],
         out_specs=[wide] * 3,
         out_shape=[wide_shape] * 3,
-        cost_estimate=pl.CostEstimate(flops=7 * flops, bytes_accessed=8 << 20, transcendentals=0),
-    )(v, g, fq, fk, gates, query_map, key_map, query_inside, key_inside, carried)
+        cost_estimate=pl.CostEstimate(flops=5 * flops, bytes_accessed=8 << 20, transcendentals=0),
+    )(v, g, value_inside, fk, gates, query_map, key_map, query_inside, key_inside, carried)
     maps, query_grad = lax.optimization_barrier((exchange(maps, NEAR), query_grad))
     maps = pl.pallas_call(
         gather_kernel,

time: 100 us -> 100 us (level)
  the two profiles are of different devices: /device:TPU:1 before, /device:TPU:8 now
where the time goes in v10:
time: 100 us; the launch traced here: 99.7 us
  Pallas kernels  30.4 us (30%)
  starting transfers between devices  29.4 us (29%)
  blocking collectives  19.7 us (20%)
  waiting for transfers between devices  18.1 us (18%)
  local copies, waits for them, and re-layouts  1.43 us (1%)
    all_to_all x4, starting transfers between devices, exchange(): return lax.all_to_all(value, axes, 0, 0, tiled=True)  23.2 us
    all_to_all x1, blocking collectives, exchange(): return lax.all_to_all(value, axes, 0, 0, tiled=True)  19.7 us
    all_to_all x4, waiting for transfers between devices, exchange(): return lax.all_to_all(value, axes, 0, 0, tiled=True)  18.1 us
    pallas_call x1, Pallas kernels, per_device(): pl.pallas_call(functools.partial(inside_kernel, key_scale, map_scale), gr...  9.64 us
    pallas_call x1, Pallas kernels, per_device(): pl.pallas_call(functools.partial(grads_kernel, key_scale), grid=(steps,),...  6.11 us
    pallas_call x1, Pallas kernels, per_device(): pl.pallas_call(values_kernel, grid=(steps,), in_specs=[wide] * 3 + [gate_...  6.01 us
    pallas_call x1, Pallas kernels, per_device(): pl.pallas_call(products_kernel, grid=(steps,), in_specs=[wide, wide, wide...  3.69 us
    ppermute x1, starting transfers between devices, per_device(): inside_got = lax.ppermute(send, 'y_lo', swap)  2.36 us
  transfers between devices with their start and end apart: 7, of which 4 were waited for; matrix products, arithmetic and copies ran while one was open for 0% of the time, Pallas kernels for 24%

profile of v10, /device:TPU:8, one launch (start us, length us, event | category | flops | bytes accessed | tf_op | source)
XLA Modules:
  0.0 99.7 jit_solution(15883677796926964653)
XLA Ops:
  0.6 3.7 %shard_map.102 = bf16[16,264,128]{2,1,0:T(8,128)(2,1)} custom-call(bf16[128,2048]{1,0:T(8,128)(2,1)} %bitcast.24, bf16[128,2048]{1,0:T(8,128)(2,1)} %bitcast.26, bf16[128,2048]{1,0:T(8,128)(2,1)} %bitcast.20, bf16[128,2048]{1,0:T(8,128)(2,1)} %bitcast.16, f32[16,128]{1,0:T(8,128)} %bitcast.28), custom_call_target="tpu_custom_call" | custom-call | flops 134217728 | bytes 3145728 | tf_op jit(solution)/shard_map/pallas_call | solution.py:286
  4.3 6.1 %all-to-all-start = ((bf16[8,2,264,128]{3,2,1,0:T(8,128)(2,1)}), bf16[8,2,264,128]{3,2,1,0:T(8,128)(2,1)S(1)}, u32[]{:S(2)}, u32[]{:S(2)}) async-start(bf16[8,2,264,128]{3,2,1,0:T(8,128)(2,1)} %bitcast.23), calls=%async_computation | async-start | bytes 2162688 | tf_op jit(solution)/shard_map/all_to_all | solution.py:267
  10.4 0.0 copy-start
  10.4 0.0 copy-start.1
  10.4 9.6 %shard_map.103 = (bf16[128,2048]{1,0:T(8,128)(2,1)}, bf16[128,2048]{1,0:T(8,128)(2,1)}, f32[128,2048]{1,0:T(8,128)}, f32[128,2048]{1,0:T(8,128)}, bf16[2,8,2,2,3...) custom-call(bf16[128,2048]{1,0:T(8,128)(2,1)} %bitcast.25, bf16[128,2048]{1,0:T(8,128)(2,1)} %bitcast.27, ...), custom_call_target="tpu_custom_call" | custom-call | flops 469762048 | bytes 8388608 | tf_op jit(solution)/shard_map/pallas_call | solution.py:298
  20.1 1.9 %collective-permute-start = (bf16[2,8,128,128]{3,2,1,0:T(8,128)(2,1)}, bf16[2,8,128,128]{3,2,1,0:T(8,128)(2,1)S(1)}, u32[]{:S(2)}, u32[]{:S(2)}) collective-permute-start(bf16[2,8,128,128]{3,2,1,0:T(8,128)(2,1)} %bitcast.35), channel_id=1, source_target_pairs={{0,32},{32,0},{1,33},{33,1},{2,34},{34,2},{3,35},{35,3},{4,36},{36... | collective-permute-start | bytes 1572872 | tf_op jit(solution)/shard_map/ppermute | solution.py:325
  22.0 3.6 %all-to-all-done.in_ref = bf16[8,2,264,128]{3,2,1,0:T(8,128)(2,1)S(1)} async-done(((bf16[8,2,264,128]{3,2,1,0:T(8,128)(2,1)}), bf16[8,2,264,128]{3,2,1,0:T(8,128)(2,1)S(1)}, u32[]{:S(2)}, u32[]{:S(2)}) %all-to-all-start) | async-done | bytes 1081376 | tf_op jit(solution)/shard_map/all_to_all | solution.py:267
  25.6 0.0 copy-done
  25.6 0.0 copy-done.1
  25.6 0.0 copy-start.2
  25.6 1.2 %shard_map.105 = bf16[4,2,144,128]{3,2,1,0:T(8,128)(2,1)} custom-call(bf16[8,2,264,128]{3,2,1,0:T(8,128)(2,1)S(1)} %all-to-all-done.in_ref, bf16[16,128,128]{2,1,0:T(8,128)(2,1)S(1)} %copy-done, bf16[16,128,128]{2,1,0:T(8,128)(2,1)S(1)} %copy-done.1), custom_call_target="tpu_custom_call" | custom-call | tf_op jit(solution)/shard_map/pallas_call | solution.py:312
  26.8 9.4 %all-to-all-start.1 = ((bf16[4,2,144,128]{3,2,1,0:T(8,128)(2,1)}), bf16[4,2,144,128]{3,2,1,0:T(8,128)(2,1)S(1)}, u32[]{:S(2)}, u32[]{:S(2)}) async-start(bf16[4,2,144,128]{3,2,1,0:T(8,128)(2,1)} %shard_map.105), calls=%async_computation.1 | async-start | bytes 589824 | tf_op jit(solution)/shard_map/all_to_all | solution.py:267
  36.2 0.0 collective-permute-done.got_ref
  36.2 0.0 copy-done.2
  36.2 0.1 shard_map.106
  36.3 0.0 copy-start.3
  36.4 0.7 copy-done.3
  37.1 0.0 copy-start.5
  37.1 0.7 copy-done.5
  37.8 0.5 shard_map.104.blocks_ref
  38.3 9.6 %all-to-all-done.1.totals_ref = bf16[4,2,144,128]{3,2,1,0:T(8,128)(2,1)S(1)} async-done(((bf16[4,2,144,128]{3,2,1,0:T(8,128)(2,1)}), bf16[4,2,144,128]{3,2,1,0:T(8,128)(2,1)S(1)}, u32[]{:S(2)}, u32[]{:S(2)}) %all-to-all-start.1) | async-done | bytes 294944 | tf_op jit(solution)/shard_map/all_to_all | solution.py:267
  47.8 1.6 %shard_map.107 = (bf16[8,512,128]{2,1,0:T(8,128)(2,1)}, bf16[2,8,32,128]{3,2,1,0:T(8,128)(2,1)S(1)}) custom-call(bf16[8,2,264,128]{3,2,1,0:T(8,128)(2,1)S(1)} %all-to-all-done.in_ref, bf16[8,2,256,128]{3,2,1,0:T(8,128)(2,1)S(1)} %shard_map.104.blocks_ref, bf16[4,2,144,128]{3,2,1,0:T(8,128)(2,1)S(1)} %all-to-all-done.1.totals_ref), custom_call_target="tpu_custom_call" | custom-call | tf_op jit(solution)/shard_map/pallas_call | solution.py:332
  49.5 0.0 copy-start.6
  49.5 4.0 %all-to-all-start.2 = ((bf16[8,512,128]{2,1,0:T(8,128)(2,1)}), bf16[8,512,128]{2,1,0:T(8,128)(2,1)S(1)}, u32[]{:S(2)}, u32[]{:S(2)}) async-start(bf16[8,512,128]{2,1,0:T(8,128)(2,1)} %get-tuple-element.33), calls=%async_computation.2 | async-start | bytes 2097152 | tf_op jit(solution)/shard_map/all_to_all | solution.py:267
  53.5 0.0 copy-done.6
  53.5 2.4 %collective-permute-start.1 = (bf16[8,128,128]{2,1,0:T(8,128)(2,1)S(1)}, bf16[8,128,128]{2,1,0:T(8,128)(2,1)S(1)}, u32[]{:S(2)}, u32[]{:S(2)}) collective-permute-start(bf16[8,128,128]{2,1,0:T(8,128)(2,1)S(1)} %copy-done.6), channel_id=1, source_target_pairs={{0,64},{64,0},{1,65},{65,1},{2,66},{66,2},{3,67},{67,3},{4,68},{68... | collective-permute-start | bytes 786440 | tf_op jit(solution)/shard_map/ppermute | solution.py:331
  55.9 1.9 %collective-permute-start.2 = (bf16[8,32,128]{2,1,0:T(8,128)(2,1)S(1)}, bf16[8,32,128]{2,1,0:T(8,128)(2,1)S(1)}, u32[]{:S(2)}, u32[]{:S(2)}) collective-permute-start(bf16[8,32,128]{2,1,0:T(8,128)(2,1)S(1)} %slice_bitcast_fusion), channel_id=1, source_target_pairs={{0,32},{32,0},{1,33},{33,1},{2,34},{34,2},{3,35},{35,3},{4,36},{36... | collective-permute-start | bytes 196616 | tf_op jit(solution)/shard_map/ppermute | solution.py:355
  57.8 0.0 copy-start.4
  57.8 6.0 %shard_map.108.vgi_ref = f32[128,2048]{1,0:T(8,128)} custom-call(bf16[128,2048]{1,0:T(8,128)(2,1)} %bitcast.18, bf16[128,2048]{1,0:T(8,128)(2,1)} %get-tuple-element.34.fq_ref, bf16[128,2048]{1,0:T(8,128)(2,1)} %get-tuple-element.35.fk_ref, f32[16,128]{1,0:T(8,128)} %bitcast.30), custom_call_target="tpu_custom_call" | custom-call | flops 134217728 | bytes 3145728 | tf_op jit(solution)/shard_map/pallas_call | solution.py:341
  63.8 0.0 collective-permute-done.2.carried_got_ref
  63.8 0.0 collective-permute-done.1.inside_got_ref
  63.8 0.0 copy-done.4
  63.9 0.8 shard_map.109
  64.7 3.1 %all-to-all-done.2.in_ref = bf16[8,512,128]{2,1,0:T(8,128)(2,1)S(1)} async-done(((bf16[8,512,128]{2,1,0:T(8,128)(2,1)}), bf16[8,512,128]{2,1,0:T(8,128)(2,1)S(1)}, u32[]{:S(2)}, u32[]{:S(2)}) %all-to-all-start.2) | async-done | bytes 1048608 | tf_op jit(solution)/shard_map/all_to_all | solution.py:267
  67.7 0.0 copy-start.7
  67.7 3.6 %all-to-all-start.3 = ((bf16[8,160,128]{2,1,0:T(8,128)(2,1)}), bf16[8,160,128]{2,1,0:T(8,128)(2,1)S(1)}, u32[]{:S(2)}, u32[]{:S(2)}) async-start(bf16[8,160,128]{2,1,0:T(8,128)(2,1)} %shard_map.109), calls=%async_computation.3 | async-start | bytes 655360 | tf_op jit(solution)/shard_map/all_to_all | solution.py:267
  71.4 0.0 copy-done.7
  71.4 6.1 %shard_map.110 = (bf16[128,2048]{1,0:T(8,128)(2,1)}, bf16[128,2048]{1,0:T(8,128)(2,1)}, bf16[128,2048]{1,0:T(8,128)(2,1)}) custom-call(bf16[128,2048]{1,0:T(8,128)(2,1)} %bitcast.22, bf16[128,2048]{1,0:T(8,128)(2,1)} %bitcast.19, f32[128,2048]{1,0:T(8,128)} %shard_map.108.vgi_ref, bf16[128,2048]{1,0:T(8,128)(2,1)} %get-tuple-element.35.fk_ref, ...), custom_call_target="tpu_custom_call" | custom-call | flops 335544320 | bytes 8388608 | tf_op jit(solution)/shard_map/pallas_call | solution.py:357
  77.5 1.9 %all-to-all-done.3.in_ref = bf16[8,160,128]{2,1,0:T(8,128)(2,1)S(1)} async-done(((bf16[8,160,128]{2,1,0:T(8,128)(2,1)}), bf16[8,160,128]{2,1,0:T(8,128)(2,1)S(1)}, u32[]{:S(2)}, u32[]{:S(2)}) %all-to-all-start.3) | async-done | bytes 327712 | tf_op jit(solution)/shard_map/all_to_all | solution.py:267
  79.4 19.7 %all_to_all.25.in_ref = bf16[32,8,128]{2,1,0:T(8,128)(2,1)S(1)} all-to-all(bf16[32,8,128]{2,1,0:T(8,128)(2,1)S(1)} %bitcast.15), channel_id=1, replica_groups=mesh['y_hi'=4,'y_lo'=2,'core'=2,'outer'=4,'inner'=2,'x'=4] {'y_hi','y_lo..., dimensions={0} | all-to-all | bytes 131072 | tf_op jit(solution)/shard_map/all_to_all | solution.py:267
  99.1 0.6 shard_map.112
  (2 shorter events, 0.1 us)
Async XLA Ops:
  4.3 21.3 %all-to-all-start = ((bf16[8,2,264,128]{3,2,1,0:T(8,128)(2,1)}), bf16[8,2,264,128]{3,2,1,0:T(8,128)(2,1)S(1)}, u32[]{:S(2)}, u32[]{:S(2)}) async-start(bf16[8,2,264,128]{3,2,1,0:T(8,128)(2,1)} %bitcast.23), calls=%async_computation | async-start | bytes 2162688 | tf_op jit(solution)/shard_map/all_to_all | solution.py:267
  10.4 15.2 %copy-start = (bf16[16,128,128]{2,1,0:T(8,128)(2,1)S(1)}, bf16[16,128,128]{2,1,0:T(8,128)(2,1)}, u32[]{:S(2)}) copy-start(bf16[16,128,128]{2,1,0:T(8,128)(2,1)} %mq_ref.7) | copy-start | bytes 1572868
  10.4 15.2 %copy-start.1 = (bf16[16,128,128]{2,1,0:T(8,128)(2,1)S(1)}, bf16[16,128,128]{2,1,0:T(8,128)(2,1)}, u32[]{:S(2)}) copy-start(bf16[16,128,128]{2,1,0:T(8,128)(2,1)} %mk_ref.7) | copy-start | bytes 1572868
  20.1 16.1 %collective-permute-start = (bf16[2,8,128,128]{3,2,1,0:T(8,128)(2,1)}, bf16[2,8,128,128]{3,2,1,0:T(8,128)(2,1)S(1)}, u32[]{:S(2)}, u32[]{:S(2)}) collective-permute-start(bf16[2,8,128,128]{3,2,1,0:T(8,128)(2,1)} %bitcast.35), channel_id=1, source_target_pairs={{0,32},{32,0},{1,33},{33,1},{2,34},{34,2},{3,35},{35,3},{4,36},{36... | collective-permute-start | bytes 1572872 | tf_op jit(solution)/shard_map/ppermute | solution.py:325
  25.6 10.6 %copy-start.2 = (bf16[2,8,2,2,32,128]{5,4,3,2,1,0:T(8,128)(2,1)S(1)}, bf16[2,8,2,2,32,128]{5,4,3,2,1,0:T(8,128)(2,1)}, u32[]{:S(2)}) copy-start(bf16[2,8,2,2,32,128]{5,4,3,2,1,0:T(8,128)(2,1)} %get-tuple-element.27) | copy-start | bytes 1572868
  26.8 21.0 %all-to-all-start.1 = ((bf16[4,2,144,128]{3,2,1,0:T(8,128)(2,1)}), bf16[4,2,144,128]{3,2,1,0:T(8,128)(2,1)S(1)}, u32[]{:S(2)}, u32[]{:S(2)}) async-start(bf16[4,2,144,128]{3,2,1,0:T(8,128)(2,1)} %shard_map.105), calls=%async_computation.1 | async-start | bytes 589824 | tf_op jit(solution)/shard_map/all_to_all | solution.py:267
  36.3 0.7 copy-start.3
  37.1 0.7 copy-start.5
  49.5 4.0 %copy-start.6 = (bf16[8,128,128]{2,1,0:T(8,128)(2,1)S(1)}, bf16[8,128,128]{2,1,0:T(8,128)(2,1)}, u32[]{:S(2)}) copy-start(bf16[8,128,128]{2,1,0:T(8,128)(2,1)} %copy-done.5) | copy-start | bytes 786436
  49.5 18.3 %all-to-all-start.2 = ((bf16[8,512,128]{2,1,0:T(8,128)(2,1)}), bf16[8,512,128]{2,1,0:T(8,128)(2,1)S(1)}, u32[]{:S(2)}, u32[]{:S(2)}) async-start(bf16[8,512,128]{2,1,0:T(8,128)(2,1)} %get-tuple-element.33), calls=%async_computation.2 | async-start | bytes 2097152 | tf_op jit(solution)/shard_map/all_to_all | solution.py:267
  53.5 10.3 %collective-permute-start.1 = (bf16[8,128,128]{2,1,0:T(8,128)(2,1)S(1)}, bf16[8,128,128]{2,1,0:T(8,128)(2,1)S(1)}, u32[]{:S(2)}, u32[]{:S(2)}) collective-permute-start(bf16[8,128,128]{2,1,0:T(8,128)(2,1)S(1)} %copy-done.6), channel_id=1, source_target_pairs={{0,64},{64,0},{1,65},{65,1},{2,66},{66,2},{3,67},{67,3},{4,68},{68... | collective-permute-start | bytes 786440 | tf_op jit(solution)/shard_map/ppermute | solution.py:331
  55.9 8.0 %collective-permute-start.2 = (bf16[8,32,128]{2,1,0:T(8,128)(2,1)S(1)}, bf16[8,32,128]{2,1,0:T(8,128)(2,1)S(1)}, u32[]{:S(2)}, u32[]{:S(2)}) collective-permute-start(bf16[8,32,128]{2,1,0:T(8,128)(2,1)S(1)} %slice_bitcast_fusion), channel_id=1, source_target_pairs={{0,32},{32,0},{1,33},{33,1},{2,34},{34,2},{3,35},{35,3},{4,36},{36... | collective-permute-start | bytes 196616 | tf_op jit(solution)/shard_map/ppermute | solution.py:355
  57.8 6.0 %copy-start.4 = (bf16[8,128,128]{2,1,0:T(8,128)(2,1)S(1)}, bf16[8,128,128]{2,1,0:T(8,128)(2,1)}, u32[]{:S(2)}) copy-start(bf16[8,128,128]{2,1,0:T(8,128)(2,1)} %copy-done.3) | copy-start | bytes 786436
  67.7 3.6 %copy-start.7 = (bf16[8,512,128]{2,1,0:T(8,128)(2,1)}, bf16[8,512,128]{2,1,0:T(8,128)(2,1)S(1)}, u32[]{:S(2)}) copy-start(bf16[8,512,128]{2,1,0:T(8,128)(2,1)S(1)} %all-to-all-done.2.in_ref) | copy-start | bytes 3145732
  67.7 11.6 %all-to-all-start.3 = ((bf16[8,160,128]{2,1,0:T(8,128)(2,1)}), bf16[8,160,128]{2,1,0:T(8,128)(2,1)S(1)}, u32[]{:S(2)}, u32[]{:S(2)}) async-start(bf16[8,160,128]{2,1,0:T(8,128)(2,1)} %shard_map.109), calls=%async_computation.3 | async-start | bytes 655360 | tf_op jit(solution)/shard_map/all_to_all | solution.py:267
